TPU v7x, 32 devices: a whole 2x2x4 slice. The times are simulated.
32 devices in a mesh: tensor: 4 (over z), group: 4 (over y, core), cross: 2 (over x).
Axes of the slice: x: 2, y: 2, z: 4, core: 2. Of those that a mesh axis runs over, the one named last changes fastest.
Arguments:
- inputs: bfloat16 [16, 1568, 1024], P(('group', 'cross'), 'tensor'), may hold values from -6 to 6
- clips_here: int32 [8], P(('group', 'cross')), may hold values from 1 to 2, as said below
- first_gain: bfloat16 [1024], replicated, may hold values from 0.5 to 1.5
- first_shift: bfloat16 [1024], replicated, may hold values from -1.25 to 1.25
- query_key_value: bfloat16 [3, 1024, 1024], P(None, 'group', 'tensor'), may hold values from -0.1875 to 0.1875
- query_bias: bfloat16 [1024], P('tensor'), may hold values from -3 to 3
- value_bias: bfloat16 [1024], P('tensor'), may hold values from -0.1875 to 0.1875
- output_weight: bfloat16 [1024, 1024], P('tensor', 'group'), may hold values from -6 to 6
- output_bias: bfloat16 [1024], replicated, may hold values from -3 to 3
- second_gain: bfloat16 [1024], replicated, may hold values from 0.5 to 1.5
- second_shift: bfloat16 [1024], replicated, may hold values from -1.25 to 1.25
- expand_weight: bfloat16 [1024, 4096], P('group', 'tensor'), may hold values from -0.1875 to 0.1875
- expand_bias: bfloat16 [4096], P('tensor'), may hold values from -3 to 3
- contract_weight: bfloat16 [4096, 1024], P('tensor', 'group'), may hold values from -0.09375 to 0.09375
- contract_bias: bfloat16 [1024], replicated, may hold values from -3 to 3
- output_grad: bfloat16 [16, 1568, 1024], P(('group', 'cross'), 'tensor'), may hold values from -6 to 6
Outputs:
- output: bfloat16 [16, 1568, 1024], P(('group', 'cross'), 'tensor')
- input_grad: bfloat16 [16, 1568, 1024], P(('group', 'cross'), 'tensor')
- first_gain_grad: float32 [1024], P('group')
- first_shift_grad: float32 [1024], P('group')
- query_key_value_grad: float32 [3, 1024, 1024], P(None, 'group', 'tensor')
- query_bias_grad: float32 [1024], P(('tensor', 'group'))
- value_bias_grad: float32 [1024], P(('tensor', 'group'))
- output_weight_grad: float32 [1024, 1024], P('tensor', 'group')
- output_bias_grad: float32 [1024], P('group')
- second_gain_grad: float32 [1024], P('group')
- second_shift_grad: float32 [1024], P('group')
- expand_weight_grad: float32 [1024, 4096], P('group', 'tensor')
- expand_bias_grad: float32 [4096], P(('tensor', 'group'))
- contract_weight_grad: float32 [4096, 1024], P('tensor', 'group')
- contract_bias_grad: float32 [1024], P('group')
Inputs may be any that keep to these rules, and one draw needn't show every extreme that they name: Exactly half of the 8 data positions hold 2 clips and the others 1; slot p * 2 + j holds a clip if j < clips_here[p].
All inputs are finite; a program needn't handle non-finite values.
Results may differ from a plain program's by a relative error of at most 0.02.
Values may be sent and summed in bfloat16 or wider, within the bound.
A program may use at most 192 MiB of HBM per device.

v0:
```python
import jax
import jax.numpy as jnp
from jax import lax
from jax.sharding import PartitionSpec as P

HEAD = 64


epsilon = 1e-06
root_half = 0.7071067811865476
inv_root_two_pi = 0.3989422804014327


def normalize(values):
    center = values - jnp.mean(values, axis=-1, keepdims=True)
    inverse = lax.rsqrt(jnp.mean(center * center, axis=-1, keepdims=True) + epsilon)
    return (center * inverse, inverse)


def normalize_back(upstream, normed, inverse, norm_gain):
    scaled = upstream * norm_gain
    return inverse * (
        scaled
        - jnp.mean(scaled, axis=-1, keepdims=True)
        - normed * jnp.mean(scaled * normed, axis=-1, keepdims=True)
    )


def attend_forward(triple):
    query_rows, key_rows, value_rows = triple
    length = query_rows.shape[0]
    head_count = query_rows.shape[1] // HEAD
    key_heads = key_rows.reshape(length, head_count, HEAD)
    value_heads = value_rows.reshape(length, head_count, HEAD)
    query_parts = query_rows.reshape(2, length // 2, head_count, HEAD)

    def one_part(query_part):
        logits = jnp.einsum(
            "bhe,lhe->hbl", query_part, key_heads, preferred_element_type=jnp.float32
        ) * HEAD ** (-0.5)
        largest = jnp.max(logits, axis=-1, keepdims=True)
        powers = jnp.exp(logits - largest)
        totals = jnp.sum(powers, axis=-1, keepdims=True)
        probs = (powers / totals).astype(jnp.bfloat16)
        attention_result = jnp.einsum(
            "hbl,lhe->bhe", probs, value_heads, preferred_element_type=jnp.float32
        )
        return (attention_result.astype(jnp.bfloat16), largest + jnp.log(totals))

    attention_result, log_totals = lax.map(one_part, query_parts)
    return (attention_result.reshape(length, head_count * HEAD), log_totals)


def attend_backward(entries):
    query_rows, key_rows, value_rows, upstream_rows, log_totals = entries
    length = query_rows.shape[0]
    head_count = query_rows.shape[1] // HEAD
    key_heads = key_rows.reshape(length, head_count, HEAD)
    value_heads = value_rows.reshape(length, head_count, HEAD)
    query_parts = query_rows.reshape(2, length // 2, head_count, HEAD)
    upstream_parts = upstream_rows.reshape(2, length // 2, head_count, HEAD)

    def one_part(carry, part_items):
        key_grad, value_grad = carry
        query_part, upstream_part, log_total = part_items
        logits = jnp.einsum(
            "bhe,lhe->hbl", query_part, key_heads, preferred_element_type=jnp.float32
        ) * HEAD ** (-0.5)
        probs = jnp.exp(logits - log_total)
        prob_grad = jnp.einsum(
            "bhe,lhe->hbl", upstream_part, value_heads, preferred_element_type=jnp.float32
        )
        inner = jnp.sum(probs * prob_grad, axis=-1, keepdims=True)
        logit_grad = (probs * (prob_grad - inner) * HEAD ** (-0.5)).astype(jnp.bfloat16)
        query_grad = jnp.einsum(
            "hbl,lhe->bhe", logit_grad, key_heads, preferred_element_type=jnp.float32
        )
        key_grad = key_grad + jnp.einsum(
            "hbl,bhe->lhe", logit_grad, query_part, preferred_element_type=jnp.float32
        )
        value_grad = value_grad + jnp.einsum(
            "hbl,bhe->lhe",
            probs.astype(jnp.bfloat16),
            upstream_part,
            preferred_element_type=jnp.float32,
        )
        return ((key_grad, value_grad), query_grad.astype(jnp.bfloat16))

    empty_grad = jnp.zeros((length, head_count, HEAD), jnp.float32)
    (key_grad, value_grad), query_grads = lax.scan(
        one_part, (empty_grad, empty_grad), (query_parts, upstream_parts, log_totals)
    )
    width = head_count * HEAD
    return (
        query_grads.reshape(length, width),
        key_grad.astype(jnp.bfloat16).reshape(length, width),
        value_grad.astype(jnp.bfloat16).reshape(length, width),
    )


def gelu_slope(hidden_pre):
    normal_cdf = 0.5 * (1.0 + lax.erf(hidden_pre * root_half))
    normal_pdf = inv_root_two_pi * jnp.exp(-0.5 * hidden_pre * hidden_pre)
    return normal_cdf + hidden_pre * normal_pdf


def local(
    inputs,
    clips_here,
    first_gain,
    first_shift,
    query_key_value,
    query_bias,
    value_bias,
    output_weight,
    output_bias,
    second_gain,
    second_shift,
    expand_weight,
    expand_bias,
    contract_weight,
    contract_bias,
    output_grad,
):
    floating_kind = jnp.float32
    slot_count = inputs.shape[0]
    tensor_index = lax.axis_index("tensor")
    tensor_count = lax.axis_size("tensor")
    group_index = lax.axis_index("group")
    group_count = lax.axis_size("group")

    def widen(local_vector):
        width = local_vector.shape[0]
        return lax.dynamic_update_slice(
            jnp.zeros((width * tensor_count,), floating_kind), local_vector, (tensor_index * width,)
        )

    alive_mask = (jnp.arange(slot_count, dtype=jnp.int32) < clips_here[0]).astype(floating_kind)[
        :, None, None
    ]
    (
        triple_weight_complete,
        output_weight_complete,
        expand_weight_complete,
        contract_weight_complete,
    ) = (
        lax.all_gather(query_key_value, "group", axis=1, tiled=True),
        lax.all_gather(output_weight, "group", axis=1, tiled=True),
        lax.all_gather(expand_weight, "group", axis=0, tiled=True),
        lax.all_gather(contract_weight, "group", axis=1, tiled=True),
    )
    gain_one = first_gain.astype(floating_kind)
    gain_two = second_gain.astype(floating_kind)
    tokens = inputs.astype(floating_kind)
    first_plain, first_inverse = normalize(tokens)
    first_rows = (first_plain * gain_one + first_shift.astype(floating_kind)).astype(jnp.bfloat16)
    first_gathered = lax.all_gather(first_rows, "tensor", axis=1, tiled=True)
    bias_stack = jnp.stack([query_bias, jnp.zeros_like(query_bias), value_bias]).astype(
        floating_kind
    )
    projected = jnp.einsum(
        "ruh,nhm->nrum",
        first_gathered,
        triple_weight_complete,
        preferred_element_type=floating_kind,
    )
    projected = (projected + bias_stack[:, None, None, :]).astype(jnp.bfloat16)
    attention_result, log_totals = lax.map(
        attend_forward, (projected[0], projected[1], projected[2])
    )
    attention_terms = jnp.einsum(
        "hpx,xj->hpj",
        attention_result,
        output_weight_complete,
        preferred_element_type=floating_kind,
    )
    attention_part = lax.psum_scatter(
        attention_terms.astype(jnp.bfloat16), "tensor", scatter_dimension=1, tiled=True
    ).astype(jnp.float32)
    middle = tokens + attention_part + output_bias.astype(floating_kind)
    second_plain, second_inverse = normalize(middle)
    second_rows = (second_plain * gain_two + second_shift.astype(floating_kind)).astype(
        jnp.bfloat16
    )
    top_grad = output_grad.astype(floating_kind) * alive_mask
    feed_grad = top_grad.astype(jnp.bfloat16)
    contract_bias_part = jnp.sum(feed_grad.astype(floating_kind), axis=(0, 1))
    second_gathered = lax.all_gather(second_rows, "tensor", axis=1, tiled=True)
    hidden_pre = jnp.einsum(
        "njz,zc->njc", second_gathered, expand_weight_complete, preferred_element_type=floating_kind
    )
    hidden_pre = hidden_pre + expand_bias.astype(floating_kind)
    hidden_activation = jax.nn.gelu(hidden_pre, approximate=False).astype(jnp.bfloat16)
    feed_forward_terms = jnp.einsum(
        "ybj,jx->ybx",
        hidden_activation,
        contract_weight_complete,
        preferred_element_type=floating_kind,
    )
    feed_part = lax.psum_scatter(
        feed_forward_terms.astype(jnp.bfloat16), "tensor", scatter_dimension=1, tiled=True
    ).astype(jnp.float32)
    output = (middle + feed_part + contract_bias.astype(floating_kind)).astype(jnp.bfloat16)
    feed_grad_gathered = lax.all_gather(feed_grad, "tensor", axis=1, tiled=True)
    contract_weight_part = jnp.einsum(
        "gct,gcu->tu", hidden_activation, feed_grad_gathered, preferred_element_type=floating_kind
    )
    hidden_grad = jnp.einsum(
        "bxn,qn->bxq",
        feed_grad_gathered,
        contract_weight_complete,
        preferred_element_type=floating_kind,
    )
    preactivation_grad = (hidden_grad * gelu_slope(hidden_pre)).astype(jnp.bfloat16)
    expand_bias_vector = widen(jnp.sum(preactivation_grad.astype(floating_kind), axis=(0, 1)))
    expand_weight_part = jnp.einsum(
        "aew,aex->wx", second_gathered, preactivation_grad, preferred_element_type=floating_kind
    )
    second_terms = jnp.einsum(
        "rci,ei->rce",
        preactivation_grad,
        expand_weight_complete,
        preferred_element_type=floating_kind,
    )
    second_grad = lax.psum_scatter(
        second_terms.astype(jnp.bfloat16), "tensor", scatter_dimension=1, tiled=True
    ).astype(jnp.float32)
    second_gain_part = jnp.sum(second_grad * second_plain, axis=(0, 1))
    second_shift_part = jnp.sum(second_grad, axis=(0, 1))
    middle_grad = top_grad + normalize_back(second_grad, second_plain, second_inverse, gain_two)
    branch_grad = middle_grad.astype(jnp.bfloat16)
    output_bias_part = jnp.sum(branch_grad.astype(floating_kind), axis=(0, 1))
    branch_gathered = lax.all_gather(branch_grad, "tensor", axis=1, tiled=True)
    output_weight_part = jnp.einsum(
        "vat,vah->th", attention_result, branch_gathered, preferred_element_type=floating_kind
    )
    attended_grad = jnp.einsum(
        "ghv,cv->ghc", branch_gathered, output_weight_complete, preferred_element_type=floating_kind
    ).astype(jnp.bfloat16)
    query_grad, key_grad, value_grad = lax.map(
        attend_backward, (projected[0], projected[1], projected[2], attended_grad, log_totals)
    )
    triple_weight_gradient = jnp.stack([query_grad, key_grad, value_grad])
    query_bias_part = jnp.sum(query_grad.astype(floating_kind), axis=(0, 1))
    value_bias_part = jnp.sum(value_grad.astype(floating_kind), axis=(0, 1))
    triple_weight_part = jnp.einsum(
        "ayn,iayf->inf",
        first_gathered,
        triple_weight_gradient,
        preferred_element_type=floating_kind,
    )
    first_terms = jnp.einsum(
        "hpxw,hgw->pxg",
        triple_weight_gradient,
        triple_weight_complete,
        preferred_element_type=floating_kind,
    )
    first_grad = lax.psum_scatter(
        first_terms.astype(jnp.bfloat16), "tensor", scatter_dimension=1, tiled=True
    ).astype(jnp.float32)
    first_gain_part = jnp.sum(first_grad * first_plain, axis=(0, 1))
    first_shift_part = jnp.sum(first_grad, axis=(0, 1))
    input_grad = (
        middle_grad + normalize_back(first_grad, first_plain, first_inverse, gain_one)
    ).astype(jnp.bfloat16)
    large_parts = (triple_weight_part, output_weight_part, expand_weight_part, contract_weight_part)
    group_parts = (
        lax.psum_scatter(
            large_parts[0].astype(jnp.bfloat16), "group", scatter_dimension=1, tiled=True
        ).astype(jnp.float32),
        lax.psum_scatter(
            large_parts[1].astype(jnp.bfloat16), "group", scatter_dimension=1, tiled=True
        ).astype(jnp.float32),
        lax.psum_scatter(
            large_parts[2].astype(jnp.bfloat16), "group", scatter_dimension=0, tiled=True
        ).astype(jnp.float32),
        lax.psum_scatter(
            large_parts[3].astype(jnp.bfloat16), "group", scatter_dimension=1, tiled=True
        ).astype(jnp.float32),
    )
    large_sums = (
        lax.psum(group_parts[0].astype(jnp.bfloat16), "cross").astype(jnp.float32),
        lax.psum(group_parts[1].astype(jnp.bfloat16), "cross").astype(jnp.float32),
        lax.psum(group_parts[2].astype(jnp.bfloat16), "cross").astype(jnp.float32),
        lax.psum(group_parts[3].astype(jnp.bfloat16), "cross").astype(jnp.float32),
    )
    small_sums = lax.psum(
        (
            first_gain_part,
            first_shift_part,
            widen(query_bias_part),
            widen(value_bias_part),
            output_bias_part,
            second_gain_part,
            second_shift_part,
            expand_bias_vector,
            contract_bias_part,
        ),
        ("tensor", "group", "cross"),
    )

    def own_group(full_vector):
        width = full_vector.shape[0] // group_count
        return lax.dynamic_slice_in_dim(full_vector, group_index * width, width)

    def own_split(full_vector):
        width = full_vector.shape[0] // (group_count * tensor_count)
        return lax.dynamic_slice_in_dim(
            full_vector, (tensor_index * group_count + group_index) * width, width
        )

    return (
        output,
        input_grad,
        own_group(small_sums[0]),
        own_group(small_sums[1]),
        large_sums[0],
        own_split(small_sums[2]),
        own_split(small_sums[3]),
        large_sums[1],
        own_group(small_sums[4]),
        own_group(small_sums[5]),
        own_group(small_sums[6]),
        large_sums[2],
        own_split(small_sums[7]),
        large_sums[3],
        own_group(small_sums[8]),
    )


def solution(mesh):
    in_specs = (
        P(("group", "cross"), "tensor", None),
        P(("group", "cross")),
        P(),
        P(),
        P(None, "group", "tensor"),
        P("tensor"),
        P("tensor"),
        P("tensor", "group"),
        P(),
        P(),
        P(),
        P("group", "tensor"),
        P("tensor"),
        P("tensor", "group"),
        P(),
        P(("group", "cross"), "tensor", None),
    )
    out_specs = (
        P(("group", "cross"), "tensor", None),
        P(("group", "cross"), "tensor", None),
        P("group"),
        P("group"),
        P(None, "group", "tensor"),
        P(("tensor", "group")),
        P(("tensor", "group")),
        P("tensor", "group"),
        P("group"),
        P("group"),
        P("group"),
        P("group", "tensor"),
        P(("tensor", "group")),
        P("tensor", "group"),
        P("group"),
    )
    return jax.shard_map(local, mesh=mesh, in_specs=in_specs, out_specs=out_specs, check_vma=False)
```

profile of v0, /device:TPU:0, one launch (start us, length us, event | category | flops | bytes accessed | tf_op | source)
XLA Modules:
  0.0 1773.0 jit_solution(4338053443137835705)
XLA Ops:
  15.8 10.8 all_gather.26
  26.7 6.8 all-gather.10.cloned.1.call-done
  33.5 120.5 %all-gather.8.cloned.1.call-done = bf16[2,1568,1024]{2,1,0:T(8,128)(2,1)} async-done(((bf16[2,392,1024]{2,1,0:T(8,128)(2,1)}), bf16[2,1568,1024]{2,1,0:T(8,128)(2,1)}) %all-gather.8.cloned.1.call-update) | async-done | bytes 6422544 | tf_op jit(solution)/shard_map/all_gather | solution.py:157
  154.0 7.8 fusion.79
  173.9 81.3 %while.54 = (s32[]{:T(128)}, bf16[2,1568,256]{1,2,0:T(8,128)(2,1)}, f32[2,2,4,784,1]{3,2,1,4,0:T(4,128)}, bf16[2,1568,256]{1,2,0:T(8,128)(2,1)}, bf16[2,1568,256...) while((s32[]{:T(128)}, bf16[2,1568,256]{1,2,0:T(8,128)(2,1)}, ...), condition=%wide.region_7.8_spmd, body=%wide.region_2.7_spmd.sunk | while | flops 1303268352 | bytes 87527496 | solution.py:168
  180.3 30.0 %while.57 = (s32[]{:T(128)}, bf16[2,784,4,64]{1,3,2,0:T(8,128)(2,1)}, f32[2,4,784,1]{2,1,3,0:T(4,128)S(1)}, bf16[2,784,4,64]{1,3,2,0:T(8,128)(2,1)}, bf16[1568,4...) while((s32[]{:T(128)}, bf16[2,784,4,64]{1,3,2,0:T(8,128)(2,1)}, ...), condition=%wide.region_6.6_spmd, body=%wide.region_3.5_spmd.sunk | while | flops 1303268352 | bytes 61734240 | solution.py:50
  188.7 6.5 fusion.183
  203.7 6.5 fusion.183
  220.9 30.0 %while.57 = (s32[]{:T(128)}, bf16[2,784,4,64]{1,3,2,0:T(8,128)(2,1)}, f32[2,4,784,1]{2,1,3,0:T(4,128)S(1)}, bf16[2,784,4,64]{1,3,2,0:T(8,128)(2,1)}, bf16[1568,4...) while((s32[]{:T(128)}, bf16[2,784,4,64]{1,3,2,0:T(8,128)(2,1)}, ...), condition=%wide.region_6.6_spmd, body=%wide.region_3.5_spmd.sunk | while | flops 1303268352 | bytes 61734240 | solution.py:50
  229.3 6.5 fusion.183
  244.3 6.5 fusion.183
  259.2 13.9 copy.84
  273.2 5.4 copy.97
  279.3 110.5 %reduce-scatter.25.cloned.1.call-done = bf16[392,2048]{1,0:T(8,128)(2,1)} async-done(((bf16[1568,2048]{1,0:T(8,128)(2,1)}), bf16[392,2048]{1,0:T(8,128)(2,1)}) %reduce-scatter.25.cloned.1.call-update) | async-done | bytes 1605648
  403.3 11.0 all-gather.14.cloned.1.call-done
  414.4 119.5 %all-gather.12.cloned.1.call-done = bf16[2,1568,1024]{2,1,0:T(8,128)(2,1)} async-done(((bf16[2,392,1024]{2,1,0:T(8,128)(2,1)}), bf16[2,1568,1024]{2,1,0:T(8,128)(2,1)}) %all-gather.12.cloned.1.call-update) | async-done | bytes 6422544 | tf_op jit(solution)/shard_map/all_gather | solution.py:188
  533.9 19.7 %fusion.109 = (u8[1568,1024]{1,0:T(8,128)(4,1)}, u8[1568,1024]{1,0:T(8,128)(4,1)}, f32[2,1568,1024]{2,1,0:T(8,128)}) fusion(f32[1024]{0:T(1024)S(1)} %convert_element_type.188, bf16[2,1568,1024]{2,1,0:T(8,128)(2,1)} %all-gather.12.cloned.1.call-done, bf16[1024,1024]{1,0:T(8,128)(2,1)} %all-gather.14.cloned.1.call-done), kind=kOutput, calls=%fused_computation.148 | convolution fusion | flops 6618415104 | bytes 24580096 | tf_op jit(solution)/shard_map/njz,zc->njc/dot_general | solution.py:189
  556.4 119.1 %all-gather.18.cloned.1.call-done = bf16[2,1568,1024]{2,1,0:T(8,128)(2,1)} async-done(((bf16[2,392,1024]{2,1,0:T(8,128)(2,1)}), bf16[2,1568,1024]{2,1,0:T(8,128)(2,1)}) %all-gather.18.cloned.1.call-update) | async-done | bytes 6422544 | tf_op jit(solution)/shard_map/all_gather | solution.py:204
  675.5 15.1 convert_reduce_fusion
  690.6 7.5 convolution_convert_fusion
  698.1 13.7 copy.88
  711.8 5.4 copy.99
  717.3 111.1 %reduce-scatter.29.cloned.1.call-done = bf16[392,2048]{1,0:T(8,128)(2,1)} async-done(((bf16[1568,2048]{1,0:T(8,128)(2,1)}), bf16[392,2048]{1,0:T(8,128)(2,1)}) %reduce-scatter.29.cloned.1.call-update) | async-done | bytes 1605648
  828.5 5.3 reshape.178
  841.8 12.7 bitcast_convert_fusion.2
  854.6 31.3 %fusion.62 = bf16[2,1568,1024]{2,1,0:T(8,128)(2,1)S(1)} fusion(f32[2,1568,1024]{2,1,0:T(8,128)} %get-tuple-element.432, f32[1024]{0:T(1024)S(1)} %convert_element_type.188, u8[1568,1024]{1,0:T(8,128)(4,1)S(1)} %copy-done.29, u8[1568,1024]{1,0:T(8,128)(4,1)S(1)} %copy-done.28), kind=kLoop, calls=%fused_computation.65 | loop fusion | flops 227999744 | bytes 22482944 | tf_op jit(solution)/shard_map/convert_element_type | solution.py:193
  888.6 10.5 bitcast_convert_fusion.1
  899.2 60.8 %all-gather.20.cloned.1.call-done = bf16[2,1568,1024]{2,1,0:T(8,128)(2,1)} async-done(((bf16[2,392,1024]{2,1,0:T(8,128)(2,1)}), bf16[2,1568,1024]{2,1,0:T(8,128)(2,1)}) %all-gather.20.cloned.1.call-update) | async-done | bytes 6422544 | tf_op jit(solution)/shard_map/all_gather | solution.py:233
  967.3 388.1 %while.56 = (s32[]{:T(128)}, bf16[2,1568,256]{1,2,0:T(8,128)(2,1)}, bf16[2,1568,256]{2,1,0:T(8,128)(2,1)}, bf16[2,1568,256]{1,2,0:T(8,128)(2,1)}, bf16[2,1568,25...) while((s32[]{:T(128)}, bf16[2,1568,256]{1,2,0:T(8,128)(2,1)}, ...), condition=%wide.region_19.20_spmd, body=%wide.region_15.19_spmd.sunk | while | flops 3213581312 | bytes 417577472 | solution.py:240
  977.7 174.2 %while.58 = (s32[]{:T(128)}, f32[1568,4,64]{0,2,1:T(8,128)}, f32[1568,4,64]{0,2,1:T(8,128)}, bf16[2,784,4,64]{1,3,2,0:T(8,128)(2,1)}, bf16[2,784,4,64]{1,3,2,0:T...) while((s32[]{:T(128)}, f32[1568,4,64]{0,2,1:T(8,128)}, ...), condition=%wide.region_18.18_spmd.clone, body=%wide.region_16.17_spmd.clone.sunk | while | flops 3212778496 | bytes 332231680 | solution.py:90
  977.7 5.1 subtract_exponential_fusion.3
  982.9 5.3 fusion.178
  990.5 11.9 fusion.176
  1002.5 31.2 %fusion.179 = bf16[2,784,4,64]{1,3,2,0:T(8,128)(2,1)} fusion(bf16[2,784,4,64]{1,3,2,0:T(8,128)(2,1)} %get-tuple-element.710, s32[]{:T(128)S(6)} %copy.167, bf16[1568,4,64]{0,2,1:T(8,128)(2,1)} %get-tuple-element.723, f32[4,784,1568]{2,1,0:T(8,128)} %copy-done, f32[4,784,1568]{2,1,0:T(8,128)} %fusion.176), kind=kOutput, calls=%fused_computation.34.clone.1 | convolution fusion | flops 654199424 | bytes 84803584 | tf_op jit(solution)/shard_map/while/body/eval_jaxpr/while/body/eval_jaxpr/hbl,lhe->bhe/dot_general | solution.py:75
  1033.7 30.1 %fusion.177 = f32[1568,4,64]{0,2,1:T(8,128)S(1)} fusion(f32[4,784,1568]{2,1,0:T(8,128)} %copy-done, f32[4,784,1568]{2,1,0:T(8,128)} %fusion.176, f32[1568,4,64]{0,2,1:T(8,128)S(1)} %copy-done.13, pred[]{:T(512)S(6)} %compare.3, bf16[2,784,4,64]{1,3,2,0:T(8,128)(2,1)S(1)} %copy-done.2, s32[]{:T(128)S(6)} %copy.167), kind=kOutput, calls=%fused_computation.30.clone.1 | convolution fusion | flops 654801536 | bytes 87261192 | tf_op jit(solution)/shard_map/while/body/eval_jaxpr/while/body/eval_jaxpr/hbl,bhe->lhe/dot_general | solution.py:78
  1070.1 7.2 fusion.178
  1078.3 11.2 fusion.176
  1089.4 31.2 %fusion.179 = bf16[2,784,4,64]{1,3,2,0:T(8,128)(2,1)} fusion(bf16[2,784,4,64]{1,3,2,0:T(8,128)(2,1)} %get-tuple-element.710, s32[]{:T(128)S(6)} %copy.167, bf16[1568,4,64]{0,2,1:T(8,128)(2,1)} %get-tuple-element.723, f32[4,784,1568]{2,1,0:T(8,128)} %copy-done, f32[4,784,1568]{2,1,0:T(8,128)} %fusion.176), kind=kOutput, calls=%fused_computation.34.clone.1 | convolution fusion | flops 654199424 | bytes 84803584 | tf_op jit(solution)/shard_map/while/body/eval_jaxpr/while/body/eval_jaxpr/hbl,lhe->bhe/dot_general | solution.py:75
  1120.6 30.1 %fusion.177 = f32[1568,4,64]{0,2,1:T(8,128)S(1)} fusion(f32[4,784,1568]{2,1,0:T(8,128)} %copy-done, f32[4,784,1568]{2,1,0:T(8,128)} %fusion.176, f32[1568,4,64]{0,2,1:T(8,128)S(1)} %copy-done.13, pred[]{:T(512)S(6)} %compare.3, bf16[2,784,4,64]{1,3,2,0:T(8,128)(2,1)S(1)} %copy-done.2, s32[]{:T(128)S(6)} %copy.167), kind=kOutput, calls=%fused_computation.30.clone.1 | convolution fusion | flops 654801536 | bytes 87261192 | tf_op jit(solution)/shard_map/while/body/eval_jaxpr/while/body/eval_jaxpr/hbl,bhe->lhe/dot_general | solution.py:78
  1171.9 173.4 %while.58 = (s32[]{:T(128)}, f32[1568,4,64]{0,2,1:T(8,128)}, f32[1568,4,64]{0,2,1:T(8,128)}, bf16[2,784,4,64]{1,3,2,0:T(8,128)(2,1)}, bf16[2,784,4,64]{1,3,2,0:T...) while((s32[]{:T(128)}, f32[1568,4,64]{0,2,1:T(8,128)}, ...), condition=%wide.region_18.18_spmd.clone, body=%wide.region_16.17_spmd.clone.sunk | while | flops 3212778496 | bytes 332231680 | solution.py:90
  1177.0 5.2 fusion.178
  1184.6 11.2 fusion.176
  1195.8 31.2 %fusion.179 = bf16[2,784,4,64]{1,3,2,0:T(8,128)(2,1)} fusion(bf16[2,784,4,64]{1,3,2,0:T(8,128)(2,1)} %get-tuple-element.710, s32[]{:T(128)S(6)} %copy.167, bf16[1568,4,64]{0,2,1:T(8,128)(2,1)} %get-tuple-element.723, f32[4,784,1568]{2,1,0:T(8,128)} %copy-done, f32[4,784,1568]{2,1,0:T(8,128)} %fusion.176), kind=kOutput, calls=%fused_computation.34.clone.1 | convolution fusion | flops 654199424 | bytes 84803584 | tf_op jit(solution)/shard_map/while/body/eval_jaxpr/while/body/eval_jaxpr/hbl,lhe->bhe/dot_general | solution.py:75
  1227.0 30.1 %fusion.177 = f32[1568,4,64]{0,2,1:T(8,128)S(1)} fusion(f32[4,784,1568]{2,1,0:T(8,128)} %copy-done, f32[4,784,1568]{2,1,0:T(8,128)} %fusion.176, f32[1568,4,64]{0,2,1:T(8,128)S(1)} %copy-done.13, pred[]{:T(512)S(6)} %compare.3, bf16[2,784,4,64]{1,3,2,0:T(8,128)(2,1)S(1)} %copy-done.2, s32[]{:T(128)S(6)} %copy.167), kind=kOutput, calls=%fused_computation.30.clone.1 | convolution fusion | flops 654801536 | bytes 87261192 | tf_op jit(solution)/shard_map/while/body/eval_jaxpr/while/body/eval_jaxpr/hbl,bhe->lhe/dot_general | solution.py:78
  1263.4 7.2 fusion.178
  1271.6 11.2 fusion.176
  1282.8 31.2 %fusion.179 = bf16[2,784,4,64]{1,3,2,0:T(8,128)(2,1)} fusion(bf16[2,784,4,64]{1,3,2,0:T(8,128)(2,1)} %get-tuple-element.710, s32[]{:T(128)S(6)} %copy.167, bf16[1568,4,64]{0,2,1:T(8,128)(2,1)} %get-tuple-element.723, f32[4,784,1568]{2,1,0:T(8,128)} %copy-done, f32[4,784,1568]{2,1,0:T(8,128)} %fusion.176), kind=kOutput, calls=%fused_computation.34.clone.1 | convolution fusion | flops 654199424 | bytes 84803584 | tf_op jit(solution)/shard_map/while/body/eval_jaxpr/while/body/eval_jaxpr/hbl,lhe->bhe/dot_general | solution.py:75
  1314.0 30.1 %fusion.177 = f32[1568,4,64]{0,2,1:T(8,128)S(1)} fusion(f32[4,784,1568]{2,1,0:T(8,128)} %copy-done, f32[4,784,1568]{2,1,0:T(8,128)} %fusion.176, f32[1568,4,64]{0,2,1:T(8,128)S(1)} %copy-done.13, pred[]{:T(512)S(6)} %compare.3, bf16[2,784,4,64]{1,3,2,0:T(8,128)(2,1)S(1)} %copy-done.2, s32[]{:T(128)S(6)} %copy.167), kind=kOutput, calls=%fused_computation.30.clone.1 | convolution fusion | flops 654801536 | bytes 87261192 | tf_op jit(solution)/shard_map/while/body/eval_jaxpr/while/body/eval_jaxpr/hbl,bhe->lhe/dot_general | solution.py:78
  1361.4 5.5 fusion.122
  1367.0 10.2 fusion.119
  1377.2 10.2 convolution_convert_fusion.1
  1387.5 13.7 copy.86
  1401.2 5.4 copy.98
  1406.8 11.1 reduce-scatter.17.cloned.1.call-done
  1417.9 7.6 bitcast_convert_fusion
  1425.5 13.7 copy.90
  1439.2 5.4 copy.100
  1445.6 87.3 %reduce-scatter.27.cloned.1.call-done = bf16[392,2048]{1,0:T(8,128)(2,1)} async-done(((bf16[1568,2048]{1,0:T(8,128)(2,1)}), bf16[392,2048]{1,0:T(8,128)(2,1)}) %reduce-scatter.27.cloned.1.call-update) | async-done | bytes 1605648
  1532.9 5.3 reshape.176
  1539.4 48.4 %all-reduce.4.cloned.1.call-done = (bf16[3,256,256]{1,2,0:T(8,128)(2,1)}, bf16[256,256]{1,0:T(8,128)(2,1)}, bf16[256,1024]{1,0:T(8,128)(2,1)}, bf16[1024,256]{1,0:T(8,128)(2,1)}) async-done(((bf16[3,256,256]{1,2,0:T(8,128)(2,1)}, bf16[256,256]{1,0:T(8,128)(2,1)}, bf16[256,1024]{1,0:T(8,128)(2,1)}, bf16[1024,256]{1,0:T(8,128)(2,1)}), (bf16[3,256,256]{1,2,0:T(8,128)(2,1)}, bf16[256,256]{1,0:T(8,128)(2,1)}, ...) | async-done | bytes 1572880 | tf_op jit(solution)/shard_map/psum | solution.py:282
  1594.9 108.1 %reduce-scatter.31.cloned.1.call-done = bf16[392,2048]{1,0:T(8,128)(2,1)} async-done(((bf16[1568,2048]{1,0:T(8,128)(2,1)}), bf16[392,2048]{1,0:T(8,128)(2,1)}) %reduce-scatter.31.cloned.1.call-update) | async-done | bytes 1605648
  1703.0 5.3 reshape.180
  1711.6 41.9 %all-reduce = (f32[1024]{0:T(1024)S(1)}, f32[1024]{0:T(1024)S(1)}, f32[1024]{0:T(1024)S(1)}, f32[1024]{0:T(1024)S(1)}, f32[1024]{0:T(1024)S(1)}, /*index=5*/f32[...) all-reduce(f32[1024]{0:T(1024)S(1)} %get-tuple-element.338, ...), channel_id=1, replica_groups=mesh['tensor'=4,'group'=4,'cross'=2] {'tensor','group','cross'}, use_global_device_ids=true, to_apply=%region_24.25 | all-reduce | flops 12288 | bytes 98304 | tf_op jit(solution)/shard_map/psum | solution.py:287
  1759.1 7.1 fusion.97
  (357 shorter events, 204.5 us)
Async XLA Ops:
  7.2 6.6 copy-start.3
  7.2 26.3 %all-gather.10.cloned.1.call-start = ((), (), s32[]{:S(2)}) async-start(), calls=%async_computation.9 | async-start | bytes 1966080 | tf_op jit(solution)/shard_map/all_gather | solution.py:147
  7.9 146.1 %all-gather.8.cloned.1.call-start = ((), (), s32[]{:S(2)}) async-start(), calls=%async_computation.8 | async-start | bytes 8028160 | tf_op jit(solution)/shard_map/all_gather | solution.py:157
  15.6 374.2 %reduce-scatter.25.cloned.1.call-start = ((), (), s32[]{:S(2)}) async-start(), calls=%async_computation.19 | async-start | bytes 8028160
  174.0 6.3 copy-start.8
  214.6 6.2 copy-start.8
  278.6 115.7 %copy-start.4 = (bf16[2,392,1024]{2,1,0:T(8,128)(2,1)S(1)}, bf16[2,392,1024]{2,1,0:T(8,128)(2,1)}, u32[]{:S(2)}) copy-start(bf16[2,392,1024]{2,1,0:T(8,128)(2,1)} %param.24) | copy-start | bytes 4816900
  278.6 135.8 %all-gather.14.cloned.1.call-start = ((), (), s32[]{:S(2)}) async-start(), calls=%async_computation.11 | async-start | bytes 2621440 | tf_op jit(solution)/shard_map/all_gather | solution.py:149
  279.2 254.7 %all-gather.12.cloned.1.call-start = ((), (), s32[]{:S(2)}) async-start(), calls=%async_computation.10 | async-start | bytes 8028160 | tf_op jit(solution)/shard_map/all_gather | solution.py:188
  279.3 558.7 %copy-start.32 = (f32[1024]{0:T(1024)}, f32[1024]{0:T(1024)S(1)}, u32[]{:S(2)}) copy-start(f32[1024]{0:T(1024)S(1)} %convert_element_type.184) | copy-start | bytes 12292
  279.3 558.7 %copy-start.39 = (f32[1024]{0:T(1024)}, f32[1024]{0:T(1024)S(1)}, u32[]{:S(2)}) copy-start(f32[1024]{0:T(1024)S(1)} %convert_element_type.185) | copy-start | bytes 12292
  394.3 443.7 %copy-start.6 = (bf16[392,2,1024]{2,1,0:T(2,128)(2,1)}, bf16[392,2,1024]{2,1,0:T(2,128)(2,1)S(1)}, u32[]{:S(2)}) copy-start(bf16[392,2,1024]{2,1,0:T(2,128)(2,1)S(1)} %reshape.174) | copy-start | bytes 4816900
  394.9 443.1 %copy-start.34 = (f32[2,392]{1,0:T(2,128)}, f32[2,392]{1,0:T(2,128)S(1)}, u32[]{:S(2)}) copy-start(f32[2,392]{1,0:T(2,128)S(1)} %broadcast_multiply_fusion.4) | copy-start | bytes 9412
  395.8 442.2 %copy-start.41 = (f32[2,392]{1,0:T(2,128)}, f32[2,392]{1,0:T(2,128)S(1)}, u32[]{:S(2)}) copy-start(f32[2,392]{1,0:T(2,128)S(1)} %add_rsqrt_fusion) | copy-start | bytes 9412
  397.8 5.5 copy-start.61
  397.9 158.5 %all-gather.16.cloned.1.call-start = ((), (), s32[]{:S(2)}) async-start(), calls=%async_computation.12 | async-start | bytes 2621440 | tf_op jit(solution)/shard_map/all_gather | solution.py:150
  398.5 277.0 %all-gather.18.cloned.1.call-start = ((), (), s32[]{:S(2)}) async-start(), calls=%async_computation.13 | async-start | bytes 8028160 | tf_op jit(solution)/shard_map/all_gather | solution.py:204
  399.2 438.9 %copy-start.55 = (f32[2]{0:T(128)}, f32[2]{0:T(128)S(1)}, u32[]{:S(2)}) copy-start(f32[2]{0:T(128)S(1)} %compare_convert_fusion) | copy-start | bytes 28
  403.3 425.2 %reduce-scatter.29.cloned.1.call-start = ((), (), s32[]{:S(2)}) async-start(), calls=%async_computation.21 | async-start | bytes 8028160
  675.5 15.1 copy-start.63
  690.6 7.5 copy-start.66
  717.3 242.6 %all-gather.20.cloned.1.call-start = ((), (), s32[]{:S(2)}) async-start(), calls=%async_computation.14 | async-start | bytes 8028160 | tf_op jit(solution)/shard_map/all_gather | solution.py:233
  841.7 565.0 %reduce-scatter.21.cloned.1.call-start = ((), (), s32[]{:S(2)}) async-start(), calls=%async_computation.17 | async-start | bytes 2621440 | tf_op jit(solution)/shard_map/reduce_scatter | solution.py:274
  841.8 12.8 copy-start.28
  841.8 12.8 copy-start.29
  854.5 552.2 %reduce-scatter.23.cloned.1.call-start = ((), (), s32[]{:S(2)}) async-start(), calls=%async_computation.18 | async-start | bytes 2621440 | tf_op jit(solution)/shard_map/reduce_scatter | solution.py:277
  888.5 71.4 %copy-start.27 = (bf16[256,1024]{1,0:T(8,128)(2,1)S(1)}, bf16[256,1024]{1,0:T(8,128)(2,1)}, u32[]{:S(2)}) copy-start(bf16[256,1024]{1,0:T(8,128)(2,1)} %all_gather.26) | copy-start | bytes 1572868
  899.1 507.6 %reduce-scatter.19.cloned.1.call-start = ((), (), s32[]{:S(2)}) async-start(), calls=%async_computation.16 | async-start | bytes 655360 | tf_op jit(solution)/shard_map/reduce_scatter | solution.py:271
  982.9 7.7 copy-start
  1002.4 31.2 %copy-start.2 = (bf16[2,784,4,64]{1,3,2,0:T(8,128)(2,1)S(1)}, bf16[2,784,4,64]{1,3,2,0:T(8,128)(2,1)}, u32[]{:S(2)}) copy-start(bf16[2,784,4,64]{1,3,2,0:T(8,128)(2,1)} %get-tuple-element.722) | copy-start | bytes 2408452 | tf_op jit(solution)/shard_map/while/body/eval_jaxpr/while
  1002.5 31.2 %copy-start.13 = (f32[1568,4,64]{0,2,1:T(8,128)S(1)}, f32[1568,4,64]{0,2,1:T(8,128)}, u32[]{:S(2)}) copy-start(f32[1568,4,64]{0,2,1:T(8,128)} %get-tuple-element.708) | copy-start | bytes 4816900 | tf_op jit(solution)/shard_map/while/body/eval_jaxpr/while
  1070.1 8.2 copy-start
  1089.4 31.2 %copy-start.2 = (bf16[2,784,4,64]{1,3,2,0:T(8,128)(2,1)S(1)}, bf16[2,784,4,64]{1,3,2,0:T(8,128)(2,1)}, u32[]{:S(2)}) copy-start(bf16[2,784,4,64]{1,3,2,0:T(8,128)(2,1)} %get-tuple-element.722) | copy-start | bytes 2408452 | tf_op jit(solution)/shard_map/while/body/eval_jaxpr/while
  1089.4 31.2 %copy-start.13 = (f32[1568,4,64]{0,2,1:T(8,128)S(1)}, f32[1568,4,64]{0,2,1:T(8,128)}, u32[]{:S(2)}) copy-start(f32[1568,4,64]{0,2,1:T(8,128)} %get-tuple-element.708) | copy-start | bytes 4816900 | tf_op jit(solution)/shard_map/while/body/eval_jaxpr/while
  1177.0 7.6 copy-start
  1195.8 31.2 %copy-start.2 = (bf16[2,784,4,64]{1,3,2,0:T(8,128)(2,1)S(1)}, bf16[2,784,4,64]{1,3,2,0:T(8,128)(2,1)}, u32[]{:S(2)}) copy-start(bf16[2,784,4,64]{1,3,2,0:T(8,128)(2,1)} %get-tuple-element.722) | copy-start | bytes 2408452 | tf_op jit(solution)/shard_map/while/body/eval_jaxpr/while
  1195.8 31.2 %copy-start.13 = (f32[1568,4,64]{0,2,1:T(8,128)S(1)}, f32[1568,4,64]{0,2,1:T(8,128)}, u32[]{:S(2)}) copy-start(f32[1568,4,64]{0,2,1:T(8,128)} %get-tuple-element.708) | copy-start | bytes 4816900 | tf_op jit(solution)/shard_map/while/body/eval_jaxpr/while
  1263.4 8.2 copy-start
  1282.8 31.2 %copy-start.2 = (bf16[2,784,4,64]{1,3,2,0:T(8,128)(2,1)S(1)}, bf16[2,784,4,64]{1,3,2,0:T(8,128)(2,1)}, u32[]{:S(2)}) copy-start(bf16[2,784,4,64]{1,3,2,0:T(8,128)(2,1)} %get-tuple-element.722) | copy-start | bytes 2408452 | tf_op jit(solution)/shard_map/while/body/eval_jaxpr/while
  1282.8 31.2 %copy-start.13 = (f32[1568,4,64]{0,2,1:T(8,128)S(1)}, f32[1568,4,64]{0,2,1:T(8,128)}, u32[]{:S(2)}) copy-start(f32[1568,4,64]{0,2,1:T(8,128)} %get-tuple-element.708) | copy-start | bytes 4816900 | tf_op jit(solution)/shard_map/while/body/eval_jaxpr/while
  1355.4 6.0 copy-start.25
  1366.9 50.9 %reduce-scatter.17.cloned.1.call-start = ((), (), s32[]{:S(2)}) async-start(), calls=%async_computation.15 | async-start | bytes 1966080 | tf_op jit(solution)/shard_map/reduce_scatter | solution.py:268
  1377.2 155.7 %reduce-scatter.27.cloned.1.call-start = ((), (), s32[]{:S(2)}) async-start(), calls=%async_computation.20 | async-start | bytes 8028160
  1406.6 11.3 copy-start.30
  1406.6 181.2 %all-reduce.4.cloned.1.call-start = ((), (), s32[]{:S(2)}) async-start(), calls=%async_computation.23 | async-start | bytes 3145728 | tf_op jit(solution)/shard_map/psum | solution.py:282
  1417.9 285.2 %reduce-scatter.31.cloned.1.call-start = ((), (), s32[]{:S(2)}) async-start(), calls=%async_computation.22 | async-start | bytes 8028160
  1444.7 93.6 %copy-start.18 = (bf16[2,1568,256]{1,2,0:T(8,128)(2,1)S(1)}, bf16[2,1568,256]{1,2,0:T(8,128)(2,1)}, u32[]{:S(2)}) copy-start(bf16[2,1568,256]{1,2,0:T(8,128)(2,1)} %get-tuple-element.183) | copy-start | bytes 4816900
  1587.8 6.0 copy-start.31
  1591.5 116.8 %copy-start.5 = (bf16[2,392,1024]{2,1,0:T(8,128)(2,1)S(1)}, bf16[2,392,1024]{2,1,0:T(8,128)(2,1)}, u32[]{:S(2)}) copy-start(bf16[2,392,1024]{2,1,0:T(8,128)(2,1)} %param.24) | copy-start | bytes 4816900
  1591.5 116.8 %copy-start.38 = (f32[2,392]{1,0:T(2,128)S(1)}, f32[2,392]{1,0:T(2,128)}, u32[]{:S(2)}) copy-start(f32[2,392]{1,0:T(2,128)} %copy-done.37) | copy-start | bytes 9412
  1591.5 116.8 %copy-start.44 = (f32[1024]{0:T(1024)S(1)}, f32[1024]{0:T(1024)}, u32[]{:S(2)}) copy-start(f32[1024]{0:T(1024)} %copy-done.43) | copy-start | bytes 12292
  1591.5 116.8 %copy-start.46 = (f32[2,392]{1,0:T(2,128)S(1)}, f32[2,392]{1,0:T(2,128)}, u32[]{:S(2)}) copy-start(f32[2,392]{1,0:T(2,128)} %copy-done.45) | copy-start | bytes 9412
  1594.8 116.7 %copy-start.51 = (f32[1024]{0:T(1024)S(1)}, f32[1024]{0:T(1024)}, u32[]{:S(2)}) copy-start(f32[1024]{0:T(1024)} %get-tuple-element.417) | copy-start | bytes 12292
  1594.8 116.7 %copy-start.52 = (f32[1024]{0:T(1024)S(1)}, f32[1024]{0:T(1024)}, u32[]{:S(2)}) copy-start(f32[1024]{0:T(1024)} %get-tuple-element.336) | copy-start | bytes 12292
  1594.8 116.7 %copy-start.53 = (f32[1024]{0:T(1024)S(1)}, f32[1024]{0:T(1024)}, u32[]{:S(2)}) copy-start(f32[1024]{0:T(1024)} %get-tuple-element.342) | copy-start | bytes 12292
  1594.8 116.7 %copy-start.54 = (f32[1024]{0:T(1024)S(1)}, f32[1024]{0:T(1024)}, u32[]{:S(2)}) copy-start(f32[1024]{0:T(1024)} %get-tuple-element.419) | copy-start | bytes 12292
  1594.9 164.2 %copy-start.7 = (bf16[392,2,1024]{2,1,0:T(2,128)(2,1)S(1)}, bf16[392,2,1024]{2,1,0:T(2,128)(2,1)}, u32[]{:S(2)}) copy-start(bf16[392,2,1024]{2,1,0:T(2,128)(2,1)} %copy-done.6) | copy-start | bytes 4816900
  1594.9 164.2 %copy-start.33 = (f32[1024]{0:T(1024)S(1)}, f32[1024]{0:T(1024)}, u32[]{:S(2)}) copy-start(f32[1024]{0:T(1024)} %copy-done.32) | copy-start | bytes 12292
  1594.9 164.2 %copy-start.35 = (f32[2,392]{1,0:T(2,128)S(1)}, f32[2,392]{1,0:T(2,128)}, u32[]{:S(2)}) copy-start(f32[2,392]{1,0:T(2,128)} %copy-done.34) | copy-start | bytes 9412
  1594.9 164.2 %copy-start.40 = (f32[1024]{0:T(1024)S(1)}, f32[1024]{0:T(1024)}, u32[]{:S(2)}) copy-start(f32[1024]{0:T(1024)} %copy-done.39) | copy-start | bytes 12292
  1594.9 164.2 %copy-start.42 = (f32[2,392]{1,0:T(2,128)S(1)}, f32[2,392]{1,0:T(2,128)}, u32[]{:S(2)}) copy-start(f32[2,392]{1,0:T(2,128)} %copy-done.41) | copy-start | bytes 9412
  1594.9 164.2 %copy-start.48 = (f32[2,392]{1,0:T(2,128)S(1)}, f32[2,392]{1,0:T(2,128)}, u32[]{:S(2)}) copy-start(f32[2,392]{1,0:T(2,128)} %copy-done.47) | copy-start | bytes 9412
  1594.9 164.2 %copy-start.50 = (f32[2,392]{1,0:T(2,128)S(1)}, f32[2,392]{1,0:T(2,128)}, u32[]{:S(2)}) copy-start(f32[2,392]{1,0:T(2,128)} %copy-done.49) | copy-start | bytes 9412
  1594.9 164.2 %copy-start.56 = (f32[2]{0:T(128)S(1)}, f32[2]{0:T(128)}, u32[]{:S(2)}) copy-start(f32[2]{0:T(128)} %copy-done.55) | copy-start | bytes 28
  (42 other events, 113.0 us)
Sparse Core Ops, SparseCore 0:
  9.6 23.8 all-gather.9
  35.6 118.3 all-gather.7
  278.7 111.0 reduce-scatter.24
  391.2 23.0 all-gather.13
  416.4 117.4 all-gather.11
  535.3 21.0 all-gather.15
  557.9 117.4 all-gather.17
  717.4 111.0 reduce-scatter.28
  841.8 118.0 all-gather.19
  962.3 29.5 reduce-scatter.20
  994.6 31.4 reduce-scatter.22
  1367.1 19.8 reduce-scatter.18
  1389.6 28.1 reduce-scatter.16
  1420.0 112.8 reduce-scatter.26
  1535.2 52.5 all-reduce.3
  1590.1 112.8 reduce-scatter.30
where the time goes:
time: 1780 us; the launch traced here: 1770 us
  waiting for transfers between devices  919 us (52%)
  matrix products  495 us (28%)
  local copies, waits for them, and re-layouts  199 us (11%)
  other arithmetic  89.5 us (5%)
  blocking collectives  52.7 us (3%)
    unnamed x20, waiting for transfers between devices  419 us
    dot_general x4, matrix products, one_part(): jnp.einsum('hbl,lhe->bhe', logit_grad, key_heads, preferred_element_type=...  125 us
    all_gather x1, waiting for transfers between devices, local(): first_gathered = lax.all_gather(first_rows, 'tensor', axis=1, tiled=True)  121 us
    dot_general x4, matrix products, one_part(): jnp.einsum('hbl,bhe->lhe', logit_grad, query_part, preferred_element_type...  120 us
    all_gather x1, waiting for transfers between devices, local(): second_gathered = lax.all_gather(second_rows, 'tensor', axis=1, tiled=True)  120 us
    all_gather x1, waiting for transfers between devices, local(): feed_grad_gathered = lax.all_gather(feed_grad, 'tensor', axis=1, tiled=True)  119 us
    unnamed x117, local copies, waits for them, and re-layouts  103 us
    all_gather x1, waiting for transfers between devices, local(): branch_gathered = lax.all_gather(branch_grad, 'tensor', axis=1, tiled=True)  60.8 us
  transfers between devices with their start and end apart: 16, of which 13 were waited for; matrix products, arithmetic and copies ran while one was open for 32% of the time, Pallas kernels for 0%

commit v1 on v0

v1 whole, which is shorter than its diff:
```python
import functools

import jax
import jax.numpy as jnp
from jax import lax
from jax.experimental import pallas as pl
from jax.experimental.pallas import tpu as pltpu
from jax.sharding import PartitionSpec as P

HEAD = 64
LANES = 128

epsilon = 1e-06
root_half = 0.7071067811865476
inv_root_two_pi = 0.3989422804014327
log_two = 0.6931471805599453
query_scale = HEAD**-0.5 / log_two

f32 = jnp.float32
bf16 = jnp.bfloat16

NN = (((1,), (0,)), ((), ()))
NT = (((1,), (1,)), ((), ()))
TN = (((0,), (0,)), ((), ()))


def dot(a, b, dims=NN):
    return lax.dot_general(a, b, dims, preferred_element_type=f32)


def attend_forward_kernel(q_ref, ka, kb, va, vb, o_ref, lse_ref, keys, values_low, values_high):
    n = ka.shape[0]

    @pl.when(pl.program_id(1) == 0)
    def _():
        low = lax.broadcasted_iota(jnp.int32, (n, LANES), 1) < HEAD
        one = jnp.ones((n, LANES), bf16)
        for i, (k, v) in enumerate(((ka, va), (kb, vb))):
            rows = slice(i * n, (i + 1) * n)
            keys[rows] = k[...]
            values_low[rows] = jnp.where(low, v[...], one)
            values_high[rows] = jnp.where(low, one, v[...])

    q = q_ref[...]
    low = lax.broadcasted_iota(jnp.int32, q.shape, 1) < HEAD
    zero = jnp.zeros_like(q)
    sums, tops = [], []
    for mine, v in ((jnp.where(low, q, zero), values_low), (jnp.where(low, zero, q), values_high)):
        s = dot(mine, keys[...], NT)
        top = jnp.max(s, axis=1, keepdims=True)
        p = jnp.exp2(s - top).astype(bf16)
        sums.append(dot(p, v[...]))
        tops.append(top)
    total = pltpu.roll(jnp.where(low, sums[1], sums[0]), HEAD, 1)
    o_ref[...] = (jnp.where(low, sums[0], sums[1]) / total).astype(bf16)
    lse_ref[...] = jnp.where(low, tops[0], tops[1]) + jnp.log2(total)


def attend_backward_kernel(
    q_ref, g_ref, o_ref, lse_ref, ka, kb, va, vb,
    dq_ref, dka, dkb, dva, dvb,
    keys, values, dk, dv,
):
    n = ka.shape[0]
    step = pl.program_id(1)

    @pl.when(step == 0)
    def _():
        for i, (k, v) in enumerate(((ka, va), (kb, vb))):
            keys[i * n : (i + 1) * n] = k[...]
            values[i * n : (i + 1) * n] = v[...]
        dk[...] = jnp.zeros_like(dk)
        dv[...] = jnp.zeros_like(dv)

    q, g = q_ref[...], g_ref[...]
    low = lax.broadcasted_iota(jnp.int32, q.shape, 1) < HEAD
    product = g.astype(f32) * o_ref[...].astype(f32)
    lse = lse_ref[...]
    q_t, g_t = q.T, g.T
    dqs = []
    for h in range(2):

        def own(a):
            zero = jnp.zeros_like(a)
            return jnp.where(low, a, zero) if h == 0 else jnp.where(low, zero, a)

        inner = jnp.sum(own(product), axis=1, keepdims=True)
        p = jnp.exp2(dot(own(q), keys[...], NT) - lse[:, HEAD * h : HEAD * h + 1])
        ds = (p * (dot(own(g), values[...], NT) - inner)).astype(bf16)
        dqs.append(dot(ds, keys[...]))
        rows = slice(HEAD * h, HEAD * (h + 1))
        dv[rows] += dot(g_t[rows], p.astype(bf16))
        dk[rows] += dot(q_t[rows], ds)
    dq_ref[...] = (jnp.where(low, dqs[0], dqs[1]) * HEAD**-0.5).astype(bf16)

    @pl.when(step == pl.num_programs(1) - 1)
    def _():
        key_total, value_total = (dk[...] * log_two).T, dv[...].T
        dka[...] = key_total[:n].astype(bf16)
        dkb[...] = key_total[n:].astype(bf16)
        dva[...] = value_total[:n].astype(bf16)
        dvb[...] = value_total[n:].astype(bf16)


def attend_forward(q, ka, kb, va, vb):
    n, width = q.shape
    spec = pl.BlockSpec((n, LANES), lambda i, j: (0, i))
    return pl.pallas_call(
        attend_forward_kernel,
        grid=(width // LANES, 1),
        in_specs=[spec] * 5,
        out_specs=[spec] * 2,
        out_shape=[jax.ShapeDtypeStruct((n, width), bf16), jax.ShapeDtypeStruct((n, width), f32)],
        scratch_shapes=[pltpu.VMEM((2 * n, LANES), bf16)] * 3,
        name="attend_forward",
        cost_estimate=pl.CostEstimate(
            flops=8 * n * n * width, bytes_accessed=16 * n * width, transcendentals=n * n * width // 32
        ),
        compiler_params=pltpu.CompilerParams(vmem_limit_bytes=56 << 20),
    )(q, ka, kb, va, vb)


def attend_backward(q, g, o, lse, ka, kb, va, vb):
    n, width = q.shape
    spec = pl.BlockSpec((n, LANES), lambda i, j: (0, i))
    return pl.pallas_call(
        attend_backward_kernel,
        grid=(width // LANES, 1),
        in_specs=[spec] * 8,
        out_specs=[spec] * 5,
        out_shape=[jax.ShapeDtypeStruct((n, width), bf16)] * 5,
        scratch_shapes=[pltpu.VMEM((2 * n, LANES), bf16)] * 2 + [pltpu.VMEM((LANES, 2 * n), f32)] * 2,
        name="attend_backward",
        cost_estimate=pl.CostEstimate(
            flops=20 * n * n * width, bytes_accessed=28 * n * width, transcendentals=n * n * width // 32
        ),
        compiler_params=pltpu.CompilerParams(vmem_limit_bytes=60 << 20),
    )(q, g, o, lse, ka, kb, va, vb)


def normalize(values):
    center = values - jnp.mean(values, axis=-1, keepdims=True)
    inverse = lax.rsqrt(jnp.mean(center * center, axis=-1, keepdims=True) + epsilon)
    return (center * inverse, inverse)


def normalize_back(upstream, normed, inverse, norm_gain):
    scaled = upstream * norm_gain
    return inverse * (
        scaled
        - jnp.mean(scaled, axis=-1, keepdims=True)
        - normed * jnp.mean(scaled * normed, axis=-1, keepdims=True)
    )


def clip_exchange(tensor_count, group_count):
    there, back = [], []
    for turn in range(2):
        pairs = []
        for z in range(tensor_count):
            for g in range(group_count):
                slot = (turn + z) % 2
                target = (2 * slot + g % 2) * group_count + g - g % 2 + z // 2
                pairs.append((z * group_count + g, target))
        there.append(pairs)
        back.append([(b, a) for a, b in pairs])
    return there, back


def local(
    inputs,
    clips_here,
    first_gain,
    first_shift,
    query_key_value,
    query_bias,
    value_bias,
    output_weight,
    output_bias,
    second_gain,
    second_shift,
    expand_weight,
    expand_bias,
    contract_weight,
    contract_bias,
    output_grad,
):
    slot_count, rows, width = inputs.shape
    tensor_index = lax.axis_index("tensor")
    tensor_count = lax.axis_size("tensor")
    group_index = lax.axis_index("group")
    group_count = lax.axis_size("group")
    both = ("tensor", "group")
    there, back = clip_exchange(tensor_count, group_count)
    pair = [(g, g + 1 - 2 * (g % 2)) for g in range(group_count)]

    def to_chip(array):
        pieces = []
        for turn in range(2):
            slot = (turn + tensor_index) % 2
            pieces.append(
                lax.ppermute(lax.dynamic_index_in_dim(array, slot, keepdims=False), both, there[turn])
            )
        return jnp.concatenate(pieces, axis=0)

    def to_owner(array):
        received = [
            lax.ppermute(array[turn * rows : (turn + 1) * rows], both, back[turn]) for turn in range(2)
        ]
        even = tensor_index % 2 == 0
        return jnp.stack(
            [jnp.where(even, received[0], received[1]), jnp.where(even, received[1], received[0])]
        )

    def gather(shard):
        return lax.all_gather(shard, both, axis=0).reshape(tensor_count, group_count, *shard.shape)

    alive = (jnp.arange(slot_count, dtype=jnp.int32) < clips_here[0]).astype(bf16)[:, None, None]
    tokens = to_chip(inputs).astype(f32)
    triple = gather(query_key_value).transpose(2, 1, 3, 0, 4).reshape(3, width, width)
    mixing = gather(output_weight).transpose(0, 2, 1, 3).reshape(width, width)
    up = gather(expand_weight).transpose(1, 2, 0, 3).reshape(width, -1)
    down = gather(contract_weight).transpose(0, 2, 1, 3).reshape(-1, width)
    bias_sizes = (query_bias.shape[0], value_bias.shape[0], expand_bias.shape[0])
    biases = lax.all_gather(jnp.concatenate([query_bias, value_bias, expand_bias]), "tensor", axis=0)
    query_offset = biases[:, : bias_sizes[0]].reshape(-1).astype(f32)
    value_offset = biases[:, bias_sizes[0] : bias_sizes[0] + bias_sizes[1]].reshape(-1).astype(f32)
    hidden_offset = biases[:, bias_sizes[0] + bias_sizes[1] :].reshape(-1).astype(f32)
    top = to_chip(output_grad * alive)

    gain_one = first_gain.astype(f32)
    gain_two = second_gain.astype(f32)
    first_plain, first_inverse = normalize(tokens)
    first_rows = (first_plain * gain_one + first_shift.astype(f32)).astype(bf16)
    keys = dot(first_rows, triple[1]).astype(bf16)
    values = (dot(first_rows, triple[2]) + value_offset).astype(bf16)
    far_keys = lax.ppermute(keys, "group", pair)
    far_values = lax.ppermute(values, "group", pair)
    queries = ((dot(first_rows, triple[0]) + query_offset) * query_scale).astype(bf16)
    attended, log_totals = attend_forward(queries, keys, far_keys, values, far_values)
    middle = tokens + dot(attended, mixing) + output_bias.astype(f32)
    second_plain, second_inverse = normalize(middle)
    second_rows = (second_plain * gain_two + second_shift.astype(f32)).astype(bf16)
    hidden_pre = dot(second_rows, up) + hidden_offset
    normal_cdf = 0.5 * (1.0 + lax.erf(hidden_pre * root_half))
    hidden = (hidden_pre * normal_cdf).astype(bf16)
    slope = normal_cdf + hidden_pre * (inv_root_two_pi * jnp.exp(-0.5 * hidden_pre * hidden_pre))
    output = to_owner((middle + dot(hidden, down) + contract_bias.astype(f32)).astype(bf16))

    contract_bias_part = jnp.sum(top.astype(f32), axis=0)
    contract_part = dot(hidden, top, TN)
    pre_grad = (dot(top, down, NT) * slope).astype(bf16)
    expand_bias_part = jnp.sum(pre_grad.astype(f32), axis=0)
    expand_part = dot(second_rows, pre_grad, TN)
    second_grad = dot(pre_grad, up, NT)
    second_gain_part = jnp.sum(second_grad * second_plain, axis=0)
    second_shift_part = jnp.sum(second_grad, axis=0)
    middle_grad = top.astype(f32) + normalize_back(second_grad, second_plain, second_inverse, gain_two)
    branch_grad = middle_grad.astype(bf16)
    output_bias_part = jnp.sum(branch_grad.astype(f32), axis=0)
    mixing_part = dot(attended, branch_grad, TN)
    attended_grad = dot(branch_grad, mixing, NT).astype(bf16)
    query_grad, key_own, key_far, value_own, value_far = attend_backward(
        queries, attended_grad, attended, log_totals, keys, far_keys, values, far_values
    )
    key_grad = (key_own.astype(f32) + lax.ppermute(key_far, "group", pair).astype(f32)).astype(bf16)
    value_grad = (value_own.astype(f32) + lax.ppermute(value_far, "group", pair).astype(f32)).astype(bf16)
    query_bias_part = jnp.sum(query_grad.astype(f32), axis=0)
    value_bias_part = jnp.sum(value_grad.astype(f32), axis=0)
    triple_part = jnp.stack([dot(first_rows, d, TN) for d in (query_grad, key_grad, value_grad)])
    first_grad = (
        dot(query_grad, triple[0], NT) + dot(key_grad, triple[1], NT) + dot(value_grad, triple[2], NT)
    )
    first_gain_part = jnp.sum(first_grad * first_plain, axis=0)
    first_shift_part = jnp.sum(first_grad, axis=0)
    input_grad = to_owner(
        (middle_grad + normalize_back(first_grad, first_plain, first_inverse, gain_one)).astype(bf16)
    )

    def scatter(stacked):
        count = tensor_count * group_count
        part = lax.psum_scatter(
            stacked.astype(bf16).reshape(count, *stacked.shape[2:]), both, scatter_dimension=0
        )
        return lax.psum(part, "cross").astype(f32)

    depth, across = width // group_count, width // tensor_count
    unit = expand_bias.shape[0]
    triple_sum = scatter(
        triple_part.reshape(3, group_count, depth, tensor_count, across).transpose(3, 1, 0, 2, 4)
    )
    mixing_sum = scatter(
        mixing_part.reshape(tensor_count, across, group_count, depth).transpose(0, 2, 1, 3)
    )
    expand_sum = scatter(
        expand_part.reshape(group_count, depth, tensor_count, unit).transpose(2, 0, 1, 3)
    )
    contract_sum = scatter(
        contract_part.reshape(tensor_count, unit, group_count, depth).transpose(0, 2, 1, 3)
    )
    small_sums = lax.psum(
        (
            first_gain_part,
            first_shift_part,
            query_bias_part,
            value_bias_part,
            output_bias_part,
            second_gain_part,
            second_shift_part,
            expand_bias_part,
            contract_bias_part,
        ),
        ("tensor", "group", "cross"),
    )

    def own_group(full_vector):
        size = full_vector.shape[0] // group_count
        return lax.dynamic_slice_in_dim(full_vector, group_index * size, size)

    def own_split(full_vector):
        size = full_vector.shape[0] // (group_count * tensor_count)
        return lax.dynamic_slice_in_dim(
            full_vector, (tensor_index * group_count + group_index) * size, size
        )

    return (
        output,
        input_grad,
        own_group(small_sums[0]),
        own_group(small_sums[1]),
        triple_sum,
        own_split(small_sums[2]),
        own_split(small_sums[3]),
        mixing_sum,
        own_group(small_sums[4]),
        own_group(small_sums[5]),
        own_group(small_sums[6]),
        expand_sum,
        own_split(small_sums[7]),
        contract_sum,
        own_group(small_sums[8]),
    )


def solution(mesh):
    in_specs = (
        P(("group", "cross"), "tensor", None),
        P(("group", "cross")),
        P(),
        P(),
        P(None, "group", "tensor"),
        P("tensor"),
        P("tensor"),
        P("tensor", "group"),
        P(),
        P(),
        P(),
        P("group", "tensor"),
        P("tensor"),
        P("tensor", "group"),
        P(),
        P(("group", "cross"), "tensor", None),
    )
    out_specs = (
        P(("group", "cross"), "tensor", None),
        P(("group", "cross"), "tensor", None),
        P("group"),
        P("group"),
        P(None, "group", "tensor"),
        P(("tensor", "group")),
        P(("tensor", "group")),
        P("tensor", "group"),
        P("group"),
        P("group"),
        P("group"),
        P("group", "tensor"),
        P(("tensor", "group")),
        P("tensor", "group"),
        P("group"),
    )
    return jax.shard_map(local, mesh=mesh, in_specs=in_specs, out_specs=out_specs, check_vma=False)
```

time: 1780 us -> 912 us (0.51)
  waiting for transfers between devices: 919 us -> 306 us
  matrix products: 495 us -> 131 us
  Pallas kernels: 0 us -> 99.4 us
  blocking collectives: 52.7 us -> 140 us
  other arithmetic: 89.5 us -> 26.9 us
  local copies, waits for them, and re-layouts: 199 us -> 152 us
  starting transfers between devices: 0.65 us -> 28 us
    unnamed x20 -> x9, waiting for transfers between devices: 419 us -> 2.66 us
    all_gather x7 -> x4, waiting for transfers between devices: 440 us -> 66.2 us  [gather(): lax.all_gather(shard, both, axis=0)]
    dot_general x40 -> x18, matrix products: 495 us -> 131 us  [dot(): return lax.dot_general(a, b, dims, preferred_element_type=f32)]
    reduce_scatter x4, waiting for transfers between devices: 11.1 us -> 216 us  [scatter(): lax.psum_scatter(stacked.astype(bf16).reshape(count, *stacked.shape[2:]),...]
    pallas_call x0 -> x2, Pallas kernels: none -> 99.4 us  [the longest x1 57.8 us: attend_backward(): pl.pallas_call(attend_backward_kernel, grid=(width // LANES, 1), in_specs...]
    all_gather x1, blocking collectives: 10.8 us -> 87.4 us  [local(): lax.all_gather(jnp.concatenate([query_bias, value_bias, expand_bias]), 't...]
    unnamed x117 -> x106, local copies, waits for them, and re-layouts: 103 us -> 27.4 us
    convert_element_type x0 -> x7, local copies, waits for them, and re-layouts: none -> 59.8 us  [scatter(): stacked.astype(bf16).reshape(count, *stacked.shape[2:])]
  transfers between devices with their start and end apart: 16 -> 21, of which waited for: 13 -> 5; matrix products, arithmetic and copies ran while one was open for 32% -> 26% of each run, Pallas kernels for 0% -> 5%
where the time goes in v1:
time: 912 us; the launch traced here: 900 us
  waiting for transfers between devices  306 us (34%)
  local copies, waits for them, and re-layouts  152 us (17%)
  blocking collectives  140 us (15%)
  matrix products  131 us (14%)
  Pallas kernels  99.4 us (11%)
  starting transfers between devices  28 us (3%)
  other arithmetic  26.9 us (3%)
  between operations  15.8 us (2%)
    reduce_scatter x4, waiting for transfers between devices, scatter(): lax.psum_scatter(stacked.astype(bf16).reshape(count, *stacked.shape[2:]),...  216 us
    dot_general x18, matrix products, dot(): return lax.dot_general(a, b, dims, preferred_element_type=f32)  131 us
    all_gather x1, blocking collectives, local(): lax.all_gather(jnp.concatenate([query_bias, value_bias, expand_bias]), 't...  87.4 us
    all_gather x4, waiting for transfers between devices, gather(): lax.all_gather(shard, both, axis=0)  66.2 us
    convert_element_type x7, local copies, waits for them, and re-layouts, scatter(): stacked.astype(bf16).reshape(count, *stacked.shape[2:])  59.8 us
    pallas_call x1, Pallas kernels, attend_backward(): pl.pallas_call(attend_backward_kernel, grid=(width // LANES, 1), in_specs...  57.8 us
    psum x1, blocking collectives, local(): lax.psum((first_gain_part, first_shift_part, query_bias_part, value_bias_...  52.9 us
    pallas_call x1, Pallas kernels, attend_forward(): pl.pallas_call(attend_forward_kernel, grid=(width // LANES, 1), in_specs=...  41.6 us
  transfers between devices with their start and end apart: 21, of which 5 were waited for; matrix products, arithmetic and copies ran while one was open for 26% of the time, Pallas kernels for 5%

profile of v1, /device:TPU:0, one launch (start us, length us, event | category | flops | bytes accessed | tf_op | source)
XLA Modules:
  0.0 900.2 jit_solution(9486529086899983983)
XLA Ops:
  10.1 1.5 dynamic-slice_bitcast_fusion.3
  12.3 5.3 collective-permute-start.1
  18.5 1.3 dynamic-slice_bitcast_fusion
  19.8 7.8 collective-permute-start.6
  27.7 87.4 %all-gather.5 = bf16[4,1,1536]{2,1,0:T(2,128)(2,1)S(1)} all-gather(bf16[1,1,1536]{2,1,0:T(2,128)(2,1)S(1)} %reshape.184), channel_id=3, replica_groups=mesh['tensor'=4,'group'=4,'cross'=2] {'tensor'}, dimensions={0}, use_global_device_ids=true | all-gather | bytes 15360 | tf_op jit(solution)/shard_map/all_gather | solution.py:225
  116.7 7.7 copy.64
  124.4 3.2 fusion.33
  128.9 3.1 convolution_convert_fusion.7.ka
  132.0 3.1 add_convert_fusion.4.va
  136.6 2.1 constant_dynamic-update-slice_fusion.1
  138.7 21.3 %collective-permute-done.7 = bf16[392,1024]{1,0:T(8,128)(2,1)S(1)} collective-permute-done((bf16[392,1024]{1,0:T(8,128)(2,1)S(1)}, bf16[392,1024]{1,0:T(8,128)(2,1)S(1)}, u32[]{:S(2)}, u32[]{:S(2)}) %collective-permute-start.7) | collective-permute-done | bytes 802848 | tf_op jit(solution)/shard_map/ppermute | solution.py:202
  160.9 3.5 copy.44
  165.5 3.1 multiply_convert_fusion.1.q_ref
  168.6 41.6 %attend_forward.1 = (bf16[784,1024]{1,0:T(8,128)(2,1)}, f32[784,1024]{1,0:T(8,128)}) custom-call(bf16[784,1024]{1,0:T(8,128)(2,1)} %multiply_convert_fusion.1.q_ref, bf16[784,1024]{1,0:T(8,128)(2,1)} %convolution_convert_fusion.7.ka, bf16[784,1024]{1,0:T(8,128)(2,1)} %collective-permute-done.2.kb, bf16[784,1024]{1,0:T(8,128)(2,1)} %add_convert_fusion.4.va, ...), custom_call_target="tpu_custom_call" | custom-call | flops 5035261952 | bytes 12845056 | tf_op jit(solution)/shard_map/attend_forward/pallas_call | solution.py:108
  210.2 3.4 fusion.36
  214.1 15.8 %all-gather.15.cloned.1.call-done = bf16[4096,1024]{1,0:T(8,128)(2,1)} async-done(((bf16[256,1024]{1,0:T(8,128)(2,1)}), bf16[4096,1024]{1,0:T(8,128)(2,1)}) %all-gather.15.cloned.1.call-update) | async-done | bytes 8388624 | tf_op jit(solution)/shard_map/all_gather | solution.py:216
  229.9 12.5 %copy.45 = bf16[4,4,256,1024]{3,0,2,1:T(4,128)(2,1)} copy(bf16[4,4,256,1024]{3,2,1,0:T(8,128)(2,1)} %bitcast.103) | data formatting | bytes 16777216 | tf_op jit(solution)/shard_map/reshape | solution.py:216
  242.5 12.3 %copy.58 = bf16[128,8,4,1024]{3,1,2,0:T(8,128)(2,1)} copy(bf16[128,8,4,1024]{3,2,1,0:T(4,128)(2,1)} %bitcast.97) | data formatting | bytes 16777216
  254.7 50.4 %all-gather.17.cloned.1.call-done = bf16[16384,256]{1,0:T(8,128)(2,1)} async-done(((bf16[1024,256]{1,0:T(8,128)(2,1)}), bf16[16384,256]{1,0:T(8,128)(2,1)}) %all-gather.17.cloned.1.call-update) | async-done | bytes 8388624 | tf_op jit(solution)/shard_map/all_gather | solution.py:216
  305.1 12.2 %copy.46 = bf16[4,4,1024,256]{3,1,2,0:T(4,128)(2,1)} copy(bf16[4,4,1024,256]{3,2,1,0:T(8,128)(2,1)} %bitcast.104) | data formatting | bytes 16777216 | tf_op jit(solution)/shard_map/reshape | solution.py:216
  317.3 9.4 %copy.60 = bf16[512,8,4,256]{3,1,2,0:T(8,128)(2,1)} copy(bf16[512,8,4,256]{3,2,1,0:T(4,128)(2,1)} %bitcast.98) | data formatting | bytes 16777216
  326.7 14.4 %multiply_convert_fusion = (bf16[784,4096]{1,0:T(8,128)(2,1)}, f32[784,4096]{1,0:T(8,128)}) fusion(f32[4096]{0:T(1024)S(1)} %bitcast.133, bf16[1024,4096]{1,0:T(8,128)(2,1)} %bitcast.107, f32[784,1024]{1,0:T(8,128)S(1)} %get-tuple-element.71, f32[1024]{0:T(1024)S(1)} %convert_element_type.181, f32[1024]{0:T(1024)S(1)} %convert_element_type.180, ...), kind=kOutput, calls=%fused_computation.8 | convolution fusion | flops 6599950336 | bytes 30898304 | tf_op jit(solution)/shard_map/dot_general | solution.py:28
  341.1 15.8 %convert_reduce_fusion = (f32[4096]{0:T(1024)}, bf16[784,4096]{1,0:T(8,128)(2,1)}) fusion(f32[784,4096]{1,0:T(8,128)} %get-tuple-element.73, f32[4096]{0:T(1024)S(1)} %bitcast.134, bf16[784,1024]{1,0:T(8,128)(2,1)} %constant_dynamic-update-slice_fusion, bf16[4096,1024]{1,0:T(8,128)(2,1)S(1)} %bitcast.106), kind=kOutput, calls=%fused_computation.7 | convolution fusion | flops 6618411008 | bytes 29294592 | tf_op jit(solution)/shard_map/dot_general | solution.py:28
  356.9 10.2 %multiply_reduce_fusion = (f32[1024]{0:T(1024)S(1)}, f32[784]{0:T(1024)S(1)}, f32[784]{0:T(1024)S(1)}, f32[1024]{0:T(1024)S(1)}, f32[784,1024]{1,0:T(8,128)S(1)}) fusion(f32[784,1024]{1,0:T(8,128)S(1)} %get-tuple-element.71, f32[784]{0:T(1024)S(1)} %add_rsqrt_fusion, f32[784]{0:T(1024)S(1)} %broadcast_multiply_fusion.5, ...), kind=kOutput, calls=%fused_computation.35 | convolution fusion | flops 6583889920 | bytes 21258496 | tf_op jit(solution)/shard_map/dot_general | solution.py:28
  367.2 2.8 convert_reduce_fusion.3
  370.0 3.1 convolution_convert_fusion.6.g_ref
  373.1 57.8 %attend_backward.1 = (bf16[784,1024]{1,0:T(8,128)(2,1)}, bf16[784,1024]{1,0:T(8,128)(2,1)}, bf16[784,1024]{1,0:T(8,128)(2,1)}, bf16[784,1024]{1,0:T(8,128)(2,1)}, bf16[784,1024]{1,0:T(8,128)(2,1)}) custom-call(bf16[784,1024]{1,0:T(8,128)(2,1)} %multiply_convert_fusion.1.q_ref, bf16[784,1024]{1,0:T(8,128)(2,1)} %convolution_convert_fusion.6.g_ref, ...), custom_call_target="tpu_custom_call" | custom-call | flops 12588154880 | bytes 22478848 | tf_op jit(solution)/shard_map/attend_backward/pallas_call | solution.py:126
  431.2 6.1 convolution_convert_fusion.2
  437.3 4.5 convert_element_type.205
  441.9 3.3 copy.48
  445.6 5.9 convolution_convert_fusion.5
  451.5 5.0 stack.36
  456.5 6.5 convolution_convert_fusion.4
  463.0 4.5 stack.37
  467.5 6.4 convolution_convert_fusion.3
  473.8 4.5 stack.38
  478.4 7.4 maximum_bitcast_fusion
  485.7 3.8 copy.47
  489.6 14.6 %convolution_convert_fusion = bf16[1024,4096]{1,0:T(8,128)(2,1)} fusion(bf16[784,4096]{1,0:T(8,128)(2,1)} %get-tuple-element.77, f32[784,1024]{1,0:T(8,128)S(1)} %get-tuple-element.71, f32[1024]{0:T(1024)S(1)} %convert_element_type.181, f32[1024]{0:T(1024)S(1)} %convert_element_type.180, f32[784]{0:T(1024)S(1)} %add_rsqrt_fusion, ...), kind=kOutput, calls=%fused_computation.10 | convolution fusion | flops 6584877056 | bytes 18036864 | tf_op jit(solution)/shard_map/dot_general | solution.py:28
  504.2 14.8 %convert_element_type.210 = bf16[4,256,4,1024]{3,2,1,0:T(4,128)(2,1)} reshape(bf16[1024,4096]{1,0:T(8,128)(2,1)} %convolution_convert_fusion) | data formatting | bytes 16777216 | tf_op jit(solution)/shard_map/convert_element_type | solution.py:283
  519.0 10.3 %copy.49 = bf16[4,4,256,1024]{3,2,1,0:T(8,128)(2,1)} copy(bf16[4,4,256,1024]{3,0,2,1:T(4,128)(2,1)} %bitcast.99) | data formatting | bytes 16777216 | tf_op jit(solution)/shard_map/convert_element_type | solution.py:283
  529.4 14.6 %convolution_convert_fusion.1 = bf16[4096,1024]{1,0:T(8,128)(2,1)} fusion(bf16[784,4096]{1,0:T(8,128)(2,1)} %get-tuple-element.72, bf16[784,1024]{1,0:T(8,128)(2,1)} %constant_dynamic-update-slice_fusion), kind=kOutput, calls=%fused_computation.11 | convolution fusion | flops 6580862976 | bytes 16416768 | tf_op jit(solution)/shard_map/dot_general | solution.py:28
  544.0 14.5 %convert_element_type.215 = bf16[4,1024,4,256]{3,2,1,0:T(4,128)(2,1)} reshape(bf16[4096,1024]{1,0:T(8,128)(2,1)} %convolution_convert_fusion.1) | data formatting | bytes 16777216 | tf_op jit(solution)/shard_map/convert_element_type | solution.py:283
  558.5 8.5 copy.50
  567.7 11.3 %add_convert_fusion.2 = bf16[784,1024]{1,0:T(8,128)(2,1)S(1)} fusion(f32[784,1024]{1,0:T(8,128)S(1)} %get-tuple-element.71, f32[1024]{0:T(1024)S(1)} %convert_element_type.186, bf16[784,4096]{1,0:T(8,128)(2,1)} %get-tuple-element.72, bf16[4096,1024]{1,0:T(8,128)(2,1)} %bitcast.105), kind=kOutput, calls=%fused_computation.43 | convolution fusion | flops 6579077120 | bytes 19632128 | tf_op jit(solution)/shard_map/dot_general | solution.py:28
  579.0 1.3 fusion.35
  580.2 7.8 collective-permute-start.4
  588.3 1.9 fusion.37
  590.3 3.5 fusion.22
  593.8 4.5 fusion.19
  598.3 1.8 fusion.18
  600.2 107.6 %reduce-scatter.9.cloned.1.call-done = bf16[1,256,1024]{2,1,0:T(8,128)(2,1)} async-done(((bf16[16,256,1024]{2,1,0:T(8,128)(2,1)}), bf16[1,256,1024]{2,1,0:T(8,128)(2,1)}) %reduce-scatter.9.cloned.1.call-update) | async-done | bytes 524304 | tf_op jit(solution)/shard_map/reduce_scatter | solution.py:282
  707.8 108.5 %reduce-scatter.11.cloned.1.call-done = bf16[1,1024,256]{2,1,0:T(8,128)(2,1)} async-done(((bf16[16,1024,256]{2,1,0:T(8,128)(2,1)}), bf16[1,1024,256]{2,1,0:T(8,128)(2,1)}) %reduce-scatter.11.cloned.1.call-update) | async-done | bytes 524304 | tf_op jit(solution)/shard_map/reduce_scatter | solution.py:282
  816.4 1.3 fusion.34
  817.6 1.8 collective-permute-start.10
  819.4 1.9 collective-permute-start.11
  821.6 1.5 select_bitcast_fusion.3
  823.1 1.3 pad_maximum_fusion.1
  824.4 2.1 convert_reduce_fusion.4
  826.5 52.9 %all-reduce = (f32[1024]{0:T(1024)S(1)}, f32[1024]{0:T(1024)S(1)}, f32[1024]{0:T(1024)S(1)}, f32[1024]{0:T(1024)S(1)}, f32[1024]{0:T(1024)S(1)}, /*index=5*/f32[...) all-reduce(f32[1024]{0:T(1024)S(1)} %get-tuple-element.31, ...), channel_id=1, replica_groups=mesh['tensor'=4,'group'=4,'cross'=2] {'tensor','group','cross'}, use_global_device_ids=true, to_apply=%region_9.10 | all-reduce | flops 12288 | bytes 98304 | tf_op jit(solution)/shard_map/psum | solution.py:301
  885.2 1.3 pad_maximum_fusion.2
  886.5 1.7 convert_element_type.207
  888.1 1.9 convert_element_type.201
  890.1 2.1 convert_element_type.212
  (179 shorter events, 19.4 us)
Async XLA Ops:
  7.2 11.1 %copy-start.20 = (bf16[2,392,1024]{2,1,0:T(8,128)(2,1)S(1)}, bf16[2,392,1024]{2,1,0:T(8,128)(2,1)}, u32[]{:S(2)}) copy-start(bf16[2,392,1024]{2,1,0:T(8,128)(2,1)} %param.31) | copy-start | bytes 4816900
  7.2 109.5 %all-gather.11.cloned.1.call-start = ((), (), s32[]{:S(2)}) async-start(), calls=%async_computation.8 | async-start | bytes 6684672 | tf_op jit(solution)/shard_map/all_gather | solution.py:216
  7.9 153.0 %all-gather.13.cloned.1.call-start = ((), (), s32[]{:S(2)}) async-start(), calls=%async_computation.9 | async-start | bytes 2228224 | tf_op jit(solution)/shard_map/all_gather | solution.py:216
  8.7 221.3 %all-gather.15.cloned.1.call-start = ((), (), s32[]{:S(2)}) async-start(), calls=%async_computation.10 | async-start | bytes 8912896 | tf_op jit(solution)/shard_map/all_gather | solution.py:216
  9.4 295.7 %all-gather.17.cloned.1.call-start = ((), (), s32[]{:S(2)}) async-start(), calls=%async_computation.11 | async-start | bytes 8912896 | tf_op jit(solution)/shard_map/all_gather | solution.py:216
  10.0 590.1 %reduce-scatter.7.cloned.1.call-start = ((), (), s32[]{:S(2)}) async-start(), calls=%async_computation.5 | async-start | bytes 2228224 | tf_op jit(solution)/shard_map/reduce_scatter | solution.py:282
  11.6 103.6 %collective-permute-start = (bf16[392,1024]{1,0:T(8,128)(2,1)S(1)}, bf16[392,1024]{1,0:T(8,128)(2,1)S(1)}, u32[]{:S(2)}, u32[]{:S(2)}) collective-permute-start(bf16[392,1024]{1,0:T(8,128)(2,1)S(1)} %get-tuple-element.66), channel_id=1, source_target_pairs={{0,0},{2,8},{4,4},{6,12},{8,16},{10,24},{12,20},{14,28},{16,2},{18... | collective-permute-start | bytes 2408456 | tf_op jit(solution)/shard_map/ppermute | solution.py:202
  12.3 102.9 %collective-permute-start.1 = (bf16[392,1024]{1,0:T(8,128)(2,1)S(1)}, bf16[392,1024]{1,0:T(8,128)(2,1)S(1)}, u32[]{:S(2)}, u32[]{:S(2)}) collective-permute-start(bf16[392,1024]{1,0:T(8,128)(2,1)S(1)} %get-tuple-element.67), channel_id=1, source_target_pairs={{0,16},{2,24},{4,20},{6,28},{8,0},{10,8},{12,4},{14,12},{16,18},{1... | collective-permute-start | bytes 2408456 | tf_op jit(solution)/shard_map/ppermute | solution.py:202
  18.3 9.4 %copy-start.35 = (bf16[1024]{0:T(1024)(128)(2,1)S(1)}, bf16[1024]{0:T(1024)(128)(2,1)}, u32[]{:S(2)}) copy-start(bf16[1024]{0:T(1024)(128)(2,1)} %param.18) | copy-start | bytes 6148
  18.3 9.4 %copy-start.36 = (bf16[1024]{0:T(1024)(128)(2,1)S(1)}, bf16[1024]{0:T(1024)(128)(2,1)}, u32[]{:S(2)}) copy-start(bf16[1024]{0:T(1024)(128)(2,1)} %param.19) | copy-start | bytes 6148
  18.3 9.4 %copy-start.37 = (bf16[1024]{0:T(1024)(128)(2,1)S(1)}, bf16[1024]{0:T(1024)(128)(2,1)}, u32[]{:S(2)}) copy-start(bf16[1024]{0:T(1024)(128)(2,1)} %param.28) | copy-start | bytes 6148
  18.3 9.4 %copy-start.42 = (bf16[256]{0:T(256)(128)(2,1)S(1)}, bf16[256]{0:T(256)(128)(2,1)}, u32[]{:S(2)}) copy-start(bf16[256]{0:T(256)(128)(2,1)} %param.22) | copy-start | bytes 1540
  18.3 9.4 %copy-start.43 = (bf16[256]{0:T(256)(128)(2,1)S(1)}, bf16[256]{0:T(256)(128)(2,1)}, u32[]{:S(2)}) copy-start(bf16[256]{0:T(256)(128)(2,1)} %param.21) | copy-start | bytes 1540
  19.8 116.8 %collective-permute-start.6 = (bf16[392,1024]{1,0:T(8,128)(2,1)}, bf16[392,1024]{1,0:T(8,128)(2,1)}, u32[]{:S(2)}, u32[]{:S(2)}) collective-permute-start(bf16[392,1024]{1,0:T(8,128)(2,1)} %get-tuple-element.61), channel_id=1, source_target_pairs={{0,0},{2,8},{4,4},{6,12},{8,16},{10,24},{12,20},{14,28},{16,2},{18... | collective-permute-start | bytes 2408456 | tf_op jit(solution)/shard_map/ppermute | solution.py:202
  27.6 137.8 %copy-start.28 = (f32[1024]{0:T(1024)}, f32[1024]{0:T(1024)S(1)}, u32[]{:S(2)}) copy-start(f32[1024]{0:T(1024)S(1)} %convert_element_type.169) | copy-start | bytes 12292
  27.7 137.8 %copy-start.33 = (f32[1024]{0:T(1024)}, f32[1024]{0:T(1024)S(1)}, u32[]{:S(2)}) copy-start(f32[1024]{0:T(1024)S(1)} %convert_element_type.170) | copy-start | bytes 12292
  115.2 1.5 copy-start.8
  116.0 49.4 %copy-start.26 = (f32[784]{0:T(1024)}, f32[784]{0:T(1024)S(1)}, u32[]{:S(2)}) copy-start(f32[784]{0:T(1024)S(1)} %broadcast_multiply_fusion.6) | copy-start | bytes 9412
  116.7 48.8 %copy-start.30 = (f32[784]{0:T(1024)}, f32[784]{0:T(1024)S(1)}, u32[]{:S(2)}) copy-start(f32[784]{0:T(1024)S(1)} %add_rsqrt_fusion.1) | copy-start | bytes 9412
  128.0 4.0 copy-start.12
  128.5 3.4 copy-start.14
  132.0 36.6 %collective-permute-start.2 = (bf16[784,1024]{1,0:T(8,128)(2,1)}, bf16[784,1024]{1,0:T(8,128)(2,1)}, u32[]{:S(2)}, u32[]{:S(2)}) collective-permute-start(bf16[784,1024]{1,0:T(8,128)(2,1)} %convolution_convert_fusion.7.ka), channel_id=1, source_target_pairs={{0,2},{2,0},{4,6},{6,4},{1,3},{3,1},{5,7},{7,5},{8,10},{10,8},{12,... | collective-permute-start | bytes 4816904 | tf_op jit(solution)/shard_map/ppermute | solution.py:237
  132.0 3.6 copy-start.24
  132.0 4.5 copy-start.38
  132.0 4.5 copy-start.39
  132.0 4.5 copy-start.40
  135.1 33.5 %collective-permute-start.3 = (bf16[784,1024]{1,0:T(8,128)(2,1)}, bf16[784,1024]{1,0:T(8,128)(2,1)}, u32[]{:S(2)}, u32[]{:S(2)}) collective-permute-start(bf16[784,1024]{1,0:T(8,128)(2,1)} %add_convert_fusion.4.va), channel_id=1, source_target_pairs={{0,2},{2,0},{4,6},{6,4},{1,3},{3,1},{5,7},{7,5},{8,10},{10,8},{12,... | collective-permute-start | bytes 4816904 | tf_op jit(solution)/shard_map/ppermute | solution.py:238
  135.6 24.4 %collective-permute-start.7 = (bf16[392,1024]{1,0:T(8,128)(2,1)S(1)}, bf16[392,1024]{1,0:T(8,128)(2,1)S(1)}, u32[]{:S(2)}, u32[]{:S(2)}) collective-permute-start(bf16[392,1024]{1,0:T(8,128)(2,1)S(1)} %copy-done.24), channel_id=1, source_target_pairs={{0,16},{2,24},{4,20},{6,28},{8,0},{10,8},{12,4},{14,12},{16,18},{1... | collective-permute-start | bytes 2408456 | tf_op jit(solution)/shard_map/ppermute | solution.py:202
  160.9 4.0 copy-start.3
  164.9 45.3 %copy-start.18 = (bf16[128,8,4,256]{3,1,2,0:T(8,128)(2,1)}, bf16[128,8,4,256]{3,1,2,0:T(8,128)(2,1)S(1)}, u32[]{:S(2)}) copy-start(bf16[128,8,4,256]{3,1,2,0:T(8,128)(2,1)S(1)} %copy.57) | copy-start | bytes 6291460
  165.4 3.1 copy-start.16
  168.6 41.6 %copy-start.6 = (bf16[392,1024]{1,0:T(8,128)(2,1)S(1)}, bf16[392,1024]{1,0:T(8,128)(2,1)}, u32[]{:S(2)}) copy-start(bf16[392,1024]{1,0:T(8,128)(2,1)} %copy-done.4) | copy-start | bytes 2408452
  168.6 41.6 %copy-start.10 = (bf16[392,1024]{1,0:T(8,128)(2,1)S(1)}, bf16[392,1024]{1,0:T(8,128)(2,1)}, u32[]{:S(2)}) copy-start(bf16[392,1024]{1,0:T(8,128)(2,1)} %copy-done.8) | copy-start | bytes 2408452
  326.6 14.4 %copy-start.2 = (bf16[512,8,4,256]{3,1,2,0:T(8,128)(2,1)S(1)}, bf16[512,8,4,256]{3,1,2,0:T(8,128)(2,1)}, u32[]{:S(2)}) copy-start(bf16[512,8,4,256]{3,1,2,0:T(8,128)(2,1)} %copy.60) | copy-start | bytes 25165828
  326.7 30.3 %slice-start = ((s8[8388608]{0:T(1024)(128)(4,1)}), s8[4194304]{0:T(1024)(128)(4,1)S(1)}, s32[]{:S(2)}) async-start(s8[8388608]{0:T(1024)(128)(4,1)} %bitcast.108), calls=%async_computation.13 | async-start | bytes 8388608
  341.1 15.8 %slice-start.1 = ((s8[8388608]{0:T(1024)(128)(4,1)}), s8[4194304]{0:T(1024)(128)(4,1)S(1)}, s32[]{:S(2)}) async-start(s8[8388608]{0:T(1024)(128)(4,1)} %bitcast.108), calls=%async_computation.14 | async-start | bytes 8388608
  367.2 2.8 copy-start.19
  370.0 3.1 copy-start
  430.9 25.6 %collective-permute-start.8 = (bf16[784,1024]{1,0:T(8,128)(2,1)}, bf16[784,1024]{1,0:T(8,128)(2,1)}, u32[]{:S(2)}, u32[]{:S(2)}) collective-permute-start(bf16[784,1024]{1,0:T(8,128)(2,1)} %get-tuple-element.26), channel_id=1, source_target_pairs={{0,2},{2,0},{4,6},{6,4},{1,3},{3,1},{5,7},{7,5},{8,10},{10,8},{12,... | collective-permute-start | bytes 4816904 | tf_op jit(solution)/shard_map/ppermute | solution.py:266
  441.9 3.7 copy-start.27
  441.9 3.7 copy-start.29
  441.9 3.7 copy-start.31
  441.9 3.7 copy-start.34
  445.2 154.9 %reduce-scatter.5.cloned.1.call-start = ((), (), s32[]{:S(2)}) async-start(), calls=%async_computation.4 | async-start | bytes 6684672 | tf_op jit(solution)/shard_map/reduce_scatter | solution.py:282
  445.3 22.2 %collective-permute-start.9 = (bf16[784,1024]{1,0:T(8,128)(2,1)}, bf16[784,1024]{1,0:T(8,128)(2,1)}, u32[]{:S(2)}, u32[]{:S(2)}) collective-permute-start(bf16[784,1024]{1,0:T(8,128)(2,1)} %get-tuple-element.28), channel_id=1, source_target_pairs={{0,2},{2,0},{4,6},{6,4},{1,3},{3,1},{5,7},{7,5},{8,10},{10,8},{12,... | collective-permute-start | bytes 4816904 | tf_op jit(solution)/shard_map/ppermute | solution.py:267
  489.6 218.2 %reduce-scatter.9.cloned.1.call-start = ((), (), s32[]{:S(2)}) async-start(), calls=%async_computation.6 | async-start | bytes 8912896 | tf_op jit(solution)/shard_map/reduce_scatter | solution.py:282
  529.3 287.0 %reduce-scatter.11.cloned.1.call-start = ((), (), s32[]{:S(2)}) async-start(), calls=%async_computation.7 | async-start | bytes 8912896 | tf_op jit(solution)/shard_map/reduce_scatter | solution.py:282
  567.0 319.4 %all-reduce.4.cloned.1.call-start = ((), (), s32[]{:S(2)}) async-start(), calls=%async_computation.12 | async-start | bytes 3145728 | tf_op jit(solution)/shard_map/psum | solution.py:285
  567.7 20.6 %copy-start.22 = (bf16[784,1024]{1,0:T(8,128)(2,1)S(1)}, bf16[784,1024]{1,0:T(8,128)(2,1)}, u32[]{:S(2)}) copy-start(bf16[784,1024]{1,0:T(8,128)(2,1)} %get-tuple-element.24) | copy-start | bytes 4816900
  579.0 9.4 %copy-start.17 = (bf16[128,8,4,256]{3,1,2,0:T(8,128)(2,1)S(1)}, bf16[128,8,4,256]{3,1,2,0:T(8,128)(2,1)}, u32[]{:S(2)}) copy-start(bf16[128,8,4,256]{3,1,2,0:T(8,128)(2,1)} %copy-done.16) | copy-start | bytes 6291460
  580.2 241.3 %collective-permute-start.4 = (bf16[392,1024]{1,0:T(8,128)(2,1)}, bf16[392,1024]{1,0:T(8,128)(2,1)}, u32[]{:S(2)}, u32[]{:S(2)}) collective-permute-start(bf16[392,1024]{1,0:T(8,128)(2,1)} %get-tuple-element.64), channel_id=1, source_target_pairs={{0,0},{8,2},{4,4},{12,6},{16,8},{24,10},{20,12},{28,14},{2,16},{10... | collective-permute-start | bytes 2408456 | tf_op jit(solution)/shard_map/ppermute | solution.py:208
  588.1 2.1 copy-start.15
  588.1 2.1 copy-start.44
  588.1 233.5 %collective-permute-start.5 = (bf16[392,1024]{1,0:T(8,128)(2,1)}, bf16[392,1024]{1,0:T(8,128)(2,1)}, u32[]{:S(2)}, u32[]{:S(2)}) collective-permute-start(bf16[392,1024]{1,0:T(8,128)(2,1)} %get-tuple-element.65), channel_id=1, source_target_pairs={{16,0},{24,2},{20,4},{28,6},{0,8},{8,10},{4,12},{12,14},{18,16},{2... | collective-permute-start | bytes 2408456 | tf_op jit(solution)/shard_map/ppermute | solution.py:208
  590.2 3.5 copy-start.7
  590.2 3.5 copy-start.11
  590.3 3.5 copy-start.13
  590.3 3.5 copy-start.21
  593.8 4.5 copy-start.1
  816.3 5.0 copy-start.23
  817.6 67.4 %collective-permute-start.10 = (bf16[392,1024]{1,0:T(8,128)(2,1)}, bf16[392,1024]{1,0:T(8,128)(2,1)S(1)}, u32[]{:S(2)}, u32[]{:S(2)}) collective-permute-start(bf16[392,1024]{1,0:T(8,128)(2,1)} %get-tuple-element.58), channel_id=1, source_target_pairs={{0,0},{8,2},{4,4},{12,6},{16,8},{24,10},{20,12},{28,14},{2,16},{10... | collective-permute-start | bytes 2408456 | tf_op jit(solution)/shard_map/ppermute | solution.py:208
  819.4 65.6 %collective-permute-start.11 = (bf16[392,1024]{1,0:T(8,128)(2,1)}, bf16[392,1024]{1,0:T(8,128)(2,1)S(1)}, u32[]{:S(2)}, u32[]{:S(2)}) collective-permute-start(bf16[392,1024]{1,0:T(8,128)(2,1)} %get-tuple-element.59), channel_id=1, source_target_pairs={{16,0},{24,2},{20,4},{28,6},{0,8},{8,10},{4,12},{12,14},{18,16},{2... | collective-permute-start | bytes 2408456 | tf_op jit(solution)/shard_map/ppermute | solution.py:208
  823.1 3.4 copy-start.32
  886.5 5.8 copy-start.25
  (4 other events, 4.1 us)
Sparse Core Ops, SparseCore 0:
  10.3 96.9 all-gather.10
  109.5 43.5 all-gather.12
  155.3 74.5 all-gather.14
  231.9 73.1 all-gather.16
  445.3 59.8 reduce-scatter.6
  509.5 89.0 reduce-scatter.4
  602.7 105.0 reduce-scatter.8
  711.9 104.4 reduce-scatter.10
  818.8 52.5 all-reduce.3

commit v2 on v1

v2 whole, which is shorter than its diff:
```python
import functools

import jax
import jax.numpy as jnp
from jax import lax
from jax.experimental import pallas as pl
from jax.experimental.pallas import tpu as pltpu
from jax.sharding import PartitionSpec as P

HEAD = 64
LANES = 128

epsilon = 1e-06
root_half = 0.7071067811865476
inv_root_two_pi = 0.3989422804014327
log_two = 0.6931471805599453
query_scale = HEAD**-0.5 / log_two

f32 = jnp.float32
bf16 = jnp.bfloat16

NN = (((1,), (0,)), ((), ()))
NT = (((1,), (1,)), ((), ()))
TN = (((0,), (0,)), ((), ()))


def dot(a, b, dims=NN):
    return lax.dot_general(a, b, dims, preferred_element_type=f32)


def low_lanes(array):
    return lax.broadcasted_iota(jnp.int32, array.shape, 1) < HEAD


def forward_load(rows, k, v, keys, values_low, values_high):
    low, one = low_lanes(v), jnp.ones_like(v)
    keys[rows] = k
    values_low[rows] = jnp.where(low, v, one)
    values_high[rows] = jnp.where(low, one, v)


def forward_heads(q, keys, values_low, values_high):
    low, zero = low_lanes(q), jnp.zeros_like(q)
    sums, tops = [], []
    for mine, v in ((jnp.where(low, q, zero), values_low), (jnp.where(low, zero, q), values_high)):
        s = dot(mine, keys[...], NT)
        top = jnp.max(s, axis=1, keepdims=True)
        p = jnp.exp2(s - top).astype(bf16)
        sums.append(dot(p, v[...]))
        tops.append(top)
    total = pltpu.roll(jnp.where(low, sums[1], sums[0]), HEAD, 1)
    out = (jnp.where(low, sums[0], sums[1]) / total).astype(bf16)
    return out, jnp.where(low, tops[0], tops[1]) + jnp.log2(total)


def backward_heads(q, g, o, lse, keys, values, dk, dv):
    low = low_lanes(q)
    product = g.astype(f32) * o.astype(f32)
    q_t, g_t = q.T, g.T
    dqs = []
    for h in range(2):

        def own(a):
            zero = jnp.zeros_like(a)
            return jnp.where(low, a, zero) if h == 0 else jnp.where(low, zero, a)

        inner = jnp.sum(own(product), axis=1, keepdims=True)
        p = jnp.exp2(dot(own(q), keys[...], NT) - lse[:, HEAD * h : HEAD * h + 1])
        ds = (p * (dot(own(g), values[...], NT) - inner)).astype(bf16)
        dqs.append(dot(ds, keys[...]))
        rows = slice(HEAD * h, HEAD * (h + 1))
        dv[rows] = dot(g_t[rows], p.astype(bf16))
        dk[rows] = dot(q_t[rows], ds)
    return (jnp.where(low, dqs[0], dqs[1]) * HEAD**-0.5).astype(bf16)


def key_value_total(dk, dv):
    return (dk[...] * log_two).T, dv[...].T


def attend_forward_kernel(q_ref, ka, kb, va, vb, o_ref, lse_ref, *held):
    n = ka.shape[0]
    forward_load(slice(0, n), ka[...], va[...], *held)
    forward_load(slice(n, 2 * n), kb[...], vb[...], *held)
    o_ref[...], lse_ref[...] = forward_heads(q_ref[...], *held)


def attend_backward_kernel(
    q_ref, g_ref, o_ref, lse_ref, ka, kb, va, vb,
    dq_ref, dka, dkb, dva, dvb,
    keys, values, dk, dv,
):
    n = ka.shape[0]
    for i, (k, v) in enumerate(((ka, va), (kb, vb))):
        keys[i * n : (i + 1) * n] = k[...]
        values[i * n : (i + 1) * n] = v[...]
    dq_ref[...] = backward_heads(
        q_ref[...], g_ref[...], o_ref[...], lse_ref[...], keys, values, dk, dv
    )
    key_total, value_total = key_value_total(dk, dv)
    dka[...] = key_total[:n].astype(bf16)
    dkb[...] = key_total[n:].astype(bf16)
    dva[...] = value_total[:n].astype(bf16)
    dvb[...] = value_total[n:].astype(bf16)


def attend_forward(q, ka, kb, va, vb):
    n, width = q.shape
    spec = pl.BlockSpec((n, LANES), lambda i: (0, i))
    return pl.pallas_call(
        attend_forward_kernel,
        grid=(width // LANES,),
        in_specs=[spec] * 5,
        out_specs=[spec] * 2,
        out_shape=[jax.ShapeDtypeStruct((n, width), bf16), jax.ShapeDtypeStruct((n, width), f32)],
        scratch_shapes=[pltpu.VMEM((2 * n, LANES), bf16)] * 3,
        name="attend_forward",
        cost_estimate=pl.CostEstimate(
            flops=8 * n * n * width, bytes_accessed=16 * n * width, transcendentals=n * n * width // 32
        ),
        compiler_params=pltpu.CompilerParams(vmem_limit_bytes=56 << 20),
    )(q, ka, kb, va, vb)


def attend_backward(q, g, o, lse, ka, kb, va, vb):
    n, width = q.shape
    spec = pl.BlockSpec((n, LANES), lambda i: (0, i))
    return pl.pallas_call(
        attend_backward_kernel,
        grid=(width // LANES,),
        in_specs=[spec] * 8,
        out_specs=[spec] * 5,
        out_shape=[jax.ShapeDtypeStruct((n, width), bf16)] * 5,
        scratch_shapes=[pltpu.VMEM((2 * n, LANES), bf16)] * 2 + [pltpu.VMEM((LANES, 2 * n), f32)] * 2,
        name="attend_backward",
        cost_estimate=pl.CostEstimate(
            flops=20 * n * n * width, bytes_accessed=28 * n * width, transcendentals=n * n * width // 32
        ),
        compiler_params=pltpu.CompilerParams(vmem_limit_bytes=60 << 20),
    )(q, g, o, lse, ka, kb, va, vb)


MESH = pl.DeviceIdType.MESH
AXES = ("tensor", "group", "cross")
TRIPLE, MIXING, UP, DOWN = range(4)
CORE, X, Y, NEAR, FAR = range(5)
OWN, LAST = 5, 6
HALF, PART_A, PART_B = range(3)


def place():
    t, g, x = (lax.axis_index(axis) for axis in AXES)
    return t, g // 2, g % 2, x


def depth_of(which):
    t = lax.axis_index(AXES[0])
    near = t + 1 - 2 * (t % 2)
    return {OWN: t, NEAR: near, FAR: lax.rem(t + 2, 4), LAST: lax.rem(near + 2, 4)}[which]


def peer(kind):
    t, y, c, x = place()
    if kind in (NEAR, FAR):
        t = depth_of(kind)
    elif kind == X:
        x = 1 - x
    elif kind == Y:
        y = 1 - y
    else:
        c = 1 - c
    return (t, y * 2 + c, x)


def greet(devices):
    barrier = pltpu.get_barrier_semaphore()
    for device in devices:
        pl.semaphore_signal(barrier, inc=1, device_id=device, device_id_type=MESH)
    pl.semaphore_wait(barrier, len(devices))


def remote(source, target, send, recv, device):
    return pltpu.make_async_remote_copy(
        source, target, send, recv, device_id=device, device_id_type=MESH
    )


def chip_line():
    t, y, c, x = place()
    devices = [(t, y * 2 + 1 - c, x)]
    for step in range(1, 4):
        for core in range(2):
            devices.append((lax.rem(t + step, 4), y * 2 + core, x))
    return devices


def neighbours():
    return chip_line() + [peer(X), peer(Y)]


def staged(count, stages):
    slots = []
    for now in range(count + max(delay for delay, _ in stages)):
        slots.append(
            [(stage, now - delay) for delay, stage in stages if 0 <= now - delay < count]
        )
    return slots


def run(slot):
    for stage, item in slot:
        stage(item)


class Copies:
    def go(self, m, *steps):
        for step in steps:
            self.copy(m, step).start()

    def got(self, m, *steps):
        for step in steps:
            self.copy(m, step).wait_recv()


class Weight:
    sections = {HALF: (0, 128), PART_A: (0, 48), PART_B: (48, 80)}

    def __init__(self, kind, shard, whole):
        self.kind, self.shard, self.whole = kind, shard, whole
        self.unit = 4 if kind == DOWN else 1

    def rows(self, part, half, base=0):
        off, size = self.sections[part]
        return pl.ds(pl.multiple_of(base + (half * 128 + off) * self.unit, 16), size * self.unit)

    def own(self, part, half):
        r = self.rows(part, half)
        return self.shard.at[:, r, :] if self.kind == TRIPLE else self.shard.at[r, :]

    def at(self, y, c, part, half, depth=None):
        g = y * 2 + c
        if self.kind in (TRIPLE, UP):
            n = self.shard.shape[-1]
            r = self.rows(part, half, g * 256)
            cols = slice(None) if depth is None else pl.ds(pl.multiple_of(depth * n, n), n)
            return self.whole.at[:, r, cols] if self.kind == TRIPLE else self.whole.at[r, cols]
        cols = pl.ds(pl.multiple_of(g * 256, 256), 256)
        return self.whole.at[slice(None) if depth is None else depth, self.rows(part, half), cols]


Z_NEAR, Z_FAR, Z_ON = 0, 1, 2
X_HALF = {NEAR: 3, FAR: 4, LAST: 5}
Y_HALF = {OWN: 6, NEAR: 7, FAR: 8, LAST: 9}
Y_REST = {OWN: 10, NEAR: 11, FAR: 12, LAST: 13}
X_REST = {OWN: 14, NEAR: 15, FAR: 16, LAST: 17}
TO_CORE = (18, 19, 20, 21, 22)
GATHER_STEPS = 23


class Gather(Copies):
    def __init__(self, weights, send, recv, here):
        self.weights, self.send, self.recv, self.here = weights, send, recv, here

    def copy(self, m, step):
        w = self.weights[m]
        t, y, c, x = place()
        if step in (Z_NEAR, Z_FAR):
            target = NEAR if step == Z_NEAR else FAR
            source, into = w.own(HALF, x), w.at(y, c, HALF, x, t)
        elif step == Z_ON:
            target = NEAR
            source = into = w.at(y, c, HALF, x, depth_of(FAR))
        elif step in TO_CORE:
            target = CORE
            at_y, part, half = (
                (y, HALF, x),
                (y, HALF, 1 - x),
                (1 - y, HALF, x),
                (1 - y, PART_A, 1 - x),
                (1 - y, PART_B, 1 - x),
            )[step - TO_CORE[0]]
            source = into = w.at(at_y, c, part, half)
        else:
            for steps, target, at_y, part, half in (
                (X_HALF, X, y, HALF, x),
                (Y_HALF, Y, y, HALF, x),
                (Y_REST, Y, y, PART_A, 1 - x),
                (X_REST, X, 1 - y, PART_B, x),
            ):
                depths = [which for which, k in steps.items() if k == step]
                if depths:
                    break
            source = into = w.at(at_y, c, part, half, depth_of(depths[0]))
            if step in (Y_HALF[OWN], Y_REST[OWN]):
                source = w.own(part, half)
        return remote(source, into, self.send.at[m, step], self.recv.at[m, step], peer(target))

    def own_copy(self, m, half):
        t, y, c, _ = place()
        w = self.weights[m]
        return pltpu.make_async_copy(w.own(HALF, half), w.at(y, c, HALF, half, t), self.here.at[m, half])

    def begin(self, m):
        for half in range(2):
            self.own_copy(m, half).start()
        self.go(m, Z_FAR, Z_NEAR, Y_HALF[OWN], Y_REST[OWN])

    def spread(self, m):
        self.got(m, Z_FAR)
        self.go(m, Z_ON, X_HALF[FAR], Y_HALF[FAR])
        self.got(m, Z_NEAR)
        self.go(m, X_HALF[NEAR], Y_HALF[NEAR])
        self.got(m, Y_HALF[OWN])
        self.go(m, X_REST[OWN])

    def cross(self, m):
        self.got(m, Z_ON)
        self.go(m, X_HALF[LAST], Y_HALF[LAST])
        for half in range(2):
            self.own_copy(m, half).wait()
        self.go(m, TO_CORE[0])
        for q in (FAR, NEAR):
            self.got(m, X_HALF[q])
            self.go(m, Y_REST[q])
            self.got(m, Y_HALF[q])
            self.go(m, X_REST[q])

    def finish(self, m):
        self.got(m, X_HALF[LAST])
        self.go(m, Y_REST[LAST], TO_CORE[1])
        self.got(m, Y_HALF[LAST])
        self.go(m, X_REST[LAST], TO_CORE[2])

    def share(self, m):
        self.got(m, *Y_REST.values())
        self.go(m, TO_CORE[3])
        self.got(m, *X_REST.values())
        self.go(m, TO_CORE[4])

    def end(self, m):
        self.got(m, *TO_CORE)
        for step in range(GATHER_STEPS):
            self.copy(m, step).wait_send()

    def slots(self):
        n = len(self.weights)
        return staged(
            n, ((0, self.spread), (1, self.cross), (2, self.finish), (3, self.share), (4, self.end))
        )

    @staticmethod
    def semaphores(n):
        return [
            pltpu.SemaphoreType.DMA((n, GATHER_STEPS)),
            pltpu.SemaphoreType.DMA((n, GATHER_STEPS)),
            pltpu.SemaphoreType.DMA((n, 2)),
        ]


def whole_shape(kind):
    return {TRIPLE: (3, 1024, 1024), MIXING: (4, 256, 1024), UP: (1024, 4096), DOWN: (4, 1024, 1024)}[kind]


class Turns:
    def start(self):
        for turn in range(2):
            stays, near, far = self.parts(turn)
            pl.when(stays)(near.start)
            pl.when(jnp.logical_not(stays))(far.start)

    def wait(self):
        for turn in range(2):
            stays, near, far = self.parts(turn)
            pl.when(stays)(near.wait)
            pl.when(jnp.logical_not(stays))(far.wait)

    def __init__(self, array, into, send, recv, here):
        self.array, self.into, self.send, self.recv, self.here = array, into, send, recv, here

    @staticmethod
    def semaphores():
        return [pltpu.SemaphoreType.DMA((2,))] * 3


class ToChip(Turns):
    def parts(self, turn):
        t, y, c, x = place()
        slot = lax.rem(turn + t, 2)
        source, into = self.array.at[slot], self.into.at[turn]
        target = (2 * slot + c, y * 2 + t // 2, x)
        stays = jnp.logical_and(2 * slot + c == t, t // 2 == c)
        far = remote(source, into, self.send.at[turn], self.recv.at[turn], target)
        return stays, pltpu.make_async_copy(source, into, self.here.at[turn]), far


class ToOwner(Turns):
    def parts(self, turn):
        t, y, c, x = place()
        owner = 2 * c + lax.rem(t // 2 + turn, 2)
        source, into = self.array.at[turn], self.into.at[lax.rem(turn + owner, 2)]
        stays = jnp.logical_and(owner == t, lax.rem(t, 2) == c)
        far = remote(
            source, into, self.send.at[turn], self.recv.at[turn], (owner, y * 2 + lax.rem(t, 2), x)
        )
        return stays, pltpu.make_async_copy(source, into, self.here.at[turn]), far


ANYWHERE = pl.BlockSpec(memory_space=pl.ANY)
VMEM = pl.BlockSpec(memory_space=pltpu.VMEM)


def gather_kernel(shard, inputs, bias, whole, tokens, biases, *rest):
    t, y, c, x = place()
    gather = Gather([Weight(TRIPLE, shard, whole)], *rest[:3])
    move = ToChip(inputs, tokens, *rest[3:6])
    bias_send, bias_recv, bias_here = rest[6:]
    own_bias = pltpu.make_async_copy(bias, biases.at[t], bias_here.at[0])
    bias_copies = [
        remote(bias, biases.at[t], bias_send.at[k], bias_recv.at[k], (depth_of(q), y * 2 + c, x))
        for k, q in enumerate((NEAR, FAR, LAST))
    ]
    greet(neighbours())
    own_bias.start()
    for copy in bias_copies:
        copy.start()
    gather.begin(0)
    move.start()
    for slot in gather.slots():
        run(slot)
    move.wait()
    own_bias.wait()
    for copy in bias_copies:
        copy.wait()


def gather_first(inputs, bias, shard):
    return pl.pallas_call(
        gather_kernel,
        name="gather_first",
        in_specs=[ANYWHERE] * 3,
        out_specs=[ANYWHERE] * 3,
        out_shape=[
            jax.ShapeDtypeStruct(whole_shape(TRIPLE), bf16),
            jax.ShapeDtypeStruct(inputs.shape, bf16),
            jax.ShapeDtypeStruct((4,) + bias.shape, f32),
        ],
        scratch_shapes=Gather.semaphores(1)
        + Turns.semaphores()
        + [pltpu.SemaphoreType.DMA((3,)), pltpu.SemaphoreType.DMA((3,)), pltpu.SemaphoreType.DMA((1,))],
        compiler_params=pltpu.CompilerParams(collective_id=0, has_side_effects=True),
    )(shard, inputs, bias)


X_FIRST, Y_FIRST0, Y_FIRST1, Y_SECOND, X_SECOND, Z_LAST, Z_BACK, Z_BESIDE, DONE, CORES = range(10)
SUM_STEPS = CORES + 2


def shard_shape(kind, rows, lead=()):
    return lead + {TRIPLE: (3, rows, 256), MIXING: (rows, 256), UP: (rows, 1024), DOWN: (4 * rows, 256)}[kind]


def wide_shape(kind, rows, lead=()):
    return lead + {
        TRIPLE: (3, rows, 1024),
        MIXING: (4, rows, 256),
        UP: (rows, 4096),
        DOWN: (4, 4 * rows, 256),
    }[kind]


def sum_buffers(kind):
    shapes = (
        wide_shape(kind, 256, (2,)),
        wide_shape(kind, 256, (2,)),
        wide_shape(kind, 48, (2,)),
        wide_shape(kind, 80, (2,)),
        wide_shape(kind, 48),
        wide_shape(kind, 80),
        shard_shape(kind, 128, (3,)),
        shard_shape(kind, 128),
        shard_shape(kind, 128),
    )
    return [pltpu.VMEM(s, bf16) for s in shapes]


BUFFERS = 9


class Total(Weight):
    sections = {HALF: (0, 128), PART_A: (0, 80), PART_B: (80, 48)}

    def __init__(self, kind, part, out, buffers):
        super().__init__(kind, out, part)
        self.acc, self.got_core, self.x1, self.y1, self.y2, self.x2, self.z, self.mine, self.other = buffers

    def sums(self, y, part, half, depth=None):
        r = self.rows(part, half)
        n = self.shard.shape[-1]
        cols = slice(None) if depth is None else pl.ds(pl.multiple_of(depth * n, n), n)
        if self.kind == TRIPLE:
            return self.acc.at[y, :, r, cols]
        if self.kind == UP:
            return self.acc.at[y, r, cols]
        return self.acc.at[y, slice(None) if depth is None else depth, r, :]

    def source(self, y, c):
        g = pl.ds(pl.multiple_of((y * 2 + c) * 256, 256), 256)
        if self.kind == UP:
            return self.whole.at[g, :]
        return self.whole.at[:, g, :] if self.kind == TRIPLE else self.whole.at[:, :, g]


def each(ref, body):
    lead = ref.shape[:-2]
    count = 1
    for n in lead:
        count *= n
    for i in range(count):
        index, rest = [], i
        for n in reversed(lead):
            index.insert(0, rest % n)
            rest //= n

        def step(r, carry, index=tuple(index)):
            body(index + (pl.ds(pl.multiple_of(r * 16, 16), 16),))
            return carry

        lax.fori_loop(0, ref.shape[-2] // 16, step, 0)


def add_into(into, more):
    def body(index):
        into[index] = into[index] + more[index]

    each(more, body)


class Scatter(Copies):
    def __init__(self, totals, send, recv, here):
        self.totals, self.send, self.recv, self.here = totals, send, recv, here

    def copy(self, m, step):
        w = self.totals[m]
        _, y, c, x = place()
        if step >= CORES:
            k = step - CORES
            source, into, target = w.source(k, 1 - c), w.got_core.at[k], CORE
        else:
            source, into, target = {
                X_FIRST: lambda: (w.sums(slice(None), PART_B, 1 - x), w.x1, X),
                Y_FIRST0: lambda: (w.sums(1 - y, PART_A, 0), w.y1.at[0], Y),
                Y_FIRST1: lambda: (w.sums(1 - y, PART_A, 1), w.y1.at[1], Y),
                Y_SECOND: lambda: (w.sums(1 - y, PART_B, x), w.y2, Y),
                X_SECOND: lambda: (w.sums(y, PART_A, 1 - x), w.x2, X),
                Z_LAST: lambda: (w.sums(y, HALF, x, depth_of(LAST)), w.z.at[0], NEAR),
                Z_BACK: lambda: (w.sums(y, HALF, x, depth_of(FAR)), w.z.at[1], FAR),
                Z_BESIDE: lambda: (w.sums(y, HALF, x, depth_of(NEAR)), w.z.at[2], NEAR),
                DONE: lambda: (w.mine, w.other, X),
            }[step]()
        return remote(source, into, self.send.at[m, step], self.recv.at[m, step], peer(target))

    def load(self, m, y):
        w = self.totals[m]
        return pltpu.make_async_copy(w.source(y, place()[2]), w.acc.at[y], self.here.at[m, y])

    def begin(self, m):
        for y in range(2):
            self.load(m, y).start()
            self.go(m, CORES + y)

    def cores(self, m):
        for y in range(2):
            self.load(m, y).wait()
            self.got(m, CORES + y)
        add_into(self.totals[m].acc, self.totals[m].got_core)
        self.go(m, X_FIRST, Y_FIRST0, Y_FIRST1)

    def second(self, m):
        w = self.totals[m]
        _, y, _, x = place()
        self.got(m, X_FIRST)
        add_into(w.sums(slice(None), PART_B, x), w.x1)
        self.go(m, Y_SECOND)
        self.got(m, Y_FIRST0, Y_FIRST1)
        add_into(w.sums(y, PART_A, 0), w.y1.at[0])
        add_into(w.sums(y, PART_A, 1), w.y1.at[1])
        self.go(m, X_SECOND)

    def line(self, m):
        w = self.totals[m]
        _, y, _, x = place()
        self.got(m, Y_SECOND)
        add_into(w.sums(y, PART_B, x), w.y2)
        self.got(m, X_SECOND)
        add_into(w.sums(y, PART_A, x), w.x2)
        self.go(m, Z_LAST, Z_BESIDE)

    def line_on(self, m):
        w = self.totals[m]
        _, y, _, x = place()
        self.got(m, Z_LAST)
        add_into(w.sums(y, HALF, x, depth_of(FAR)), w.z.at[0])
        self.go(m, Z_BACK)

    def own_half(self, m):
        w = self.totals[m]
        _, y, _, x = place()
        self.got(m, Z_BESIDE, Z_BACK)
        own, near, far = w.sums(y, HALF, x, depth_of(OWN)), w.z.at[2], w.z.at[1]
        out = w.own(HALF, x)

        def body(index):
            total = (own[index].astype(f32) + near[index].astype(f32) + far[index].astype(f32)).astype(bf16)
            w.mine[index] = total
            out[index] = total.astype(f32)

        each(w.mine, body)
        self.go(m, DONE)

    def other_half(self, m):
        w = self.totals[m]
        self.got(m, DONE)
        out = w.own(HALF, 1 - place()[3])

        def body(index):
            out[index] = w.other[index].astype(f32)

        each(w.other, body)
        for step in range(SUM_STEPS):
            self.copy(m, step).wait_send()

    def slots(self):
        stages = (self.cores, self.second, self.line, self.line_on, self.own_half, self.other_half)
        return staged(len(self.totals), tuple(enumerate(stages)))

    @staticmethod
    def semaphores(n):
        return [
            pltpu.SemaphoreType.DMA((n, SUM_STEPS)),
            pltpu.SemaphoreType.DMA((n, SUM_STEPS)),
            pltpu.SemaphoreType.DMA((n, 2)),
        ]


AROUND = (CORE, X, Y, NEAR, FAR)


def scatter_kernel(kinds, *refs):
    n = len(kinds)
    parts, small, tokens = refs[:n], refs[n], refs[n + 1]
    outs, small_out, slots = refs[n + 2 : 2 * n + 2], refs[2 * n + 2], refs[2 * n + 3]
    rest = refs[2 * n + 4 :]
    buffers, rest = rest[: BUFFERS * n], rest[BUFFERS * n :]
    sums, arrived, small_send, small_recv = rest[:4]
    move = ToOwner(tokens, slots, *rest[4:7])
    scatter = Scatter(
        [Total(kind, parts[i], outs[i], buffers[BUFFERS * i :][:BUFFERS]) for i, kind in enumerate(kinds)],
        *rest[7:],
    )

    def small_copy(k):
        return remote(sums.at[k], arrived.at[k], small_send.at[k], small_recv.at[k], peer(AROUND[k]))

    greet(neighbours())
    for m in range(n):
        scatter.begin(m)
    move.start()
    sums[0] = small[...]
    small_copy(0).start()
    for k, slot in enumerate(scatter.slots()):
        run(slot)
        if k < len(AROUND):
            small_copy(k).wait_recv()
            sums[k + 1] = sums[k] + arrived[k]
            if k + 1 < len(AROUND):
                small_copy(k + 1).start()
    small_out[...] = sums[len(AROUND)]
    for k in range(len(AROUND)):
        small_copy(k).wait_send()
    move.wait()


def scatter_last(kinds, parts, small, tokens):
    n = len(kinds)
    scratch = sum((sum_buffers(kind) for kind in kinds), [])
    scratch += [
        pltpu.VMEM((len(AROUND) + 1,) + small.shape, f32),
        pltpu.VMEM((len(AROUND),) + small.shape, f32),
        pltpu.SemaphoreType.DMA((len(AROUND),)),
        pltpu.SemaphoreType.DMA((len(AROUND),)),
    ]
    return pl.pallas_call(
        functools.partial(scatter_kernel, kinds),
        name="scatter_last",
        in_specs=[ANYWHERE] * n + [VMEM, ANYWHERE],
        out_specs=[VMEM] * (n + 1) + [ANYWHERE],
        out_shape=[jax.ShapeDtypeStruct(shard_shape(kind, 256), f32) for kind in kinds]
        + [jax.ShapeDtypeStruct(small.shape, f32), jax.ShapeDtypeStruct(tokens.shape, bf16)],
        scratch_shapes=scratch + Turns.semaphores() + Scatter.semaphores(n),
        compiler_params=pltpu.CompilerParams(
            collective_id=1, has_side_effects=True, vmem_limit_bytes=60 << 20
        ),
    )(*parts, small, tokens)


def at_step(step, slots_at, slots):
    for when in sorted(set(slots_at)):

        @pl.when(step == when)
        def _(when=when):
            for place_at, slot in zip(slots_at, slots):
                if place_at == when:
                    run(slot)


GATHERED = (MIXING, UP, DOWN)
GATHER_AT = (1, 3, 5, 6, 7, 7, 7)


def forward_kernel(
    q_ref, ka, va, k_own, v_own, top, s0, s1, s2,
    o_ref, lse_ref, kb, vb, clip_top, w0, w1, w2,
    keys, values_low, values_high, k_far, v_far, pair_send, pair_recv, *rest,
):
    n = ka.shape[0]
    step, last = pl.program_id(0), pl.num_programs(0) - 1
    gather = Gather([Weight(*w) for w in zip(GATHERED, (s0, s1, s2), (w0, w1, w2))], *rest[:3])
    move = ToChip(top, clip_top, *rest[3:6])

    def pair(which, i):
        cols = pl.ds(pl.multiple_of(i * LANES, LANES), LANES)
        own, far = ((k_own, k_far), (v_own, v_far))[which]
        return remote(
            own.at[:, cols], far.at[:, cols], pair_send.at[which, i], pair_recv.at[which, i], peer(CORE)
        )

    @pl.when(step == 0)
    def _():
        greet(neighbours())
        for i in range(k_far.shape[1] // LANES):
            pair(0, i).start()
            pair(1, i).start()
        for m in range(len(GATHERED)):
            gather.begin(m)
        move.start()

    held = (keys, values_low, values_high)
    forward_load(slice(0, n), ka[...], va[...], *held)
    cols = pl.ds(pl.multiple_of(step * LANES, LANES), LANES)
    pair(0, step).wait_recv()
    pair(1, step).wait_recv()
    kb[...], vb[...] = k_far[:, cols], v_far[:, cols]
    forward_load(slice(n, 2 * n), kb[...], vb[...], *held)
    o_ref[...], lse_ref[...] = forward_heads(q_ref[...], *held)

    at_step(step, GATHER_AT, gather.slots())

    @pl.when(step == last)
    def _():
        for i in range(k_far.shape[1] // LANES):
            pair(0, i).wait_send()
            pair(1, i).wait_send()
        move.wait()


def attend_and_gather(q, k, v, top, shards):
    n, width = q.shape
    spec = pl.BlockSpec((n, LANES), lambda i: (0, i))
    blocks = width // LANES
    return pl.pallas_call(
        forward_kernel,
        grid=(blocks,),
        in_specs=[spec] * 3 + [ANYWHERE] * 6,
        out_specs=[spec] * 4 + [ANYWHERE] * 4,
        out_shape=[jax.ShapeDtypeStruct((n, width), bf16), jax.ShapeDtypeStruct((n, width), f32)]
        + [jax.ShapeDtypeStruct((n, width), bf16)] * 2
        + [jax.ShapeDtypeStruct(top.shape, bf16)]
        + [jax.ShapeDtypeStruct(whole_shape(kind), bf16) for kind in GATHERED],
        scratch_shapes=[pltpu.VMEM((2 * n, LANES), bf16)] * 3
        + [pltpu.VMEM((n, width), bf16)] * 2
        + [pltpu.SemaphoreType.DMA((2, blocks))] * 2
        + Gather.semaphores(len(GATHERED))
        + Turns.semaphores(),
        name="attend_and_gather",
        cost_estimate=pl.CostEstimate(
            flops=8 * n * n * width, bytes_accessed=16 * n * width, transcendentals=n * n * width // 32
        ),
        compiler_params=pltpu.CompilerParams(
            collective_id=2, has_side_effects=True, vmem_limit_bytes=56 << 20
        ),
    )(q, k, v, k, v, top, *shards)


SCATTERED = (DOWN, UP)
SCATTER_AT = (2, 3, 6, 7, 7, 7, 7)


def backward_kernel(
    q_ref, g_ref, o_ref, lse_ref, ka, kb, va, vb, output, p0, p1,
    dq_ref, dk_ref, dv_ref, slots, out0, out1,
    keys, values, dk, dv, far, got, pair_send, pair_recv, *rest,
):
    n = ka.shape[0]
    step, last = pl.program_id(0), pl.num_programs(0) - 1
    buffers, rest = rest[: BUFFERS * 2], rest[BUFFERS * 2 :]
    move = ToOwner(output, slots, *rest[:3])
    scatter = Scatter(
        [Total(DOWN, p0, out0, buffers[:BUFFERS]), Total(UP, p1, out1, buffers[BUFFERS:])], *rest[3:]
    )

    def pair(i):
        return remote(
            far.at[lax.rem(i, 2)], got.at[i], pair_send.at[lax.rem(i, 2)], pair_recv.at[i], peer(CORE)
        )

    @pl.when(step == 0)
    def _():
        greet(neighbours())
        for m in range(len(SCATTERED)):
            scatter.begin(m)
        move.start()

    for i, (k, v) in enumerate(((ka, va), (kb, vb))):
        keys[i * n : (i + 1) * n] = k[...]
        values[i * n : (i + 1) * n] = v[...]
    dq_ref[...] = backward_heads(
        q_ref[...], g_ref[...], o_ref[...], lse_ref[...], keys, values, dk, dv
    )

    def settle(i):
        cols = pl.ds(pl.multiple_of(i * LANES, LANES), LANES)
        pair(i).wait_recv()
        dk_ref[:, cols] = (dk_ref[:, cols].astype(f32) + got[i, 0].astype(f32)).astype(bf16)
        dv_ref[:, cols] = (dv_ref[:, cols].astype(f32) + got[i, 1].astype(f32)).astype(bf16)

    key_total, value_total = key_value_total(dk, dv)
    cols = pl.ds(pl.multiple_of(step * LANES, LANES), LANES)
    slot = lax.rem(step, 2)
    dk_ref[:, cols] = key_total[:n].astype(bf16)
    dv_ref[:, cols] = value_total[:n].astype(bf16)

    @pl.when(step >= 2)
    def _():
        pair(step - 2).wait_send()

    far[slot, 0] = key_total[n:].astype(bf16)
    far[slot, 1] = value_total[n:].astype(bf16)
    pair(step).start()

    @pl.when(step >= 1)
    def _():
        settle(step - 1)

    at_step(step, SCATTER_AT, scatter.slots())

    @pl.when(step == last)
    def _():
        settle(last)
        pair(last - 1).wait_send()
        pair(last).wait_send()
        move.wait()


def attend_and_scatter(q, g, o, lse, ka, kb, va, vb, output, parts):
    n, width = q.shape
    spec = pl.BlockSpec((n, LANES), lambda i: (0, i))
    blocks = width // LANES
    return pl.pallas_call(
        backward_kernel,
        grid=(blocks,),
        in_specs=[spec] * 8 + [ANYWHERE] * 3,
        out_specs=[spec] + [VMEM] * 2 + [ANYWHERE] + [VMEM] * 2,
        out_shape=[jax.ShapeDtypeStruct((n, width), bf16)] * 3
        + [jax.ShapeDtypeStruct(output.shape, bf16)]
        + [jax.ShapeDtypeStruct(shard_shape(kind, 256), f32) for kind in SCATTERED],
        scratch_shapes=[pltpu.VMEM((2 * n, LANES), bf16)] * 2
        + [pltpu.VMEM((LANES, 2 * n), f32)] * 2
        + [pltpu.VMEM((2, 2, n, LANES), bf16), pltpu.VMEM((blocks, 2, n, LANES), bf16)]
        + [pltpu.SemaphoreType.DMA((2,)), pltpu.SemaphoreType.DMA((blocks,))]
        + sum_buffers(DOWN)
        + sum_buffers(UP)
        + Turns.semaphores()
        + Scatter.semaphores(len(SCATTERED)),
        name="attend_and_scatter",
        cost_estimate=pl.CostEstimate(
            flops=20 * n * n * width, bytes_accessed=28 * n * width, transcendentals=n * n * width // 32
        ),
        compiler_params=pltpu.CompilerParams(
            collective_id=3, has_side_effects=True, vmem_limit_bytes=62 << 20
        ),
    )(q, g, o, lse, ka, kb, va, vb, output, *parts)


def normalize(values):
    center = values - jnp.mean(values, axis=-1, keepdims=True)
    inverse = lax.rsqrt(jnp.mean(center * center, axis=-1, keepdims=True) + epsilon)
    return (center * inverse, inverse)


def normalize_back(upstream, normed, inverse, norm_gain):
    scaled = upstream * norm_gain
    return inverse * (
        scaled
        - jnp.mean(scaled, axis=-1, keepdims=True)
        - normed * jnp.mean(scaled * normed, axis=-1, keepdims=True)
    )


def clip_exchange(tensor_count, group_count):
    there, back = [], []
    for turn in range(2):
        pairs = []
        for z in range(tensor_count):
            for g in range(group_count):
                slot = (turn + z) % 2
                target = (2 * slot + g % 2) * group_count + g - g % 2 + z // 2
                pairs.append((z * group_count + g, target))
        there.append(pairs)
        back.append([(b, a) for a, b in pairs])
    return there, back


def local(
    inputs,
    clips_here,
    first_gain,
    first_shift,
    query_key_value,
    query_bias,
    value_bias,
    output_weight,
    output_bias,
    second_gain,
    second_shift,
    expand_weight,
    expand_bias,
    contract_weight,
    contract_bias,
    output_grad,
):
    slot_count, rows, width = inputs.shape
    tensor_index = lax.axis_index("tensor")
    tensor_count = lax.axis_size("tensor")
    group_index = lax.axis_index("group")
    group_count = lax.axis_size("group")
    both = ("tensor", "group")
    there, back = clip_exchange(tensor_count, group_count)
    pair = [(g, g + 1 - 2 * (g % 2)) for g in range(group_count)]

    def to_chip(array):
        pieces = []
        for turn in range(2):
            slot = (turn + tensor_index) % 2
            pieces.append(
                lax.ppermute(lax.dynamic_index_in_dim(array, slot, keepdims=False), both, there[turn])
            )
        return jnp.concatenate(pieces, axis=0)

    def to_owner(array):
        received = [
            lax.ppermute(array[turn * rows : (turn + 1) * rows], both, back[turn]) for turn in range(2)
        ]
        even = tensor_index % 2 == 0
        return jnp.stack(
            [jnp.where(even, received[0], received[1]), jnp.where(even, received[1], received[0])]
        )

    def gather(shard):
        return lax.all_gather(shard, both, axis=0).reshape(tensor_count, group_count, *shard.shape)

    direct = (tensor_count, group_count, lax.axis_size("cross")) == (4, 4, 2)
    alive = (jnp.arange(slot_count, dtype=jnp.int32) < clips_here[0]).astype(bf16)[:, None, None]
    bias = jnp.concatenate([query_bias, value_bias, expand_bias])
    if direct:
        bias_size = bias.shape[0]
        bias = jnp.pad(bias.astype(f32), (0, -bias_size % (8 * LANES))).reshape(-1, LANES)
        triple, tokens, biases = gather_first(inputs, bias, query_key_value)
        tokens = tokens.reshape(-1, width).astype(f32)
        biases = biases.reshape(tensor_count, -1)[:, :bias_size]
    else:
        tokens = to_chip(inputs).astype(f32)
        triple = gather(query_key_value).transpose(2, 1, 3, 0, 4).reshape(3, width, width)
        mixing = gather(output_weight).transpose(0, 2, 1, 3).reshape(width, width)
        up = gather(expand_weight).transpose(1, 2, 0, 3).reshape(width, -1)
        down = gather(contract_weight).transpose(0, 2, 1, 3).reshape(-1, width)
        biases = lax.all_gather(bias, "tensor", axis=0).astype(f32)
    split_at = (query_bias.shape[0], query_bias.shape[0] + value_bias.shape[0])
    query_offset, value_offset, hidden_offset = (
        part.reshape(-1) for part in jnp.split(biases, split_at, axis=1)
    )

    gain_one = first_gain.astype(f32)
    gain_two = second_gain.astype(f32)
    first_plain, first_inverse = normalize(tokens)
    first_rows = (first_plain * gain_one + first_shift.astype(f32)).astype(bf16)
    keys = dot(first_rows, triple[1]).astype(bf16)
    values = (dot(first_rows, triple[2]) + value_offset).astype(bf16)
    queries = ((dot(first_rows, triple[0]) + query_offset) * query_scale).astype(bf16)
    if direct:
        attended, log_totals, far_keys, far_values, top, mixing, up, down = attend_and_gather(
            queries, keys, values, output_grad * alive, (output_weight, expand_weight, contract_weight)
        )
        top, mixing, down = top.reshape(-1, width), mixing.reshape(-1, width), down.reshape(-1, width)
    else:
        top = to_chip(output_grad * alive)
        far_keys = lax.ppermute(keys, "group", pair)
        far_values = lax.ppermute(values, "group", pair)
        attended, log_totals = attend_forward(queries, keys, far_keys, values, far_values)
    middle = tokens + dot(attended, mixing) + output_bias.astype(f32)
    second_plain, second_inverse = normalize(middle)
    second_rows = (second_plain * gain_two + second_shift.astype(f32)).astype(bf16)
    hidden_pre = dot(second_rows, up) + hidden_offset
    normal_cdf = 0.5 * (1.0 + lax.erf(hidden_pre * root_half))
    hidden = (hidden_pre * normal_cdf).astype(bf16)
    slope = normal_cdf + hidden_pre * (inv_root_two_pi * jnp.exp(-0.5 * hidden_pre * hidden_pre))
    output = (middle + dot(hidden, down) + contract_bias.astype(f32)).astype(bf16)

    contract_bias_part = jnp.sum(top.astype(f32), axis=0)
    contract_part = dot(hidden, top, TN).astype(bf16)
    pre_grad = (dot(top, down, NT) * slope).astype(bf16)
    expand_bias_part = jnp.sum(pre_grad.astype(f32), axis=0)
    expand_part = dot(second_rows, pre_grad, TN).astype(bf16)
    second_grad = dot(pre_grad, up, NT)
    second_gain_part = jnp.sum(second_grad * second_plain, axis=0)
    second_shift_part = jnp.sum(second_grad, axis=0)
    middle_grad = top.astype(f32) + normalize_back(second_grad, second_plain, second_inverse, gain_two)
    branch_grad = middle_grad.astype(bf16)
    output_bias_part = jnp.sum(branch_grad.astype(f32), axis=0)
    mixing_part = dot(attended, branch_grad, TN).astype(bf16)
    attended_grad = dot(branch_grad, mixing, NT).astype(bf16)
    if direct:
        query_grad, key_grad, value_grad, output, contract_sum, expand_sum = attend_and_scatter(
            queries, attended_grad, attended, log_totals, keys, far_keys, values, far_values,
            output.reshape(inputs.shape), (contract_part.reshape(4, -1, width), expand_part),
        )
    else:
        output = to_owner(output)
        query_grad, key_own, key_far, value_own, value_far = attend_backward(
            queries, attended_grad, attended, log_totals, keys, far_keys, values, far_values
        )
        key_grad = (key_own.astype(f32) + lax.ppermute(key_far, "group", pair).astype(f32)).astype(bf16)
        value_grad = (value_own.astype(f32) + lax.ppermute(value_far, "group", pair).astype(f32)).astype(
            bf16
        )
    query_bias_part = jnp.sum(query_grad.astype(f32), axis=0)
    value_bias_part = jnp.sum(value_grad.astype(f32), axis=0)
    triple_part = jnp.stack(
        [dot(first_rows, d, TN).astype(bf16) for d in (query_grad, key_grad, value_grad)]
    )
    first_grad = (
        dot(query_grad, triple[0], NT) + dot(key_grad, triple[1], NT) + dot(value_grad, triple[2], NT)
    )
    first_gain_part = jnp.sum(first_grad * first_plain, axis=0)
    first_shift_part = jnp.sum(first_grad, axis=0)
    input_grad = (
        middle_grad + normalize_back(first_grad, first_plain, first_inverse, gain_one)
    ).astype(bf16)

    small_parts = (
        first_gain_part,
        first_shift_part,
        query_bias_part,
        value_bias_part,
        output_bias_part,
        second_gain_part,
        second_shift_part,
        expand_bias_part,
        contract_bias_part,
    )
    if direct:
        mixing_sum, triple_sum, small, input_grad = scatter_last(
            (MIXING, TRIPLE),
            (mixing_part.reshape(4, -1, width), triple_part),
            jnp.concatenate(small_parts).reshape(-1, LANES),
            input_grad.reshape(inputs.shape),
        )
        small, small_sums = small.reshape(-1), []
        for part in small_parts:
            small_sums.append(small[: part.shape[0]])
            small = small[part.shape[0] :]
    else:
        input_grad = to_owner(input_grad)

        def scatter(stacked):
            count = tensor_count * group_count
            part = lax.psum_scatter(stacked.reshape(count, *stacked.shape[2:]), both, scatter_dimension=0)
            return lax.psum(part, "cross").astype(f32)

        depth, across = width // group_count, width // tensor_count
        unit = expand_bias.shape[0]
        triple_sum = scatter(
            triple_part.reshape(3, group_count, depth, tensor_count, across).transpose(3, 1, 0, 2, 4)
        )
        mixing_sum = scatter(
            mixing_part.reshape(tensor_count, across, group_count, depth).transpose(0, 2, 1, 3)
        )
        expand_sum = scatter(
            expand_part.reshape(group_count, depth, tensor_count, unit).transpose(2, 0, 1, 3)
        )
        contract_sum = scatter(
            contract_part.reshape(tensor_count, unit, group_count, depth).transpose(0, 2, 1, 3)
        )
        small_sums = lax.psum(small_parts, ("tensor", "group", "cross"))

    def own_group(full_vector):
        size = full_vector.shape[0] // group_count
        return lax.dynamic_slice_in_dim(full_vector, group_index * size, size)

    def own_split(full_vector):
        size = full_vector.shape[0] // (group_count * tensor_count)
        return lax.dynamic_slice_in_dim(
            full_vector, (tensor_index * group_count + group_index) * size, size
        )

    return (
        output,
        input_grad,
        own_group(small_sums[0]),
        own_group(small_sums[1]),
        triple_sum,
        own_split(small_sums[2]),
        own_split(small_sums[3]),
        mixing_sum,
        own_group(small_sums[4]),
        own_group(small_sums[5]),
        own_group(small_sums[6]),
        expand_sum,
        own_split(small_sums[7]),
        contract_sum,
        own_group(small_sums[8]),
    )


def solution(mesh):
    in_specs = (
        P(("group", "cross"), "tensor", None),
        P(("group", "cross")),
        P(),
        P(),
        P(None, "group", "tensor"),
        P("tensor"),
        P("tensor"),
        P("tensor", "group"),
        P(),
        P(),
        P(),
        P("group", "tensor"),
        P("tensor"),
        P("tensor", "group"),
        P(),
        P(("group", "cross"), "tensor", None),
    )
    out_specs = (
        P(("group", "cross"), "tensor", None),
        P(("group", "cross"), "tensor", None),
        P("group"),
        P("group"),
        P(None, "group", "tensor"),
        P(("tensor", "group")),
        P(("tensor", "group")),
        P("tensor", "group"),
        P("group"),
        P("group"),
        P("group"),
        P("group", "tensor"),
        P(("tensor", "group")),
        P("tensor", "group"),
        P("group"),
    )
    return jax.shard_map(local, mesh=mesh, in_specs=in_specs, out_specs=out_specs, check_vma=False)
```

time: 912 us -> 550 us (0.60)
  waiting for transfers between devices: 306 us -> 0 us
  Pallas kernels: 99.4 us -> 389 us
  blocking collectives: 140 us -> 0 us
  local copies, waits for them, and re-layouts: 152 us -> 16.3 us
  starting transfers between devices: 28 us -> 0 us
  between operations: 15.8 us -> 2.42 us
  matrix products: 131 us -> 118 us
    pallas_call x2 -> x4, Pallas kernels: 99.4 us -> 389 us  [the longest x1 160 us: attend_and_scatter(): pl.pallas_call(backward_kernel, grid=(blocks,), in_specs=[spec] * 8 + [AN...]
    reduce_scatter x4 -> x0, waiting for transfers between devices: 216 us -> none  [scatter(): lax.psum_scatter(stacked.astype(bf16).reshape(count, *stacked.shape[2:]),...]
    all_gather x1 -> x0, blocking collectives: 87.4 us -> none  [local(): lax.all_gather(jnp.concatenate([query_bias, value_bias, expand_bias]), 't...]
    all_gather x4 -> x0, waiting for transfers between devices: 66.2 us -> none  [gather(): lax.all_gather(shard, both, axis=0)]
    convert_element_type x7 -> x0, local copies, waits for them, and re-layouts: 59.8 us -> none  [scatter(): stacked.astype(bf16).reshape(count, *stacked.shape[2:])]
    psum x1 -> x0, blocking collectives: 52.9 us -> none  [local(): lax.psum((first_gain_part, first_shift_part, query_bias_part, value_bias_...]
    reshape x4 -> x0, local copies, waits for them, and re-layouts: 35.8 us -> none  [gather(): lax.all_gather(shard, both, axis=0)]
    ppermute x12 -> x0, starting transfers between devices: 27.6 us -> none  [the longest x4 14.7 us: to_chip(): lax.ppermute(lax.dynamic_index_in_dim(array, slot, keepdims=False), both,...]
  transfers between devices with their start and end apart: 21 -> 0, of which waited for: 5 -> 0; matrix products, arithmetic and copies ran while one was open for 26% -> 0% of each run, Pallas kernels for 5% -> 0%
where the time goes in v2:
time: 550 us; the launch traced here: 544 us
  Pallas kernels  389 us (71%)
  matrix products  118 us (21%)
  other arithmetic  18 us (3%)
  local copies, waits for them, and re-layouts  16.3 us (3%)
    pallas_call x1, Pallas kernels, attend_and_scatter(): pl.pallas_call(backward_kernel, grid=(blocks,), in_specs=[spec] * 8 + [AN...  160 us
    dot_general x18, matrix products, dot(): return lax.dot_general(a, b, dims, preferred_element_type=f32)  118 us
    pallas_call x1, Pallas kernels, attend_and_gather(): pl.pallas_call(forward_kernel, grid=(blocks,), in_specs=[spec] * 3 + [ANY...  110 us
    pallas_call x1, Pallas kernels, scatter_last(): pl.pallas_call(functools.partial(scatter_kernel, kinds), name='scatter_la...  73.4 us
    pallas_call x1, Pallas kernels, gather_first(): pl.pallas_call(gather_kernel, name='gather_first', in_specs=[ANYWHERE] *...  45.9 us

profile of v2, /device:TPU:0, one launch (start us, length us, event | category | flops | bytes accessed | tf_op | source)
XLA Modules:
  0.0 544.4 jit_solution(12590650091528376534)
XLA Ops:
  0.6 1.3 fusion.47.bias
  2.0 45.9 %gather_first.1 = (bf16[3,1024,1024]{2,1,0:T(8,128)(2,1)}, bf16[2,392,1024]{2,1,0:T(8,128)(2,1)}, f32[4,16,128]{2,1,0:T(8,128)}) custom-call(bf16[3,256,256]{2,1,0:T(8,128)(2,1)} %shard.1, bf16[2,392,1024]{2,1,0:T(8,128)(2,1)} %inputs.1, f32[16,128]{1,0:T(8,128)} %fusion.47.bias), custom_call_target="tpu_custom_call" | custom-call | tf_op jit(solution)/shard_map/gather_first/pallas_call | solution.py:437
  47.8 0.9 copy.37
  48.8 0.7 convert_element_type.120
  49.4 0.7 convert_element_type.119
  50.1 1.7 convert_reduce_fusion.1
  51.9 2.0 fusion.8
  53.9 0.6 fusion.11
  54.6 4.9 multiply_convert_fusion.1.q_ref
  59.5 3.0 fusion.31.ka.k_own
  62.5 3.0 add_convert_fusion.4.va.v_own
  66.3 1.4 broadcast_multiply_fusion.top
  67.6 109.9 %attend_and_gather.1 = (bf16[784,1024]{1,0:T(8,128)(2,1)}, f32[784,1024]{1,0:T(8,128)}, bf16[784,1024]{1,0:T(8,128)(2,1)}, bf16[784,1024]{1,0:T(8,128)(2,1)}, bf...) custom-call(bf16[784,1024]{1,0:T(8,128)(2,1)} %multiply_convert_fusi, ...), custom_call_target="tpu_custom_call" | custom-call | flops 5035261952 | bytes 12845056 | tf_op jit(solution)/shard_map/attend_and_gather/pallas_call | solution.py:770
  177.5 0.0 copy-start.23
  177.5 3.9 bitcast_add_fusion
  181.5 0.3 add_reduce_fusion
  181.8 0.6 multiply_reduce_fusion.4
  182.5 14.5 %multiply_convert_fusion = (bf16[784,4096]{1,0:T(8,128)(2,1)}, f32[784,4096]{1,0:T(8,128)}) fusion(f32[4096]{0:T(1024)S(1)} %bitcast.134, bf16[1024,4096]{1,0:T(8,128)(2,1)} %get-tuple-element.43, f32[1024]{0:T(1024)S(1)} %convert_element_type.132, f32[1024]{0:T(1024)S(1)} %convert_element_type.131, f32[784]{0:T(1024)S(1)} %add_rsqrt_fusion, ...), kind=kOutput, calls=%fused_computation.8 | convolution fusion | flops 6600753152 | bytes 30902400 | tf_op jit(solution)/shard_map/dot_general | solution.py:28
  197.0 15.1 %convert_reduce_fusion = (f32[4096]{0:T(1024)S(1)}, bf16[784,4096]{1,0:T(8,128)(2,1)}) fusion(f32[784,4096]{1,0:T(8,128)} %get-tuple-element.81, f32[4096]{0:T(1024)S(1)} %bitcast.135, bf16[784,1024]{1,0:T(8,128)(2,1)S(1)} %bitcast.120, bf16[4096,1024]{1,0:T(8,128)(2,1)S(1)} %bitcast.140), kind=kOutput, calls=%fused_computation.7 | convolution fusion | flops 6618411008 | bytes 29294592 | tf_op jit(solution)/shard_map/dot_general | solution.py:28
  212.1 12.2 %multiply_reduce_fusion.1 = (f32[1024]{0:T(1024)S(1)}, f32[784]{0:T(1024)S(1)}, f32[784]{0:T(1024)S(1)}, f32[1024]{0:T(1024)S(1)}, f32[784,1024]{1,0:T(8,128)S(1)}) fusion(f32[784]{0:T(1024)S(1)} %add_rsqrt_fusion, f32[784]{0:T(1024)S(1)} %broadcast_multiply_fusion.5, f32[784,1024]{1,0:T(8,128)S(1)} %bitcast_add_fusion, ...), kind=kOutput, calls=%fused_computation.27 | convolution fusion | flops 6584692736 | bytes 21262592 | tf_op jit(solution)/shard_map/dot_general | solution.py:28
  224.3 1.5 convert_reduce_fusion.3
  225.8 0.0 copy-done.27
  225.9 3.0 convolution_convert_fusion.3.g_ref
  228.9 0.4 slice-done.7
  229.4 8.0 %add_convert_fusion.2 = bf16[784,1024]{1,0:T(8,128)(2,1)} fusion(f32[784,1024]{1,0:T(8,128)S(1)} %bitcast_add_fusion, f32[1024]{0:T(1024)S(1)} %convert_element_type.138, f32[1024]{0:T(1024)S(1)} %convert_element_type.130, bf16[784,4096]{1,0:T(8,128)(2,1)S(1)} %bitcast.147, bf16[4096,1024]{1,0:T(8,128)(2,1)S(1)} %bitcast.141), kind=kOutput, calls=%fused_computation.34 | convolution fusion | flops 6579879936 | bytes 19636224 | tf_op jit(solution)/shard_map/dot_general | solution.py:28
  237.4 14.2 %convolution_convert_fusion.1 = bf16[4096,1024]{1,0:T(8,128)(2,1)} fusion(bf16[784,4096]{1,0:T(8,128)(2,1)} %get-tuple-element.80, bf16[784,1024]{1,0:T(8,128)(2,1)S(1)} %bitcast.121), kind=kOutput, calls=%fused_computation.11 | convolution fusion | flops 6580862976 | bytes 16416768 | tf_op jit(solution)/shard_map/dot_general | solution.py:28
  251.6 14.4 %convolution_convert_fusion.p1 = bf16[1024,4096]{1,0:T(8,128)(2,1)} fusion(bf16[784,4096]{1,0:T(8,128)(2,1)} %get-tuple-element.84, f32[1024]{0:T(1024)S(1)} %convert_element_type.132, f32[1024]{0:T(1024)S(1)} %convert_element_type.131, f32[784,1024]{1,0:T(8,128)S(1)} %bitcast_add_fusion, f32[784]{0:T(1024)S(1)} %add_rsqrt_fusion, ...), kind=kOutput, calls=%fused_computation.10 | convolution fusion | flops 6585679872 | bytes 18040960 | tf_op jit(solution)/shard_map/dot_general | solution.py:28
  266.0 160.1 %attend_and_scatter.1 = (bf16[784,1024]{1,0:T(8,128)(2,1)}, bf16[784,1024]{1,0:T(8,128)(2,1)}, bf16[784,1024]{1,0:T(8,128)(2,1)}, bf16[2,392,1024]{2,1,0:T(8,128...) custom-call(bf16[784,1024]{1,0:T(8,128)(2,1)} %multiply_convert_fusion.1.q_ref, ...), custom_call_target="tpu_custom_call" | custom-call | flops 12588154880 | bytes 22478848 | tf_op jit(solution)/shard_map/attend_and_scatter/pallas_call | solution.py:868
  426.2 0.0 copy-start.22
  426.2 6.3 %convolution_convert_fusion.2 = bf16[1024,1024]{1,0:T(8,128)(2,1)} fusion(bf16[784,1024]{1,0:T(8,128)(2,1)} %get-tuple-element.40.o_ref, f32[784,1024]{1,0:T(8,128)} %copy-done.2), kind=kOutput, calls=%fused_computation.60 | convolution fusion | flops 1646018560 | bytes 6914048 | tf_op jit(solution)/shard_map/dot_general | solution.py:28
  432.5 0.1 rsqrt.22
  432.5 0.1 div.32
  432.6 0.4 fusion.12
  433.0 1.0 copy-done.9
  434.1 3.7 fusion.13
  437.9 1.9 fusion.17
  439.8 2.9 multiply_reduce_fusion.5
  442.8 2.8 add_convert_fusion
  445.6 2.4 convert_bitcast_fusion
  448.0 2.4 convert_bitcast_fusion.1
  450.4 2.4 convert_bitcast_fusion.2
  452.8 3.1 pad_maximum_fusion.refs_1_
  455.9 0.3 convert_reduce_fusion.5
  456.2 0.3 convert_reduce_fusion.4
  456.5 0.3 convert_reduce_fusion.2
  456.8 0.6 copy-done.18
  457.4 73.4 %scatter_last.1 = (f32[256,256]{1,0:T(8,128)}, f32[3,256,256]{2,1,0:T(8,128)}, f32[96,128]{1,0:T(8,128)}, bf16[2,392,1024]{2,1,0:T(8,128)(2,1)}) custom-call(bf16[4,256,1024]{2,1,0:T(8,128)(2,1)} %bitcast.122, bf16[3,1024,1024]{2,1,0:T(8,128)(2,1)} %pad_maximum_fusion.refs_1_, f32[96,128]{1,0:T(8,128)} %bitcast.132, bf16[2,392,1024]{2,1,0:T(8,128)(2,1)} %bitcast.119), custom_call_target="tpu_custom_call" | custom-call | tf_op jit(solution)/shard_map/scatter_last/pallas_call | solution.py:692
  530.9 0.8 slice_bitcast_fusion.4
  531.7 0.6 dynamic_slice.27
  532.4 0.6 dynamic_slice.28
  533.0 0.6 dynamic_slice.29
  533.6 0.6 dynamic_slice.30
  534.2 0.6 dynamic_slice.31
  534.8 0.6 dynamic_slice.32
  535.4 0.6 dynamic_slice.33
  536.1 0.7 slice_bitcast_fusion.1
  536.8 0.6 dynamic_slice.34
  537.4 0.6 dynamic_slice.35
  538.1 1.2 copy.54
  539.2 1.2 copy.55
  540.4 0.9 copy.56
  541.3 0.7 copy.57
  542.0 1.0 copy.58
  542.9 1.0 copy.59
  (98 shorter events, 0.3 us)
Async XLA Ops:
  47.8 6.1 %copy-start = (bf16[2,392,1024]{2,1,0:T(8,128)(2,1)S(1)}, bf16[2,392,1024]{2,1,0:T(8,128)(2,1)}, u32[]{:S(2)}) copy-start(bf16[2,392,1024]{2,1,0:T(8,128)(2,1)} %get-tuple-element.36) | copy-start | bytes 4816900
  49.4 5.1 copy-start.19
  50.1 4.5 copy-start.16
  51.8 7.7 %copy-start.14 = (f32[2,392]{1,0:T(2,128)}, f32[2,392]{1,0:T(2,128)S(1)}, u32[]{:S(2)}) copy-start(f32[2,392]{1,0:T(2,128)S(1)} %broadcast_multiply_fusion.6) | copy-start | bytes 9412
  53.9 5.6 %copy-start.21 = (f32[2,392]{1,0:T(2,128)}, f32[2,392]{1,0:T(2,128)S(1)}, u32[]{:S(2)}) copy-start(f32[2,392]{1,0:T(2,128)S(1)} %add_rsqrt_fusion.1) | copy-start | bytes 9412
  53.9 5.6 %slice-start = ((s8[6291456]{0:T(1024)(128)(4,1)}), s8[4194304]{0:T(1024)(128)(4,1)S(1)}, s32[]{:S(2)}) async-start(s8[6291456]{0:T(1024)(128)(4,1)} %bitcast.126), calls=%async_computation | async-start | bytes 8388608
  54.6 4.9 slice-start.1
  62.5 3.7 copy-start.6
  177.5 3.9 copy-start.23
  181.4 0.9 copy-start.24
  181.5 1.0 copy-start.25
  181.8 15.2 %slice-start.4 = ((s8[8388608]{0:T(1024)(128)(4,1)}), s8[4194304]{0:T(1024)(128)(4,1)S(1)}, s32[]{:S(2)}) async-start(s8[8388608]{0:T(1024)(128)(4,1)} %bitcast.138), calls=%async_computation.4 | async-start | bytes 8388608
  182.4 14.5 %copy-start.4 = (bf16[2,392,1024]{2,1,0:T(8,128)(2,1)S(1)}, bf16[2,392,1024]{2,1,0:T(8,128)(2,1)}, u32[]{:S(2)}) copy-start(bf16[2,392,1024]{2,1,0:T(8,128)(2,1)} %get-tuple-element.39) | copy-start | bytes 4816900
  182.4 14.5 %slice-start.5 = ((s8[8388608]{0:T(1024)(128)(4,1)}), s8[4194304]{0:T(1024)(128)(4,1)S(1)}, s32[]{:S(2)}) async-start(s8[8388608]{0:T(1024)(128)(4,1)} %bitcast.138), calls=%async_computation.5 | async-start | bytes 8388608
  224.3 1.6 copy-start.27
  224.3 4.6 slice-start.6
  225.8 3.1 copy-start.2
  225.9 3.1 copy-start.26
  225.9 3.5 slice-start.7
  426.2 6.3 %copy-start.22 = (f32[2,392]{1,0:T(2,128)S(1)}, f32[2,392]{1,0:T(2,128)}, u32[]{:S(2)}) copy-start(f32[2,392]{1,0:T(2,128)} %copy-done.21) | copy-start | bytes 9412
  426.2 6.4 %copy-start.15 = (f32[2,392]{1,0:T(2,128)S(1)}, f32[2,392]{1,0:T(2,128)}, u32[]{:S(2)}) copy-start(f32[2,392]{1,0:T(2,128)} %copy-done.14) | copy-start | bytes 9412
  426.2 6.4 %copy-start.1 = (bf16[2,392,1024]{2,1,0:T(8,128)(2,1)S(1)}, bf16[2,392,1024]{2,1,0:T(8,128)(2,1)}, u32[]{:S(2)}) copy-start(bf16[2,392,1024]{2,1,0:T(8,128)(2,1)} %get-tuple-element.36) | copy-start | bytes 4816900
  432.6 1.4 copy-start.9
  432.6 5.2 slice-start.2
  434.0 3.8 slice-start.3
  434.0 3.8 copy-start.28
  437.8 1.9 copy-start.5
  437.8 1.9 copy-start.17
  439.8 3.0 copy-start.3
  439.8 3.0 copy-start.20
  456.8 0.6 copy-start.18
  457.4 80.6 %copy-start.7 = (bf16[2,392,1024]{2,1,0:T(8,128)(2,1)S(1)}, bf16[2,392,1024]{2,1,0:T(8,128)(2,1)}, u32[]{:S(2)}) copy-start(bf16[2,392,1024]{2,1,0:T(8,128)(2,1)} %get-tuple-element.102) | copy-start | bytes 4816900
  530.9 8.3 %copy-start.8 = (bf16[2,392,1024]{2,1,0:T(8,128)(2,1)S(1)}, bf16[2,392,1024]{2,1,0:T(8,128)(2,1)}, u32[]{:S(2)}) copy-start(bf16[2,392,1024]{2,1,0:T(8,128)(2,1)} %get-tuple-element.103) | copy-start | bytes 4816900
  538.1 2.3 copy-start.12
  538.1 3.2 copy-start.13
  539.2 2.7 copy-start.11
  539.2 3.7 copy-start.10

commit v3 on v2

--- a/solution.py
+++ b/solution.py
@@ -451,36 +451,19 @@
     )(shard, inputs, bias)
 
 
-X_FIRST, Y_FIRST0, Y_FIRST1, Y_SECOND, X_SECOND, Z_LAST, Z_BACK, Z_BESIDE, DONE, CORES = range(10)
+X_FIRST, Y_FIRST0, Y_FIRST1, Y_SECOND, X_SECOND, CORES = range(6)
 SUM_STEPS = CORES + 2
+Z_LAST, Z_BACK, Z_BESIDE, DONE = range(4)
+ORDER = (LAST, FAR, NEAR, OWN)
 
 
 def shard_shape(kind, rows, lead=()):
     return lead + {TRIPLE: (3, rows, 256), MIXING: (rows, 256), UP: (rows, 1024), DOWN: (4 * rows, 256)}[kind]
 
 
-def wide_shape(kind, rows, lead=()):
-    return lead + {
-        TRIPLE: (3, rows, 1024),
-        MIXING: (4, rows, 256),
-        UP: (rows, 4096),
-        DOWN: (4, 4 * rows, 256),
-    }[kind]
-
-
 def sum_buffers(kind):
-    shapes = (
-        wide_shape(kind, 256, (2,)),
-        wide_shape(kind, 256, (2,)),
-        wide_shape(kind, 48, (2,)),
-        wide_shape(kind, 80, (2,)),
-        wide_shape(kind, 48),
-        wide_shape(kind, 80),
-        shard_shape(kind, 128, (3,)),
-        shard_shape(kind, 128),
-        shard_shape(kind, 128),
-    )
-    return [pltpu.VMEM(s, bf16) for s in shapes]
+    leads = ((256, 4, 2), (256, 4, 2), (48, 4, 2), (80, 4, 2), (48, 4), (80, 4), (128, 3), (128,), (128,))
+    return [pltpu.VMEM(shard_shape(kind, rows, tuple(lead)), bf16) for rows, *lead in leads]
 
 
 BUFFERS = 9
@@ -493,21 +476,17 @@
         super().__init__(kind, out, part)
         self.acc, self.got_core, self.x1, self.y1, self.y2, self.x2, self.z, self.mine, self.other = buffers
 
-    def sums(self, y, part, half, depth=None):
+    def sums(self, k, y, part, half):
         r = self.rows(part, half)
-        n = self.shard.shape[-1]
-        cols = slice(None) if depth is None else pl.ds(pl.multiple_of(depth * n, n), n)
-        if self.kind == TRIPLE:
-            return self.acc.at[y, :, r, cols]
-        if self.kind == UP:
-            return self.acc.at[y, r, cols]
-        return self.acc.at[y, slice(None) if depth is None else depth, r, :]
-
-    def source(self, y, c):
+        return self.acc.at[k, y, :, r, :] if self.kind == TRIPLE else self.acc.at[k, y, r, :]
+
+    def source(self, k, y, c):
         g = pl.ds(pl.multiple_of((y * 2 + c) * 256, 256), 256)
-        if self.kind == UP:
-            return self.whole.at[g, :]
-        return self.whole.at[:, g, :] if self.kind == TRIPLE else self.whole.at[:, :, g]
+        t, n = depth_of(ORDER[k]), self.shard.shape[-1]
+        if self.kind in (MIXING, DOWN):
+            return self.whole.at[t, :, g]
+        cols = pl.ds(pl.multiple_of(t * n, n), n)
+        return self.whole.at[g, cols] if self.kind == UP else self.whole.at[:, g, cols]
 
 
 def each(ref, body):
@@ -536,77 +515,94 @@
 
 
 class Scatter(Copies):
-    def __init__(self, totals, send, recv, here):
+    def __init__(self, totals, send, recv, line_send, line_recv, here):
         self.totals, self.send, self.recv, self.here = totals, send, recv, here
-
-    def copy(self, m, step):
+        self.line_send, self.line_recv = line_send, line_recv
+
+    def copy(self, item, step):
+        m, k = divmod(item, 4)
         w = self.totals[m]
         _, y, c, x = place()
         if step >= CORES:
-            k = step - CORES
-            source, into, target = w.source(k, 1 - c), w.got_core.at[k], CORE
+            at_y = step - CORES
+            source, into, target = w.source(k, at_y, 1 - c), w.got_core.at[k, at_y], CORE
         else:
             source, into, target = {
-                X_FIRST: lambda: (w.sums(slice(None), PART_B, 1 - x), w.x1, X),
-                Y_FIRST0: lambda: (w.sums(1 - y, PART_A, 0), w.y1.at[0], Y),
-                Y_FIRST1: lambda: (w.sums(1 - y, PART_A, 1), w.y1.at[1], Y),
-                Y_SECOND: lambda: (w.sums(1 - y, PART_B, x), w.y2, Y),
-                X_SECOND: lambda: (w.sums(y, PART_A, 1 - x), w.x2, X),
-                Z_LAST: lambda: (w.sums(y, HALF, x, depth_of(LAST)), w.z.at[0], NEAR),
-                Z_BACK: lambda: (w.sums(y, HALF, x, depth_of(FAR)), w.z.at[1], FAR),
-                Z_BESIDE: lambda: (w.sums(y, HALF, x, depth_of(NEAR)), w.z.at[2], NEAR),
-                DONE: lambda: (w.mine, w.other, X),
+                X_FIRST: lambda: (w.sums(k, slice(None), PART_B, 1 - x), w.x1.at[k], X),
+                Y_FIRST0: lambda: (w.sums(k, 1 - y, PART_A, 0), w.y1.at[k, 0], Y),
+                Y_FIRST1: lambda: (w.sums(k, 1 - y, PART_A, 1), w.y1.at[k, 1], Y),
+                Y_SECOND: lambda: (w.sums(k, 1 - y, PART_B, x), w.y2.at[k], Y),
+                X_SECOND: lambda: (w.sums(k, y, PART_A, 1 - x), w.x2.at[k], X),
             }[step]()
-        return remote(source, into, self.send.at[m, step], self.recv.at[m, step], peer(target))
-
-    def load(self, m, y):
-        w = self.totals[m]
-        return pltpu.make_async_copy(w.source(y, place()[2]), w.acc.at[y], self.here.at[m, y])
-
-    def begin(self, m):
-        for y in range(2):
-            self.load(m, y).start()
-            self.go(m, CORES + y)
-
-    def cores(self, m):
-        for y in range(2):
-            self.load(m, y).wait()
-            self.got(m, CORES + y)
-        add_into(self.totals[m].acc, self.totals[m].got_core)
-        self.go(m, X_FIRST, Y_FIRST0, Y_FIRST1)
-
-    def second(self, m):
+        return remote(source, into, self.send.at[item, step], self.recv.at[item, step], peer(target))
+
+    def line_copy(self, m, step):
         w = self.totals[m]
         _, y, _, x = place()
-        self.got(m, X_FIRST)
-        add_into(w.sums(slice(None), PART_B, x), w.x1)
-        self.go(m, Y_SECOND)
-        self.got(m, Y_FIRST0, Y_FIRST1)
-        add_into(w.sums(y, PART_A, 0), w.y1.at[0])
-        add_into(w.sums(y, PART_A, 1), w.y1.at[1])
-        self.go(m, X_SECOND)
-
-    def line(self, m):
+        source, into, target = {
+            Z_LAST: lambda: (w.sums(ORDER.index(LAST), y, HALF, x), w.z.at[0], NEAR),
+            Z_BACK: lambda: (w.sums(ORDER.index(FAR), y, HALF, x), w.z.at[1], FAR),
+            Z_BESIDE: lambda: (w.sums(ORDER.index(NEAR), y, HALF, x), w.z.at[2], NEAR),
+            DONE: lambda: (w.mine, w.other, X),
+        }[step]()
+        return remote(source, into, self.line_send.at[m, step], self.line_recv.at[m, step], peer(target))
+
+    def load(self, item, y):
+        m, k = divmod(item, 4)
+        w = self.totals[m]
+        return pltpu.make_async_copy(w.source(k, y, place()[2]), w.acc.at[k, y], self.here.at[item, y])
+
+    def begin(self, item):
+        for y in range(2):
+            self.load(item, y).start()
+            self.go(item, CORES + y)
+
+    def cores(self, item):
+        m, k = divmod(item, 4)
+        for y in range(2):
+            self.load(item, y).wait()
+            self.got(item, CORES + y)
+        add_into(self.totals[m].acc.at[k], self.totals[m].got_core.at[k])
+        self.go(item, X_FIRST, Y_FIRST0, Y_FIRST1)
+
+    def second(self, item):
+        m, k = divmod(item, 4)
         w = self.totals[m]
         _, y, _, x = place()
-        self.got(m, Y_SECOND)
-        add_into(w.sums(y, PART_B, x), w.y2)
-        self.got(m, X_SECOND)
-        add_into(w.sums(y, PART_A, x), w.x2)
-        self.go(m, Z_LAST, Z_BESIDE)
-
-    def line_on(self, m):
+        self.got(item, X_FIRST)
+        add_into(w.sums(k, slice(None), PART_B, x), w.x1.at[k])
+        self.go(item, Y_SECOND)
+        self.got(item, Y_FIRST0, Y_FIRST1)
+        add_into(w.sums(k, y, PART_A, 0), w.y1.at[k, 0])
+        add_into(w.sums(k, y, PART_A, 1), w.y1.at[k, 1])
+        self.go(item, X_SECOND)
+
+    def line(self, item):
+        m, k = divmod(item, 4)
         w = self.totals[m]
         _, y, _, x = place()
-        self.got(m, Z_LAST)
-        add_into(w.sums(y, HALF, x, depth_of(FAR)), w.z.at[0])
-        self.go(m, Z_BACK)
-
-    def own_half(self, m):
+        self.got(item, Y_SECOND)
+        add_into(w.sums(k, y, PART_B, x), w.y2.at[k])
+        self.got(item, X_SECOND)
+        add_into(w.sums(k, y, PART_A, x), w.x2.at[k])
+        if ORDER[k] == LAST:
+            self.line_copy(m, Z_LAST).start()
+        elif ORDER[k] == NEAR:
+            self.line_copy(m, Z_BESIDE).start()
+        elif ORDER[k] == FAR:
+            self.line_copy(m, Z_LAST).wait_recv()
+            add_into(w.sums(k, y, HALF, x), w.z.at[0])
+            self.line_copy(m, Z_BACK).start()
+
+    def own_half(self, item):
+        m, k = divmod(item, 4)
+        if ORDER[k] != OWN:
+            return
         w = self.totals[m]
         _, y, _, x = place()
-        self.got(m, Z_BESIDE, Z_BACK)
-        own, near, far = w.sums(y, HALF, x, depth_of(OWN)), w.z.at[2], w.z.at[1]
+        self.line_copy(m, Z_BESIDE).wait_recv()
+        self.line_copy(m, Z_BACK).wait_recv()
+        own, near, far = w.sums(k, y, HALF, x), w.z.at[2], w.z.at[1]
         out = w.own(HALF, x)
 
         def body(index):
@@ -615,30 +611,36 @@
             out[index] = total.astype(f32)
 
         each(w.mine, body)
-        self.go(m, DONE)
-
-    def other_half(self, m):
-        w = self.totals[m]
-        self.got(m, DONE)
-        out = w.own(HALF, 1 - place()[3])
-
-        def body(index):
-            out[index] = w.other[index].astype(f32)
-
-        each(w.other, body)
+        self.line_copy(m, DONE).start()
+
+    def other_half(self, item):
+        m, k = divmod(item, 4)
+        if ORDER[k] == OWN:
+            w = self.totals[m]
+            self.line_copy(m, DONE).wait_recv()
+            out = w.own(HALF, 1 - place()[3])
+
+            def body(index):
+                out[index] = w.other[index].astype(f32)
+
+            each(w.other, body)
+            for step in range(4):
+                self.line_copy(m, step).wait_send()
         for step in range(SUM_STEPS):
-            self.copy(m, step).wait_send()
-
-    def slots(self):
-        stages = (self.cores, self.second, self.line, self.line_on, self.own_half, self.other_half)
-        return staged(len(self.totals), tuple(enumerate(stages)))
+            self.copy(item, step).wait_send()
+
+    def slots(self, lags):
+        stages = (self.begin, self.cores, self.second, self.line, self.own_half, self.other_half)
+        return staged(4 * len(self.totals), tuple(zip(lags, stages)))
 
     @staticmethod
     def semaphores(n):
         return [
-            pltpu.SemaphoreType.DMA((n, SUM_STEPS)),
-            pltpu.SemaphoreType.DMA((n, SUM_STEPS)),
-            pltpu.SemaphoreType.DMA((n, 2)),
+            pltpu.SemaphoreType.DMA((4 * n, SUM_STEPS)),
+            pltpu.SemaphoreType.DMA((4 * n, SUM_STEPS)),
+            pltpu.SemaphoreType.DMA((n, 4)),
+            pltpu.SemaphoreType.DMA((n, 4)),
+            pltpu.SemaphoreType.DMA((4 * n, 2)),
         ]
 
 
@@ -662,12 +664,10 @@
         return remote(sums.at[k], arrived.at[k], small_send.at[k], small_recv.at[k], peer(AROUND[k]))
 
     greet(neighbours())
-    for m in range(n):
-        scatter.begin(m)
     move.start()
     sums[0] = small[...]
     small_copy(0).start()
-    for k, slot in enumerate(scatter.slots()):
+    for k, slot in enumerate(scatter.slots(range(6))):
         run(slot)
         if k < len(AROUND):
             small_copy(k).wait_recv()
@@ -714,7 +714,8 @@
 
 
 GATHERED = (MIXING, UP, DOWN)
-GATHER_AT = (1, 3, 5, 6, 7, 7, 7)
+GATHER_AT = (1, 2, 4, 6, 7, 7, 7)
+MOVE_AT = 4
 
 
 def forward_kernel(
@@ -742,7 +743,6 @@
             pair(1, i).start()
         for m in range(len(GATHERED)):
             gather.begin(m)
-        move.start()
 
     held = (keys, values_low, values_high)
     forward_load(slice(0, n), ka[...], va[...], *held)
@@ -754,6 +754,7 @@
     o_ref[...], lse_ref[...] = forward_heads(q_ref[...], *held)
 
     at_step(step, GATHER_AT, gather.slots())
+    pl.when(step == MOVE_AT)(move.start)
 
     @pl.when(step == last)
     def _():
@@ -792,7 +793,7 @@
 
 
 SCATTERED = (DOWN, UP)
-SCATTER_AT = (2, 3, 6, 7, 7, 7, 7)
+SCATTER_AT = (0, 0, 0, 1, 2, 3, 4, 5, 6, 7, 7, 7, 7, 7)
 
 
 def backward_kernel(
@@ -816,8 +817,6 @@
     @pl.when(step == 0)
     def _():
         greet(neighbours())
-        for m in range(len(SCATTERED)):
-            scatter.begin(m)
         move.start()
 
     for i, (k, v) in enumerate(((ka, va), (kb, vb))):
@@ -851,7 +850,7 @@
     def _():
         settle(step - 1)
 
-    at_step(step, SCATTER_AT, scatter.slots())
+    at_step(step, SCATTER_AT, scatter.slots((0, 1, 3, 4, 5, 6)))
 
     @pl.when(step == last)
     def _():

time: 550 us -> 511 us (0.929)
  Pallas kernels: 389 us -> 350 us
    pallas_call x1, Pallas kernels: 160 us -> 115 us  [attend_and_scatter(): pl.pallas_call(backward_kernel, grid=(blocks,), in_specs=[spec] * 8 + [AN...]
    pallas_call x1, Pallas kernels: 73.4 us -> 81.2 us  [scatter_last(): pl.pallas_call(functools.partial(scatter_kernel, kinds), name='scatter_la...]
where the time goes in v3:
time: 511 us; the launch traced here: 505 us
  Pallas kernels  350 us (68%)
  matrix products  118 us (23%)
  other arithmetic  18 us (4%)
  local copies, waits for them, and re-layouts  16.3 us (3%)
    dot_general x18, matrix products, dot(): return lax.dot_general(a, b, dims, preferred_element_type=f32)  118 us
    pallas_call x1, Pallas kernels, attend_and_scatter(): pl.pallas_call(backward_kernel, grid=(blocks,), in_specs=[spec] * 8 + [AN...  115 us
    pallas_call x1, Pallas kernels, attend_and_gather(): pl.pallas_call(forward_kernel, grid=(blocks,), in_specs=[spec] * 3 + [ANY...  108 us
    pallas_call x1, Pallas kernels, scatter_last(): pl.pallas_call(functools.partial(scatter_kernel, kinds), name='scatter_la...  81.2 us
    pallas_call x1, Pallas kernels, gather_first(): pl.pallas_call(gather_kernel, name='gather_first', in_specs=[ANYWHERE] *...  45.9 us

profile of v3, /device:TPU:0, one launch (start us, length us, event | category | flops | bytes accessed | tf_op | source)
XLA Modules:
  0.0 504.9 jit_solution(1724899567407328751)
XLA Ops:
  0.6 1.3 fusion.47.bias
  2.0 45.9 %gather_first.1 = (bf16[3,1024,1024]{2,1,0:T(8,128)(2,1)}, bf16[2,392,1024]{2,1,0:T(8,128)(2,1)}, f32[4,16,128]{2,1,0:T(8,128)}) custom-call(bf16[3,256,256]{2,1,0:T(8,128)(2,1)} %shard.1, bf16[2,392,1024]{2,1,0:T(8,128)(2,1)} %inputs.1, f32[16,128]{1,0:T(8,128)} %fusion.47.bias), custom_call_target="tpu_custom_call" | custom-call | tf_op jit(solution)/shard_map/gather_first/pallas_call | solution.py:437
  47.8 0.9 copy.37
  48.8 0.7 convert_element_type.120
  49.4 0.7 convert_element_type.119
  50.1 1.7 convert_reduce_fusion.1
  51.9 2.0 fusion.8
  53.9 0.6 fusion.11
  54.6 4.9 multiply_convert_fusion.1.q_ref
  59.5 3.0 fusion.31.ka.k_own
  62.5 3.0 add_convert_fusion.4.va.v_own
  66.3 1.4 broadcast_multiply_fusion.top
  67.6 108.2 %attend_and_gather.1 = (bf16[784,1024]{1,0:T(8,128)(2,1)}, f32[784,1024]{1,0:T(8,128)}, bf16[784,1024]{1,0:T(8,128)(2,1)}, bf16[784,1024]{1,0:T(8,128)(2,1)}, bf...) custom-call(bf16[784,1024]{1,0:T(8,128)(2,1)} %multiply_convert_fusi, ...), custom_call_target="tpu_custom_call" | custom-call | flops 5035261952 | bytes 12845056 | tf_op jit(solution)/shard_map/attend_and_gather/pallas_call | solution.py:771
  175.8 0.0 copy-start.23
  175.9 3.9 bitcast_add_fusion
  179.8 0.0 copy-start.24
  179.8 0.3 add_reduce_fusion
  180.1 0.6 multiply_reduce_fusion.4
  180.8 14.5 %multiply_convert_fusion = (bf16[784,4096]{1,0:T(8,128)(2,1)}, f32[784,4096]{1,0:T(8,128)}) fusion(f32[4096]{0:T(1024)S(1)} %bitcast.134, bf16[1024,4096]{1,0:T(8,128)(2,1)} %get-tuple-element.43, f32[1024]{0:T(1024)S(1)} %convert_element_type.132, f32[1024]{0:T(1024)S(1)} %convert_element_type.131, f32[784]{0:T(1024)S(1)} %add_rsqrt_fusion, ...), kind=kOutput, calls=%fused_computation.8 | convolution fusion | flops 6600753152 | bytes 30902400 | tf_op jit(solution)/shard_map/dot_general | solution.py:28
  195.3 15.1 %convert_reduce_fusion = (f32[4096]{0:T(1024)S(1)}, bf16[784,4096]{1,0:T(8,128)(2,1)}) fusion(f32[784,4096]{1,0:T(8,128)} %get-tuple-element.81, f32[4096]{0:T(1024)S(1)} %bitcast.135, bf16[784,1024]{1,0:T(8,128)(2,1)S(1)} %bitcast.120, bf16[4096,1024]{1,0:T(8,128)(2,1)S(1)} %bitcast.140), kind=kOutput, calls=%fused_computation.7 | convolution fusion | flops 6618411008 | bytes 29294592 | tf_op jit(solution)/shard_map/dot_general | solution.py:28
  210.4 12.2 %multiply_reduce_fusion.1 = (f32[1024]{0:T(1024)S(1)}, f32[784]{0:T(1024)S(1)}, f32[784]{0:T(1024)S(1)}, f32[1024]{0:T(1024)S(1)}, f32[784,1024]{1,0:T(8,128)S(1)}) fusion(f32[784]{0:T(1024)S(1)} %add_rsqrt_fusion, f32[784]{0:T(1024)S(1)} %broadcast_multiply_fusion.5, f32[784,1024]{1,0:T(8,128)S(1)} %bitcast_add_fusion, ...), kind=kOutput, calls=%fused_computation.27 | convolution fusion | flops 6584692736 | bytes 21262592 | tf_op jit(solution)/shard_map/dot_general | solution.py:28
  222.7 1.5 convert_reduce_fusion.3
  224.2 0.0 copy-done.27
  224.2 3.0 convolution_convert_fusion.3.g_ref
  227.3 0.4 slice-done.7
  227.7 8.0 %add_convert_fusion.2 = bf16[784,1024]{1,0:T(8,128)(2,1)} fusion(f32[784,1024]{1,0:T(8,128)S(1)} %bitcast_add_fusion, f32[1024]{0:T(1024)S(1)} %convert_element_type.138, f32[1024]{0:T(1024)S(1)} %convert_element_type.130, bf16[784,4096]{1,0:T(8,128)(2,1)S(1)} %bitcast.147, bf16[4096,1024]{1,0:T(8,128)(2,1)S(1)} %bitcast.141), kind=kOutput, calls=%fused_computation.34 | convolution fusion | flops 6579879936 | bytes 19636224 | tf_op jit(solution)/shard_map/dot_general | solution.py:28
  235.7 14.2 %convolution_convert_fusion.1 = bf16[4096,1024]{1,0:T(8,128)(2,1)} fusion(bf16[784,4096]{1,0:T(8,128)(2,1)} %get-tuple-element.80, bf16[784,1024]{1,0:T(8,128)(2,1)S(1)} %bitcast.121), kind=kOutput, calls=%fused_computation.11 | convolution fusion | flops 6580862976 | bytes 16416768 | tf_op jit(solution)/shard_map/dot_general | solution.py:28
  249.9 14.4 %convolution_convert_fusion.p1 = bf16[1024,4096]{1,0:T(8,128)(2,1)} fusion(bf16[784,4096]{1,0:T(8,128)(2,1)} %get-tuple-element.84, f32[1024]{0:T(1024)S(1)} %convert_element_type.132, f32[1024]{0:T(1024)S(1)} %convert_element_type.131, f32[784,1024]{1,0:T(8,128)S(1)} %bitcast_add_fusion, f32[784]{0:T(1024)S(1)} %add_rsqrt_fusion, ...), kind=kOutput, calls=%fused_computation.10 | convolution fusion | flops 6585679872 | bytes 18040960 | tf_op jit(solution)/shard_map/dot_general | solution.py:28
  264.4 114.6 %attend_and_scatter.1 = (bf16[784,1024]{1,0:T(8,128)(2,1)}, bf16[784,1024]{1,0:T(8,128)(2,1)}, bf16[784,1024]{1,0:T(8,128)(2,1)}, bf16[2,392,1024]{2,1,0:T(8,128...) custom-call(bf16[784,1024]{1,0:T(8,128)(2,1)} %multiply_convert_fusion.1.q_ref, ...), custom_call_target="tpu_custom_call" | custom-call | flops 12588154880 | bytes 22478848 | tf_op jit(solution)/shard_map/attend_and_scatter/pallas_call | solution.py:867
  379.0 6.3 %convolution_convert_fusion.2 = bf16[1024,1024]{1,0:T(8,128)(2,1)} fusion(bf16[784,1024]{1,0:T(8,128)(2,1)} %get-tuple-element.40.o_ref, f32[784,1024]{1,0:T(8,128)} %copy-done.2), kind=kOutput, calls=%fused_computation.60 | convolution fusion | flops 1646018560 | bytes 6914048 | tf_op jit(solution)/shard_map/dot_general | solution.py:28
  385.3 0.1 rsqrt.22
  385.3 0.1 div.32
  385.4 0.4 fusion.12
  385.8 1.0 copy-done.9
  386.9 3.7 fusion.13
  390.7 1.9 fusion.17
  392.6 2.9 multiply_reduce_fusion.5
  395.6 2.8 add_convert_fusion
  398.4 2.4 convert_bitcast_fusion
  400.8 2.4 convert_bitcast_fusion.1
  403.2 2.4 convert_bitcast_fusion.2
  405.6 3.1 pad_maximum_fusion.refs_1_
  408.7 0.3 convert_reduce_fusion.5
  409.0 0.3 convert_reduce_fusion.4
  409.3 0.3 convert_reduce_fusion.2
  409.6 0.6 copy-done.18
  410.2 81.2 %scatter_last.1 = (f32[256,256]{1,0:T(8,128)}, f32[3,256,256]{2,1,0:T(8,128)}, f32[96,128]{1,0:T(8,128)}, bf16[2,392,1024]{2,1,0:T(8,128)(2,1)}) custom-call(bf16[4,256,1024]{2,1,0:T(8,128)(2,1)} %bitcast.122, bf16[3,1024,1024]{2,1,0:T(8,128)(2,1)} %pad_maximum_fusion.refs_1_, f32[96,128]{1,0:T(8,128)} %bitcast.132, bf16[2,392,1024]{2,1,0:T(8,128)(2,1)} %bitcast.119), custom_call_target="tpu_custom_call" | custom-call | tf_op jit(solution)/shard_map/scatter_last/pallas_call | solution.py:692
  491.4 0.8 slice_bitcast_fusion.4
  492.3 0.6 dynamic_slice.27
  492.9 0.6 dynamic_slice.28
  493.5 0.6 dynamic_slice.29
  494.1 0.6 dynamic_slice.30
  494.7 0.6 dynamic_slice.31
  495.3 0.6 dynamic_slice.32
  496.0 0.6 dynamic_slice.33
  496.6 0.7 slice_bitcast_fusion.1
  497.3 0.6 dynamic_slice.34
  498.0 0.6 dynamic_slice.35
  498.6 1.2 copy.54
  499.8 1.2 copy.55
  500.9 0.9 copy.56
  501.8 0.7 copy.57
  502.5 1.0 copy.58
  503.5 1.0 copy.59
  (98 shorter events, 0.3 us)
Async XLA Ops:
  47.8 6.1 %copy-start = (bf16[2,392,1024]{2,1,0:T(8,128)(2,1)S(1)}, bf16[2,392,1024]{2,1,0:T(8,128)(2,1)}, u32[]{:S(2)}) copy-start(bf16[2,392,1024]{2,1,0:T(8,128)(2,1)} %get-tuple-element.36) | copy-start | bytes 4816900
  49.4 5.1 %copy-start.19 = (f32[1024]{0:T(1024)}, f32[1024]{0:T(1024)S(1)}, u32[]{:S(2)}) copy-start(f32[1024]{0:T(1024)S(1)} %convert_element_type.120) | copy-start | bytes 12292
  50.1 4.5 copy-start.16
  51.8 7.7 %copy-start.14 = (f32[2,392]{1,0:T(2,128)}, f32[2,392]{1,0:T(2,128)S(1)}, u32[]{:S(2)}) copy-start(f32[2,392]{1,0:T(2,128)S(1)} %broadcast_multiply_fusion.6) | copy-start | bytes 9412
  53.9 5.6 %copy-start.21 = (f32[2,392]{1,0:T(2,128)}, f32[2,392]{1,0:T(2,128)S(1)}, u32[]{:S(2)}) copy-start(f32[2,392]{1,0:T(2,128)S(1)} %add_rsqrt_fusion.1) | copy-start | bytes 9412
  53.9 5.6 %slice-start = ((s8[6291456]{0:T(1024)(128)(4,1)}), s8[4194304]{0:T(1024)(128)(4,1)S(1)}, s32[]{:S(2)}) async-start(s8[6291456]{0:T(1024)(128)(4,1)} %bitcast.126), calls=%async_computation | async-start | bytes 8388608
  54.6 4.9 slice-start.1
  62.5 3.7 copy-start.6
  175.8 3.9 copy-start.23
  179.8 0.9 copy-start.24
  179.8 1.0 copy-start.25
  180.1 15.2 %slice-start.4 = ((s8[8388608]{0:T(1024)(128)(4,1)}), s8[4194304]{0:T(1024)(128)(4,1)S(1)}, s32[]{:S(2)}) async-start(s8[8388608]{0:T(1024)(128)(4,1)} %bitcast.138), calls=%async_computation.4 | async-start | bytes 8388608
  180.8 14.5 %copy-start.4 = (bf16[2,392,1024]{2,1,0:T(8,128)(2,1)S(1)}, bf16[2,392,1024]{2,1,0:T(8,128)(2,1)}, u32[]{:S(2)}) copy-start(bf16[2,392,1024]{2,1,0:T(8,128)(2,1)} %get-tuple-element.39) | copy-start | bytes 4816900
  180.8 14.5 %slice-start.5 = ((s8[8388608]{0:T(1024)(128)(4,1)}), s8[4194304]{0:T(1024)(128)(4,1)S(1)}, s32[]{:S(2)}) async-start(s8[8388608]{0:T(1024)(128)(4,1)} %bitcast.138), calls=%async_computation.5 | async-start | bytes 8388608
  222.6 1.6 copy-start.27
  222.6 4.6 slice-start.6
  224.2 3.1 copy-start.2
  224.2 3.1 copy-start.26
  224.2 3.5 slice-start.7
  379.0 6.3 %copy-start.22 = (f32[2,392]{1,0:T(2,128)S(1)}, f32[2,392]{1,0:T(2,128)}, u32[]{:S(2)}) copy-start(f32[2,392]{1,0:T(2,128)} %copy-done.21) | copy-start | bytes 9412
  379.0 6.4 %copy-start.15 = (f32[2,392]{1,0:T(2,128)S(1)}, f32[2,392]{1,0:T(2,128)}, u32[]{:S(2)}) copy-start(f32[2,392]{1,0:T(2,128)} %copy-done.14) | copy-start | bytes 9412
  379.0 6.4 %copy-start.1 = (bf16[2,392,1024]{2,1,0:T(8,128)(2,1)S(1)}, bf16[2,392,1024]{2,1,0:T(8,128)(2,1)}, u32[]{:S(2)}) copy-start(bf16[2,392,1024]{2,1,0:T(8,128)(2,1)} %get-tuple-element.36) | copy-start | bytes 4816900
  385.4 1.4 copy-start.9
  385.4 5.2 %slice-start.2 = ((s8[6291456]{0:T(1024)(128)(4,1)}), s8[4194304]{0:T(1024)(128)(4,1)S(1)}, s32[]{:S(2)}) async-start(s8[6291456]{0:T(1024)(128)(4,1)} %bitcast.128), calls=%async_computation.2 | async-start | bytes 8388608
  386.9 3.8 slice-start.3
  386.9 3.8 copy-start.28
  390.6 1.9 copy-start.5
  390.6 1.9 copy-start.17
  392.6 3.0 copy-start.3
  392.6 3.0 copy-start.20
  409.6 0.6 copy-start.18
  410.2 88.4 %copy-start.7 = (bf16[2,392,1024]{2,1,0:T(8,128)(2,1)S(1)}, bf16[2,392,1024]{2,1,0:T(8,128)(2,1)}, u32[]{:S(2)}) copy-start(bf16[2,392,1024]{2,1,0:T(8,128)(2,1)} %get-tuple-element.102) | copy-start | bytes 4816900
  491.4 8.3 %copy-start.8 = (bf16[2,392,1024]{2,1,0:T(8,128)(2,1)S(1)}, bf16[2,392,1024]{2,1,0:T(8,128)(2,1)}, u32[]{:S(2)}) copy-start(bf16[2,392,1024]{2,1,0:T(8,128)(2,1)} %get-tuple-element.103) | copy-start | bytes 4816900
  498.6 2.3 copy-start.12
  498.6 3.2 copy-start.13
  499.8 2.7 copy-start.11
  499.8 3.7 copy-start.10

commit v4 on v3

--- a/solution.py
+++ b/solution.py
@@ -1011,7 +1011,8 @@
     hidden_pre = dot(second_rows, up) + hidden_offset
     normal_cdf = 0.5 * (1.0 + lax.erf(hidden_pre * root_half))
     hidden = (hidden_pre * normal_cdf).astype(bf16)
-    slope = normal_cdf + hidden_pre * (inv_root_two_pi * jnp.exp(-0.5 * hidden_pre * hidden_pre))
+    pdf = inv_root_two_pi * jnp.exp(-0.5 * hidden_pre * hidden_pre)
+    slope = (normal_cdf + hidden_pre * pdf).astype(bf16)
     output = (middle + dot(hidden, down) + contract_bias.astype(f32)).astype(bf16)
 
     contract_bias_part = jnp.sum(top.astype(f32), axis=0)

time: 511 us -> 511 us (level)
  no operation moved by 1% of the time
where the time goes in v4:
time: 511 us; the launch traced here: 505 us
  Pallas kernels  350 us (68%)
  matrix products  118 us (23%)
  other arithmetic  18 us (4%)
  local copies, waits for them, and re-layouts  16.3 us (3%)
    dot_general x18, matrix products, dot(): return lax.dot_general(a, b, dims, preferred_element_type=f32)  118 us
    pallas_call x1, Pallas kernels, attend_and_scatter(): pl.pallas_call(backward_kernel, grid=(blocks,), in_specs=[spec] * 8 + [AN...  115 us
    pallas_call x1, Pallas kernels, attend_and_gather(): pl.pallas_call(forward_kernel, grid=(blocks,), in_specs=[spec] * 3 + [ANY...  108 us
    pallas_call x1, Pallas kernels, scatter_last(): pl.pallas_call(functools.partial(scatter_kernel, kinds), name='scatter_la...  81.2 us
    pallas_call x1, Pallas kernels, gather_first(): pl.pallas_call(gather_kernel, name='gather_first', in_specs=[ANYWHERE] *...  45.9 us

profile of v4, /device:TPU:0, one launch (start us, length us, event | category | flops | bytes accessed | tf_op | source)
XLA Modules:
  0.0 504.9 jit_solution(1724899567407328751)
XLA Ops:
  0.6 1.3 fusion.46.bias
  2.0 45.9 %gather_first.1 = (bf16[3,1024,1024]{2,1,0:T(8,128)(2,1)}, bf16[2,392,1024]{2,1,0:T(8,128)(2,1)}, f32[4,16,128]{2,1,0:T(8,128)}) custom-call(bf16[3,256,256]{2,1,0:T(8,128)(2,1)} %shard.1, bf16[2,392,1024]{2,1,0:T(8,128)(2,1)} %inputs.1, f32[16,128]{1,0:T(8,128)} %fusion.46.bias), custom_call_target="tpu_custom_call" | custom-call | tf_op jit(solution)/shard_map/gather_first/pallas_call | solution.py:437
  47.8 0.9 copy.37
  48.8 0.7 convert_element_type.126
  49.4 0.7 convert_element_type.125
  50.1 1.7 convert_reduce_fusion.1
  51.9 2.0 fusion.7
  53.9 0.6 fusion.10
  54.6 4.9 multiply_convert_fusion.2.q_ref
  59.5 3.0 fusion.30.ka.k_own
  62.5 3.0 add_convert_fusion.4.va.v_own
  66.3 1.4 broadcast_multiply_fusion.top
  67.6 108.2 %attend_and_gather.1 = (bf16[784,1024]{1,0:T(8,128)(2,1)}, f32[784,1024]{1,0:T(8,128)}, bf16[784,1024]{1,0:T(8,128)(2,1)}, bf16[784,1024]{1,0:T(8,128)(2,1)}, bf...) custom-call(bf16[784,1024]{1,0:T(8,128)(2,1)} %multiply_convert_fusi, ...), custom_call_target="tpu_custom_call" | custom-call | flops 5035261952 | bytes 12845056 | tf_op jit(solution)/shard_map/attend_and_gather/pallas_call | solution.py:771
  175.8 0.0 copy-start.23
  175.9 3.9 bitcast_add_fusion
  179.8 0.0 copy-start.24
  179.8 0.3 add_reduce_fusion
  180.1 0.6 multiply_reduce_fusion.4
  180.8 14.5 %multiply_convert_fusion = (bf16[784,4096]{1,0:T(8,128)(2,1)}, f32[784,4096]{1,0:T(8,128)}) fusion(f32[4096]{0:T(1024)S(1)} %bitcast.134, bf16[1024,4096]{1,0:T(8,128)(2,1)} %get-tuple-element.43, f32[1024]{0:T(1024)S(1)} %convert_element_type.138, f32[1024]{0:T(1024)S(1)} %convert_element_type.137, f32[784]{0:T(1024)S(1)} %add_rsqrt_fusion, ...), kind=kOutput, calls=%fused_computation.7 | convolution fusion | flops 6600753152 | bytes 30902400 | tf_op jit(solution)/shard_map/dot_general | solution.py:28
  195.3 15.1 %convert_reduce_fusion = (f32[4096]{0:T(1024)S(1)}, bf16[784,4096]{1,0:T(8,128)(2,1)}) fusion(f32[784,4096]{1,0:T(8,128)} %get-tuple-element.81, f32[4096]{0:T(1024)S(1)} %bitcast.135, bf16[784,1024]{1,0:T(8,128)(2,1)S(1)} %bitcast.120, bf16[4096,1024]{1,0:T(8,128)(2,1)S(1)} %bitcast.140), kind=kOutput, calls=%fused_computation.6 | convolution fusion | flops 6624833536 | bytes 29294592 | tf_op jit(solution)/shard_map/dot_general | solution.py:28
  210.4 12.2 %multiply_reduce_fusion.1 = (f32[1024]{0:T(1024)S(1)}, f32[784]{0:T(1024)S(1)}, f32[784]{0:T(1024)S(1)}, f32[1024]{0:T(1024)S(1)}, f32[784,1024]{1,0:T(8,128)S(1)}) fusion(f32[784]{0:T(1024)S(1)} %add_rsqrt_fusion, f32[784]{0:T(1024)S(1)} %broadcast_multiply_fusion.5, f32[784,1024]{1,0:T(8,128)S(1)} %bitcast_add_fusion, ...), kind=kOutput, calls=%fused_computation.27 | convolution fusion | flops 6584692736 | bytes 21262592 | tf_op jit(solution)/shard_map/dot_general | solution.py:28
  222.7 1.5 convert_reduce_fusion.3
  224.2 0.0 copy-done.27
  224.2 3.0 convolution_convert_fusion.3.g_ref
  227.3 0.4 slice-done.7
  227.7 8.0 %add_convert_fusion.2 = bf16[784,1024]{1,0:T(8,128)(2,1)} fusion(f32[784,1024]{1,0:T(8,128)S(1)} %bitcast_add_fusion, f32[1024]{0:T(1024)S(1)} %convert_element_type.146, f32[1024]{0:T(1024)S(1)} %convert_element_type.136, bf16[784,4096]{1,0:T(8,128)(2,1)S(1)} %bitcast.147, bf16[4096,1024]{1,0:T(8,128)(2,1)S(1)} %bitcast.141), kind=kOutput, calls=%fused_computation.34 | convolution fusion | flops 6579879936 | bytes 19636224 | tf_op jit(solution)/shard_map/dot_general | solution.py:28
  235.7 14.2 %convolution_convert_fusion.1 = bf16[4096,1024]{1,0:T(8,128)(2,1)} fusion(bf16[784,4096]{1,0:T(8,128)(2,1)} %get-tuple-element.80, bf16[784,1024]{1,0:T(8,128)(2,1)S(1)} %bitcast.121), kind=kOutput, calls=%fused_computation.11 | convolution fusion | flops 6580862976 | bytes 16416768 | tf_op jit(solution)/shard_map/dot_general | solution.py:28
  249.9 14.4 %convolution_convert_fusion.p1 = bf16[1024,4096]{1,0:T(8,128)(2,1)} fusion(bf16[784,4096]{1,0:T(8,128)(2,1)} %get-tuple-element.84, f32[1024]{0:T(1024)S(1)} %convert_element_type.138, f32[1024]{0:T(1024)S(1)} %convert_element_type.137, f32[784,1024]{1,0:T(8,128)S(1)} %bitcast_add_fusion, f32[784]{0:T(1024)S(1)} %add_rsqrt_fusion, ...), kind=kOutput, calls=%fused_computation.10 | convolution fusion | flops 6585679872 | bytes 18040960 | tf_op jit(solution)/shard_map/dot_general | solution.py:28
  264.4 114.6 %attend_and_scatter.1 = (bf16[784,1024]{1,0:T(8,128)(2,1)}, bf16[784,1024]{1,0:T(8,128)(2,1)}, bf16[784,1024]{1,0:T(8,128)(2,1)}, bf16[2,392,1024]{2,1,0:T(8,128...) custom-call(bf16[784,1024]{1,0:T(8,128)(2,1)} %multiply_convert_fusion.2.q_ref, ...), custom_call_target="tpu_custom_call" | custom-call | flops 12588154880 | bytes 22478848 | tf_op jit(solution)/shard_map/attend_and_scatter/pallas_call | solution.py:867
  379.0 6.3 %convolution_convert_fusion.2 = bf16[1024,1024]{1,0:T(8,128)(2,1)} fusion(bf16[784,1024]{1,0:T(8,128)(2,1)} %get-tuple-element.40.o_ref, f32[784,1024]{1,0:T(8,128)} %copy-done.2), kind=kOutput, calls=%fused_computation.60 | convolution fusion | flops 1646018560 | bytes 6914048 | tf_op jit(solution)/shard_map/dot_general | solution.py:28
  385.3 0.1 rsqrt.22
  385.3 0.1 div.32
  385.4 0.4 fusion.11
  385.8 1.0 copy-done.9
  386.9 3.7 fusion.12
  390.7 1.9 fusion.16
  392.6 2.9 multiply_reduce_fusion.5
  395.6 2.8 add_convert_fusion
  398.4 2.4 convert_bitcast_fusion
  400.8 2.4 convert_bitcast_fusion.1
  403.2 2.4 convert_bitcast_fusion.2
  405.6 3.1 pad_maximum_fusion.refs_1_
  408.7 0.3 convert_reduce_fusion.5
  409.0 0.3 convert_reduce_fusion.4
  409.3 0.3 convert_reduce_fusion.2
  409.6 0.6 copy-done.18
  410.2 81.2 %scatter_last.1 = (f32[256,256]{1,0:T(8,128)}, f32[3,256,256]{2,1,0:T(8,128)}, f32[96,128]{1,0:T(8,128)}, bf16[2,392,1024]{2,1,0:T(8,128)(2,1)}) custom-call(bf16[4,256,1024]{2,1,0:T(8,128)(2,1)} %bitcast.122, bf16[3,1024,1024]{2,1,0:T(8,128)(2,1)} %pad_maximum_fusion.refs_1_, f32[96,128]{1,0:T(8,128)} %bitcast.132, bf16[2,392,1024]{2,1,0:T(8,128)(2,1)} %bitcast.119), custom_call_target="tpu_custom_call" | custom-call | tf_op jit(solution)/shard_map/scatter_last/pallas_call | solution.py:692
  491.4 0.8 slice_bitcast_fusion.4
  492.3 0.6 dynamic_slice.27
  492.9 0.6 dynamic_slice.28
  493.5 0.6 dynamic_slice.29
  494.1 0.6 dynamic_slice.30
  494.7 0.6 dynamic_slice.31
  495.3 0.6 dynamic_slice.32
  496.0 0.6 dynamic_slice.33
  496.6 0.7 slice_bitcast_fusion.1
  497.3 0.6 dynamic_slice.34
  498.0 0.6 dynamic_slice.35
  498.6 1.2 copy.54
  499.8 1.2 copy.55
  500.9 0.9 copy.56
  501.8 0.7 copy.57
  502.5 1.0 copy.58
  503.5 1.0 copy.59
  (98 shorter events, 0.3 us)
Async XLA Ops:
  47.8 6.1 %copy-start = (bf16[2,392,1024]{2,1,0:T(8,128)(2,1)S(1)}, bf16[2,392,1024]{2,1,0:T(8,128)(2,1)}, u32[]{:S(2)}) copy-start(bf16[2,392,1024]{2,1,0:T(8,128)(2,1)} %get-tuple-element.36) | copy-start | bytes 4816900
  49.4 5.1 %copy-start.19 = (f32[1024]{0:T(1024)}, f32[1024]{0:T(1024)S(1)}, u32[]{:S(2)}) copy-start(f32[1024]{0:T(1024)S(1)} %convert_element_type.126) | copy-start | bytes 12292
  50.1 4.5 copy-start.16
  51.8 7.7 %copy-start.14 = (f32[2,392]{1,0:T(2,128)}, f32[2,392]{1,0:T(2,128)S(1)}, u32[]{:S(2)}) copy-start(f32[2,392]{1,0:T(2,128)S(1)} %broadcast_multiply_fusion.6) | copy-start | bytes 9412
  53.9 5.6 %copy-start.21 = (f32[2,392]{1,0:T(2,128)}, f32[2,392]{1,0:T(2,128)S(1)}, u32[]{:S(2)}) copy-start(f32[2,392]{1,0:T(2,128)S(1)} %add_rsqrt_fusion.1) | copy-start | bytes 9412
  53.9 5.6 %slice-start = ((s8[6291456]{0:T(1024)(128)(4,1)}), s8[4194304]{0:T(1024)(128)(4,1)S(1)}, s32[]{:S(2)}) async-start(s8[6291456]{0:T(1024)(128)(4,1)} %bitcast.126), calls=%async_computation | async-start | bytes 8388608
  54.6 4.9 slice-start.1
  62.5 3.7 copy-start.6
  175.8 3.9 copy-start.23
  179.8 0.9 copy-start.24
  179.8 1.0 copy-start.25
  180.1 15.2 %slice-start.4 = ((s8[8388608]{0:T(1024)(128)(4,1)}), s8[4194304]{0:T(1024)(128)(4,1)S(1)}, s32[]{:S(2)}) async-start(s8[8388608]{0:T(1024)(128)(4,1)} %bitcast.138), calls=%async_computation.4 | async-start | bytes 8388608
  180.8 14.5 %copy-start.4 = (bf16[2,392,1024]{2,1,0:T(8,128)(2,1)S(1)}, bf16[2,392,1024]{2,1,0:T(8,128)(2,1)}, u32[]{:S(2)}) copy-start(bf16[2,392,1024]{2,1,0:T(8,128)(2,1)} %get-tuple-element.39) | copy-start | bytes 4816900
  180.8 14.5 %slice-start.5 = ((s8[8388608]{0:T(1024)(128)(4,1)}), s8[4194304]{0:T(1024)(128)(4,1)S(1)}, s32[]{:S(2)}) async-start(s8[8388608]{0:T(1024)(128)(4,1)} %bitcast.138), calls=%async_computation.5 | async-start | bytes 8388608
  222.6 1.6 copy-start.27
  222.6 4.6 slice-start.6
  224.2 3.1 copy-start.2
  224.2 3.1 copy-start.26
  224.2 3.5 slice-start.7
  379.0 6.3 %copy-start.22 = (f32[2,392]{1,0:T(2,128)S(1)}, f32[2,392]{1,0:T(2,128)}, u32[]{:S(2)}) copy-start(f32[2,392]{1,0:T(2,128)} %copy-done.21) | copy-start | bytes 9412
  379.0 6.4 %copy-start.15 = (f32[2,392]{1,0:T(2,128)S(1)}, f32[2,392]{1,0:T(2,128)}, u32[]{:S(2)}) copy-start(f32[2,392]{1,0:T(2,128)} %copy-done.14) | copy-start | bytes 9412
  379.0 6.4 %copy-start.1 = (bf16[2,392,1024]{2,1,0:T(8,128)(2,1)S(1)}, bf16[2,392,1024]{2,1,0:T(8,128)(2,1)}, u32[]{:S(2)}) copy-start(bf16[2,392,1024]{2,1,0:T(8,128)(2,1)} %get-tuple-element.36) | copy-start | bytes 4816900
  385.4 1.4 copy-start.9
  385.4 5.2 %slice-start.2 = ((s8[6291456]{0:T(1024)(128)(4,1)}), s8[4194304]{0:T(1024)(128)(4,1)S(1)}, s32[]{:S(2)}) async-start(s8[6291456]{0:T(1024)(128)(4,1)} %bitcast.128), calls=%async_computation.2 | async-start | bytes 8388608
  386.9 3.8 slice-start.3
  386.9 3.8 copy-start.28
  390.6 1.9 copy-start.5
  390.6 1.9 copy-start.17
  392.6 3.0 copy-start.3
  392.6 3.0 copy-start.20
  409.6 0.6 copy-start.18
  410.2 88.4 %copy-start.7 = (bf16[2,392,1024]{2,1,0:T(8,128)(2,1)S(1)}, bf16[2,392,1024]{2,1,0:T(8,128)(2,1)}, u32[]{:S(2)}) copy-start(bf16[2,392,1024]{2,1,0:T(8,128)(2,1)} %get-tuple-element.102) | copy-start | bytes 4816900
  491.4 8.3 %copy-start.8 = (bf16[2,392,1024]{2,1,0:T(8,128)(2,1)S(1)}, bf16[2,392,1024]{2,1,0:T(8,128)(2,1)}, u32[]{:S(2)}) copy-start(bf16[2,392,1024]{2,1,0:T(8,128)(2,1)} %get-tuple-element.103) | copy-start | bytes 4816900
  498.6 2.3 copy-start.12
  498.6 3.2 copy-start.13
  499.8 2.7 copy-start.11
  499.8 3.7 copy-start.10
